TPU v7x, 128 devices: a whole 4x4x4 slice. The times are simulated.
128 devices in a mesh: member: 4 (over y), space: 32 (over z, x, core).
Axes of the slice: x: 4, y: 4, z: 4, core: 2. Of those that a mesh axis runs over, the one named last changes fastest.
Arguments:
- grid_in: bfloat16 [4, 32768, 256], P('member', 'space'), may hold values from -6 to 6
- mesh_embed: bfloat16 [8192, 512], P('space'), may hold values from -6 to 6
- g2m_src: int32 [32, 32, 256], P('space'), may hold values from 0 to 1023
- g2m_dst: int32 [32, 32, 256], P('space'), may hold values from 0 to 255
- g2m_own_src: int32 [32, 1536], P('space'), may hold values from 0 to 1023
- g2m_own_dst: int32 [32, 1536], P('space'), may hold values from 0 to 255
- g2m_len: int32 [32, 32], P(None, 'space'), may hold values from 0 to 1536, as said below
- mesh_nbr: int32 [8192, 32], P('space'), may hold values from 0 to 767
- halo_rows: int32 [32, 16], P('space'), may hold values from 0 to 255
- m2g_src: int32 [32, 32, 256], P('space'), may hold values from 0 to 255
- m2g_dst: int32 [32, 32, 256], P('space'), may hold values from 0 to 1023
- m2g_own_src: int32 [32, 2560], P('space'), may hold values from 0 to 255
- m2g_own_dst: int32 [32, 2560], P('space'), may hold values from 0 to 1023
- m2g_len: int32 [32, 32], P(None, 'space'), may hold values from 0 to 2560, as said below
- w_embed: bfloat16 [256, 512], replicated, may hold values from -0.375 to 0.375
- w_send: bfloat16 [512, 512], replicated, may hold values from -0.25 to 0.25
- w_mesh: bfloat16 [512, 512], replicated, may hold values from -0.25 to 0.25
- attn_gain: float32 [512], replicated, may hold values from 0.1 to 1.9
- w_query: bfloat16 [512, 512], P('member')
- w_key: bfloat16 [512, 512], P('member')
- w_value: bfloat16 [512, 512], P('member'), may hold values from -0.25 to 0.25
- w_project: bfloat16 [512, 512], P('member'), may hold values from -0.25 to 0.25
- mlp_gain: float32 [512], replicated, may hold values from 0.1 to 1.9
- w_up: bfloat16 [512, 2048], P('member'), may hold values from -0.25 to 0.25
- w_down: bfloat16 [2048, 512], P('member'), may hold values from -0.125 to 0.125
- w_return: bfloat16 [512, 512], replicated, may hold values from -0.25 to 0.25
- w_grid: bfloat16 [512, 512], replicated, may hold values from -0.25 to 0.25
- w_skip: bfloat16 [512, 512], replicated, may hold values from -0.25 to 0.25
- w_out: bfloat16 [512, 84], replicated, may hold values from -0.25 to 0.25
Outputs:
- denoised: bfloat16 [4, 84, 32768], P('member', None, 'space')
Inputs may be any that keep to these rules, and one draw needn't show every extreme that they name: Pairs with |s - d| > 1 are empty (length 0). For |s - d| = 1 slot j carries an edge exactly when j < g2m_len[s, d] <= 256; on the diagonal, slot j of g2m_own_src and g2m_own_dst carries an edge exactly when j < g2m_len[p, p] <= 1536. Other slots hold arbitrary indices. The bands at the two ends of the axis (4 at each) receive the most edges. Pairs with |s - d| > 1 are empty (length 0). For |s - d| = 1 slot j carries an edge exactly when j < m2g_len[s, d] <= 256; on the diagonal, slot j of m2g_own_src and m2g_own_dst carries an edge exactly when j < m2g_len[p, p] <= 2560. Other slots hold arbitrary indices. The bands at the two ends of the axis (4 at each) receive the most edges.
All inputs are finite; a program needn't handle non-finite values.
Results may differ from a plain program's by a relative error of at most 0.015.
Values may be sent and summed in bfloat16 or wider, within the bound.
No kernel may reach another device: no remote copies, remote signals or barrier semaphores. Data moves between devices by JAX's collectives and lax.ppermute only.
A program may use at most 64 MiB of HBM per device.

v0:
```python
import math

import jax
import jax.numpy as jnp
from jax import lax
from jax.sharding import PartitionSpec as P

DH = 128


EPS = 1e-05


def from_behind(block, axis, distance):
    devices = range(lax.axis_size(axis))
    route = [(i - distance, i) for i in devices if i - distance in devices]
    return lax.ppermute(block, axis, route)


def layer_norm(values, norm_gain):
    centred = values - jnp.mean(values, axis=-1, keepdims=True)
    spread = jnp.mean(centred * centred, axis=-1, keepdims=True)
    return centred * lax.rsqrt(spread + EPS) * norm_gain


def pick_rows(table, wanted):
    picker = (wanted[:, None] == lax.broadcasted_iota(jnp.int32, (1, table.shape[0]), 1)).astype(
        table.dtype
    )
    return jnp.dot(picker, table, preferred_element_type=jnp.float32).astype(table.dtype)


def land_rows(arrived, dst_local, length, dst_rows):
    live_slot = lax.broadcasted_iota(jnp.int32, (dst_local.shape[0], 1), 0) < length
    placer = (
        (dst_local[:, None] == lax.broadcasted_iota(jnp.int32, (1, dst_rows), 1)) & live_slot
    ).astype(jnp.bfloat16)
    return lax.dot_general(
        placer, arrived, (((0,), (0,)), ((), ())), preferred_element_type=jnp.float32
    )


def adjacency(src_local, dst_local, length, src_rows, dst_rows, block):
    total = jnp.zeros((dst_rows, src_rows), jnp.float32)
    for start in range(0, src_local.shape[0], block):
        src_part = src_local[start : start + block]
        dst_part = dst_local[start : start + block]
        live_slot = start + lax.broadcasted_iota(jnp.int32, (block, 1), 0) < length
        src_hot = (src_part[:, None] == lax.broadcasted_iota(jnp.int32, (1, src_rows), 1)).astype(
            jnp.bfloat16
        )
        dst_hot = (
            (dst_part[:, None] == lax.broadcasted_iota(jnp.int32, (1, dst_rows), 1)) & live_slot
        ).astype(jnp.bfloat16)
        total = total + lax.dot_general(
            dst_hot, src_hot, (((0,), (0,)), ((), ())), preferred_element_type=jnp.float32
        )
    return total.astype(jnp.bfloat16)


def attend_block(queries, label_block, key_table, value_table):
    block = queries.shape[0]
    width = queries.shape[1]
    heads = width // DH
    table_size = key_table.shape[0]
    repeats = jnp.sum(
        (label_block[:, :, None] == lax.broadcasted_iota(jnp.int32, (1, 1, table_size), 2)).astype(
            jnp.float32
        ),
        axis=1,
    )
    query_heads = queries.reshape(block, heads, DH)
    key_heads = key_table.reshape(table_size, heads, DH)
    value_heads = value_table.reshape(table_size, heads, DH)
    scores = jnp.einsum(
        "bhd,thd->bht", query_heads, key_heads, preferred_element_type=jnp.float32
    ) / math.sqrt(DH)
    present = (repeats > 0.0)[:, None, :]
    top_score = jnp.max(jnp.where(present, scores, -jnp.inf), axis=-1, keepdims=True)
    weights = repeats[:, None, :] * jnp.exp(jnp.where(present, scores - top_score, 0.0))
    probs = (weights / jnp.sum(weights, axis=-1, keepdims=True)).astype(jnp.bfloat16)
    mixed = jnp.einsum("bht,thd->bhd", probs, value_heads, preferred_element_type=jnp.float32)
    return mixed.reshape(block, width).astype(jnp.bfloat16)


def shards(
    grid_in,
    mesh_embed,
    g2m_src,
    g2m_dst,
    g2m_own_src,
    g2m_own_dst,
    g2m_len,
    mesh_nbr,
    halo_rows,
    m2g_src,
    m2g_dst,
    m2g_own_src,
    m2g_own_dst,
    m2g_len,
    w_embed,
    w_send,
    w_mesh,
    attn_gain,
    w_query,
    w_key,
    w_value,
    w_project,
    mlp_gain,
    w_up,
    w_down,
    w_return,
    w_grid,
    w_skip,
    w_out,
):
    member_in = grid_in[0]
    grid_rows = member_in.shape[0]
    mesh_rows = mesh_embed.shape[0]
    width = mesh_embed.shape[1]
    edge_block = grid_rows // 2
    band = lax.axis_index("space")
    bands = lax.axis_size("space")
    upper = jnp.minimum(band + 1, bands - 1)
    lower = jnp.maximum(band - 1, 0)
    has_lower = band > 0
    has_upper = band < bands - 1
    grid_latent = jax.nn.silu(
        jnp.dot(member_in, w_embed, preferred_element_type=jnp.float32)
    ).astype(jnp.bfloat16)
    send_rows = jnp.dot(grid_latent, w_send, preferred_element_type=jnp.float32).astype(
        jnp.bfloat16
    )
    rows_up = g2m_src[0][upper]
    rows_down = g2m_src[0][lower]
    from_below = from_behind(pick_rows(send_rows, rows_up), "space", 1)
    from_above = from_behind(pick_rows(send_rows, rows_down), "space", -1)
    g2m_column = g2m_len[:, 0]
    own_links = adjacency(
        g2m_own_src[0], g2m_own_dst[0], g2m_column[band], grid_rows, mesh_rows, edge_block
    )
    mesh_agg = jnp.dot(own_links, send_rows, preferred_element_type=jnp.float32)
    mesh_agg = mesh_agg + land_rows(
        from_below, g2m_dst[0][lower], jnp.where(has_lower, g2m_column[lower], 0), mesh_rows
    )
    mesh_agg = mesh_agg + land_rows(
        from_above, g2m_dst[0][upper], jnp.where(has_upper, g2m_column[upper], 0), mesh_rows
    )
    gathered = (
        lax.all_gather(w_query, "member", axis=0, tiled=True),
        lax.all_gather(w_key, "member", axis=0, tiled=True),
        lax.all_gather(w_value, "member", axis=0, tiled=True),
        lax.all_gather(w_project, "member", axis=0, tiled=True),
        lax.all_gather(w_up, "member", axis=0, tiled=True),
        lax.all_gather(w_down, "member", axis=0, tiled=True),
    )
    full_query, full_key, full_value, full_project, full_up, full_down = gathered
    update = jax.nn.silu(
        jnp.dot(mesh_agg.astype(jnp.bfloat16), w_mesh, preferred_element_type=jnp.float32)
    )
    mesh_state = (mesh_embed.astype(jnp.float32) + update).astype(jnp.bfloat16)
    normed = layer_norm(mesh_state.astype(jnp.float32), attn_gain).astype(jnp.bfloat16)
    queries = jnp.dot(normed, full_query, preferred_element_type=jnp.float32).astype(jnp.bfloat16)
    key_local = jnp.dot(normed, full_key, preferred_element_type=jnp.float32).astype(jnp.bfloat16)
    value_local = jnp.dot(normed, full_value, preferred_element_type=jnp.float32).astype(
        jnp.bfloat16
    )
    published = halo_rows[0]
    far_keys, far_values = (
        lax.all_gather(pick_rows(key_local, published), "space", axis=0, tiled=True),
        lax.all_gather(pick_rows(value_local, published), "space", axis=0, tiled=True),
    )
    key_table = jnp.concatenate([key_local, far_keys], axis=0)
    value_table = jnp.concatenate([value_local, far_values], axis=0)
    own_rows = lax.broadcasted_iota(jnp.int32, (mesh_rows, 1), 0)
    label_all = jnp.concatenate([own_rows, mesh_nbr], axis=1)
    block = min(512, mesh_rows)
    count = mesh_rows // block

    def run_block(item):
        query_block, label_block = item
        return attend_block(query_block, label_block, key_table, value_table)

    attended = lax.map(
        run_block, (queries.reshape(count, block, width), label_all.reshape(count, block, -1))
    ).reshape(mesh_rows, width)
    after_attn = mesh_state.astype(jnp.float32) + jnp.dot(
        attended, full_project, preferred_element_type=jnp.float32
    )
    normed_two = layer_norm(after_attn, mlp_gain).astype(jnp.bfloat16)
    expanded = jax.nn.silu(jnp.dot(normed_two, full_up, preferred_element_type=jnp.float32)).astype(
        jnp.bfloat16
    )
    mesh_out = (
        after_attn + jnp.dot(expanded, full_down, preferred_element_type=jnp.float32)
    ).astype(jnp.bfloat16)
    return_rows = jnp.dot(mesh_out, w_return, preferred_element_type=jnp.float32).astype(
        jnp.bfloat16
    )
    back_below = from_behind(pick_rows(return_rows, m2g_src[0][upper]), "space", 1)
    back_above = from_behind(pick_rows(return_rows, m2g_src[0][lower]), "space", -1)
    m2g_column = m2g_len[:, 0]
    back_links = adjacency(
        m2g_own_src[0], m2g_own_dst[0], m2g_column[band], mesh_rows, grid_rows, edge_block
    )
    grid_agg = jnp.dot(back_links, return_rows, preferred_element_type=jnp.float32)
    grid_agg = grid_agg + land_rows(
        back_below, m2g_dst[0][lower], jnp.where(has_lower, m2g_column[lower], 0), grid_rows
    )
    grid_agg = grid_agg + land_rows(
        back_above, m2g_dst[0][upper], jnp.where(has_upper, m2g_column[upper], 0), grid_rows
    )
    pre = jnp.dot(grid_agg.astype(jnp.bfloat16), w_grid, preferred_element_type=jnp.float32)
    pre = pre + jnp.dot(grid_latent, w_skip, preferred_element_type=jnp.float32)
    updated = jax.nn.silu(pre).astype(jnp.bfloat16)
    result = lax.dot_general(
        w_out, updated, (((0,), (1,)), ((), ())), preferred_element_type=jnp.float32
    )
    return result.astype(jnp.bfloat16)[None]


def solution(mesh):
    placed = (
        P("member", "space", None),
        P("space", None),
        P("space", None, None),
        P("space", None, None),
        P("space", None),
        P("space", None),
        P(None, "space"),
        P("space", None),
        P("space", None),
        P("space", None, None),
        P("space", None, None),
        P("space", None),
        P("space", None),
        P(None, "space"),
        P(),
        P(),
        P(),
        P(),
        P("member", None),
        P("member", None),
        P("member", None),
        P("member", None),
        P(),
        P("member", None),
        P("member", None),
        P(),
        P(),
        P(),
        P(),
    )
    return jax.shard_map(
        shards, mesh=mesh, in_specs=placed, out_specs=P("member", None, "space"), check_vma=False
    )
```

profile of v0, /device:TPU:7, one launch (start us, length us, event | category | flops | bytes accessed | tf_op | source)
XLA Modules:
  0.0 204.3 jit_solution(7528923807072326013)
XLA Ops:
  8.1 1.7 multiply_convert_fusion.2
  11.8 4.1 %collective-permute-start = (bf16[256,512]{1,0:T(8,128)(2,1)}, bf16[256,512]{1,0:T(8,128)(2,1)S(1)}, u32[]{:S(2)}, u32[]{:S(2)}) collective-permute-start(bf16[256,512]{1,0:T(8,128)(2,1)} %convolution_convert_fusion.8), channel_id=1, source_target_pairs={{0,1},{1,2},{2,3},{3,4},{4,5},{5,6},{6,7},{7,8},{8,9},{9,10},{10,1... | collective-permute-start | bytes 786440 | tf_op jit(solution)/shard_map/ppermute | solution.py:17
  17.2 2.0 collective-permute-start.1
  26.4 15.2 %all_gather.26 = bf16[512,512]{1,0:T(8,128)(2,1)} all-gather(bf16[128,512]{1,0:T(8,128)(2,1)S(1)} %copy-done.7), channel_id=1, replica_groups=mesh['member'=4,'space'=32] {'member'}, dimensions={0}, use_global_device_ids=true | all-gather | bytes 655360 | tf_op jit(solution)/shard_map/all_gather | solution.py:151
  41.7 10.9 %all_gather.28 = bf16[512,512]{1,0:T(8,128)(2,1)} all-gather(bf16[128,512]{1,0:T(8,128)(2,1)S(1)} %copy-done.8), channel_id=1, replica_groups=mesh['member'=4,'space'=32] {'member'}, dimensions={0}, use_global_device_ids=true | all-gather | bytes 655360 | tf_op jit(solution)/shard_map/all_gather | solution.py:150
  52.6 3.1 %convert_reduce_fusion = f32[256,768]{1,0:T(8,128)S(1)} fusion(s32[256,33]{0,1:T(8,128)S(1)} %pad_add_fusion), kind=kLoop, calls=%fused_computation.1 | loop fusion | flops 19267584 | bytes 820224 | tf_op jit(solution)/shard_map/while/body/eval_jaxpr/reduce_sum | solution.py:66
  55.8 14.0 %all_gather.24 = bf16[512,512]{1,0:T(8,128)(2,1)} all-gather(bf16[128,512]{1,0:T(8,128)(2,1)S(1)} %copy-done.9), channel_id=1, replica_groups=mesh['member'=4,'space'=32] {'member'}, dimensions={0}, use_global_device_ids=true | all-gather | bytes 655360 | tf_op jit(solution)/shard_map/all_gather | solution.py:152
  69.8 14.3 %all_gather.29 = bf16[512,512]{1,0:T(8,128)(2,1)S(1)} all-gather(bf16[128,512]{1,0:T(8,128)(2,1)S(1)} %copy-done.10), channel_id=1, replica_groups=mesh['member'=4,'space'=32] {'member'}, dimensions={0}, use_global_device_ids=true | all-gather | bytes 655360 | tf_op jit(solution)/shard_map/all_gather | solution.py:153
  85.4 2.0 fusion.7
  88.2 3.1 %fusion.51 = f32[256,512]{1,0:T(8,128)} fusion(bf16[1024,512]{1,0:T(8,128)(2,1)} %copy-done.25, f32[256,1024]{1,0:T(8,128)S(1)} %fusion.30, s32[512]{0:T(512)S(1)} %bitcast.119, s32[512]{0:T(512)S(1)} %bitcast.118, pred[512]{0:T(512)(128)(4,1)S(1)} %fusion.141), kind=kOutput, calls=%fused_computation.52 | convolution fusion | flops 538181632 | bytes 2626048 | tf_op jit(solution)/shard_map/dot_general | solution.py:142
  91.3 2.2 %fusion.40 = f32[1024,256]{1,0:T(8,128)S(1)} fusion(f32[1024,256]{1,0:T(8,128)} %fusion.7, s32[512]{0:T(512)S(1)} %bitcast.113, pred[512]{0:T(512)(128)(4,1)S(1)} %fusion.144, s32[512]{0:T(512)S(1)} %bitcast.115), kind=kOutput, calls=%fused_computation.47 | convolution fusion | flops 269877248 | bytes 2101760 | tf_op jit(solution)/shard_map/dot_general | solution.py:55
  94.5 2.0 fusion.34
  101.4 2.0 convert_reduce_fusion.1
  104.1 33.1 %all_gather.25 = bf16[512,512]{1,0:T(8,128)(2,1)S(1)} all-gather(bf16[16,512]{1,0:T(8,128)(2,1)S(1)} %convolution_convert_fusion.10), channel_id=1, replica_groups=mesh['member'=4,'space'=32] {'space'}, dimensions={0}, use_global_device_ids=true | all-gather | bytes 540672 | tf_op jit(solution)/shard_map/all_gather | solution.py:171
  140.0 22.6 %all_gather.27 = bf16[512,512]{1,0:T(8,128)(2,1)S(1)} all-gather(bf16[16,512]{1,0:T(8,128)(2,1)S(1)} %convolution_convert_fusion.9), channel_id=1, replica_groups=mesh['member'=4,'space'=32] {'space'}, dimensions={0}, use_global_device_ids=true | all-gather | bytes 540672 | tf_op jit(solution)/shard_map/all_gather | solution.py:170
  166.7 3.8 %fusion.106 = f32[256,2048]{1,0:T(8,128)} fusion(bf16[512,2048]{1,0:T(8,128)(2,1)} %all-gather.3.cloned.1.call-done, f32[256,512]{1,0:T(8,128)S(1)} %get-tuple-element.58, f32[512]{0:T(512)S(1)} %copy-done.14, f32[256]{0:T(256)S(1)} %add_rsqrt_fusion, f32[256]{0:T(256)S(1)} %broadcast_multiply_fusion), kind=kOutput, calls=%fused_computation.129 | convolution fusion | flops 537395200 | bytes 4722688 | tf_op jit(solution)/shard_map/dot_general | solution.py:191
  170.5 3.2 %convolution_convert_fusion.3 = bf16[256,512]{1,0:T(8,128)(2,1)S(1)} fusion(bf16[512,512]{1,0:T(8,128)(2,1)S(1)} %copy-done.20, f32[256,512]{1,0:T(8,128)S(1)} %get-tuple-element.58, bf16[2048,512]{1,0:T(8,128)(2,1)} %all-gather.5.cloned.1.call-done, f32[256,2048]{1,0:T(8,128)} %fusion.106), kind=kOutput, calls=%fused_computation.61 | convolution fusion | flops 674103296 | bytes 5505024 | tf_op jit(solution)/shard_map/dot_general | solution.py:197
  174.6 3.6 %collective-permute-start.2 = (bf16[256,512]{1,0:T(8,128)(2,1)}, bf16[256,512]{1,0:T(8,128)(2,1)}, u32[]{:S(2)}, u32[]{:S(2)}) collective-permute-start(bf16[256,512]{1,0:T(8,128)(2,1)} %convolution_convert_fusion.2), channel_id=1, source_target_pairs={{0,1},{1,2},{2,3},{3,4},{4,5},{5,6},{6,7},{7,8},{8,9},{9,10},{10,1... | collective-permute-start | bytes 786440 | tf_op jit(solution)/shard_map/ppermute | solution.py:17
  179.2 1.9 collective-permute-start.3
  181.1 2.6 %fusion.49 = f32[1024,512]{1,0:T(8,128)S(1)} fusion(bf16[256,512]{1,0:T(8,128)(2,1)S(1)} %convolution_convert_fusion.3, f32[1024,256]{1,0:T(8,128)} %fusion.34, s32[512]{0:T(512)S(1)} %bitcast.103, pred[512]{0:T(512)(128)(4,1)S(1)} %add_compare_fusion, s32[512]{0:T(512)S(1)} %bitcast.104), kind=kOutput, calls=%fused_computation.51 | convolution fusion | flops 538574848 | bytes 3412480 | tf_op jit(solution)/shard_map/dot_general | solution.py:206
  183.8 2.9 %fusion.77 = f32[1024,512]{1,0:T(8,128)} fusion(bf16[256,512]{1,0:T(8,128)(2,1)} %collective-permute-done.2, s32[256]{0:T(256)S(1)} %bitcast.105, pred[256]{0:T(512)(128)(4,1)S(1)} %iota_compare_fusion.52), kind=kOutput, calls=%fused_computation.93 | convolution fusion | flops 268959744 | bytes 2360576 | tf_op jit(solution)/shard_map/dot_general | solution.py:38
  186.6 2.7 %collective-permute-done.3 = bf16[256,512]{1,0:T(8,128)(2,1)} collective-permute-done((bf16[256,512]{1,0:T(8,128)(2,1)}, bf16[256,512]{1,0:T(8,128)(2,1)}, u32[]{:S(2)}, u32[]{:S(2)}) %collective-permute-start.3) | collective-permute-done | bytes 262176 | tf_op jit(solution)/shard_map/ppermute | solution.py:17
  189.3 4.2 %fusion.28 = f32[1024,512]{1,0:T(8,128)} fusion(bf16[512,512]{1,0:T(8,128)(2,1)S(1)} %copy-done.4, f32[1024,512]{1,0:T(8,128)S(1)} %fusion.49, f32[1024,512]{1,0:T(8,128)} %fusion.77, bf16[256,512]{1,0:T(8,128)(2,1)} %collective-permute-done.3, s32[256]{0:T(256)S(1)} %bitcast.109, pred[256]{0:T(512)(128)(4,1)S(1)} %iota_compare_fusion.51), kind=kOutput, calls=%fused_computation.41 | convolution fusion | flops 807403520 | bytes 7079168 | tf_op jit(solution)/shard_map/dot_general | solution.py:213
  193.5 4.0 %fusion.58 = bf16[1,84,1024]{2,1,0:T(8,128)(2,1)} fusion(bf16[512,84]{0,1:T(8,128)(2,1)S(1)} %copy-done.21, f32[1024,512]{1,0:T(8,128)} %fusion.28, bf16[1024,512]{1,0:T(8,128)(2,1)} %copy-done.24, bf16[512,512]{1,0:T(8,128)(2,1)} %param.56), kind=kOutput, calls=%fused_computation.71 | convolution fusion | flops 628183040 | bytes 3928064 | tf_op jit(solution)/shard_map/dot_general | solution.py:216
  (111 shorter events, 26.8 us)
Async XLA Ops:
  6.5 160.1 %all-gather.3.cloned.1.call-start = ((), (), s32[]{:S(2)}) async-start(), calls=%async_computation | async-start | bytes 2621440 | tf_op jit(solution)/shard_map/all_gather | solution.py:154
  7.3 163.2 %all-gather.5.cloned.1.call-start = ((), (), s32[]{:S(2)}) async-start(), calls=%async_computation.1 | async-start | bytes 2621440 | tf_op jit(solution)/shard_map/all_gather | solution.py:155
  10.6 6.6 %copy-start.25 = (bf16[1024,512]{1,0:T(8,128)(2,1)}, bf16[1024,512]{1,0:T(8,128)(2,1)S(1)}, u32[]{:S(2)}) copy-start(bf16[1024,512]{1,0:T(8,128)(2,1)S(1)} %convolution_convert_fusion) | copy-start | bytes 3145732
  10.6 8.7 %copy-start.17 = (s32[32,1]{0,1:T(1,128)S(1)}, s32[32,1]{0,1:T(1,128)}, u32[]{:S(2)}) copy-start(s32[32,1]{0,1:T(1,128)} %param.42) | copy-start | bytes 388
  10.6 8.7 %copy-start.18 = (s32[32,1]{0,1:T(1,128)S(1)}, s32[32,1]{0,1:T(1,128)}, u32[]{:S(2)}) copy-start(s32[32,1]{0,1:T(1,128)} %param.35) | copy-start | bytes 388
  10.6 14.5 %copy-start.15 = (s32[1,1536]{1,0:T(1,128)S(1)}, s32[1,1536]{1,0:T(1,128)}, u32[]{:S(2)}) copy-start(s32[1,1536]{1,0:T(1,128)} %param.34) | copy-start | bytes 18436
  10.6 14.5 %copy-start.16 = (s32[1,1536]{1,0:T(1,128)S(1)}, s32[1,1536]{1,0:T(1,128)}, u32[]{:S(2)}) copy-start(s32[1,1536]{1,0:T(1,128)} %param.33) | copy-start | bytes 18436
  10.6 15.8 %copy-start.7 = (bf16[128,512]{1,0:T(8,128)(2,1)S(1)}, bf16[128,512]{1,0:T(8,128)(2,1)}, u32[]{:S(2)}) copy-start(bf16[128,512]{1,0:T(8,128)(2,1)} %param.48) | copy-start | bytes 393220
  10.6 31.1 %copy-start.8 = (bf16[128,512]{1,0:T(8,128)(2,1)S(1)}, bf16[128,512]{1,0:T(8,128)(2,1)}, u32[]{:S(2)}) copy-start(bf16[128,512]{1,0:T(8,128)(2,1)} %param.47) | copy-start | bytes 393220
  11.8 40.7 %copy-start.11 = (s32[256,32]{0,1:T(8,128)S(1)}, s32[256,32]{0,1:T(8,128)}, u32[]{:S(2)}) copy-start(s32[256,32]{0,1:T(8,128)} %param.36) | copy-start | bytes 98308
  11.8 87.3 %collective-permute-start = (bf16[256,512]{1,0:T(8,128)(2,1)}, bf16[256,512]{1,0:T(8,128)(2,1)S(1)}, u32[]{:S(2)}, u32[]{:S(2)}) collective-permute-start(bf16[256,512]{1,0:T(8,128)(2,1)} %convolution_convert_fusion.8), channel_id=1, source_target_pairs={{0,1},{1,2},{2,3},{3,4},{4,5},{5,6},{6,7},{7,8},{8,9},{9,10},{10,1... | collective-permute-start | bytes 786440 | tf_op jit(solution)/shard_map/ppermute | solution.py:17
  17.2 38.6 %copy-start.9 = (bf16[128,512]{1,0:T(8,128)(2,1)S(1)}, bf16[128,512]{1,0:T(8,128)(2,1)}, u32[]{:S(2)}) copy-start(bf16[128,512]{1,0:T(8,128)(2,1)} %param.49) | copy-start | bytes 393220
  17.2 84.2 %collective-permute-start.1 = (bf16[256,512]{1,0:T(8,128)(2,1)}, bf16[256,512]{1,0:T(8,128)(2,1)}, u32[]{:S(2)}, u32[]{:S(2)}) collective-permute-start(bf16[256,512]{1,0:T(8,128)(2,1)} %convolution_convert_fusion.7), channel_id=1, source_target_pairs={{1,0},{2,1},{3,2},{4,3},{5,4},{6,5},{7,6},{8,7},{9,8},{10,9},{11,1... | collective-permute-start | bytes 786440 | tf_op jit(solution)/shard_map/ppermute | solution.py:17
  19.2 50.5 %copy-start.10 = (bf16[128,512]{1,0:T(8,128)(2,1)S(1)}, bf16[128,512]{1,0:T(8,128)(2,1)}, u32[]{:S(2)}) copy-start(bf16[128,512]{1,0:T(8,128)(2,1)} %param.50) | copy-start | bytes 393220
  26.4 57.6 %copy-start.12 = (s32[1,2560]{1,0:T(1,128)S(1)}, s32[1,2560]{1,0:T(1,128)}, u32[]{:S(2)}) copy-start(s32[1,2560]{1,0:T(1,128)} %param.41) | copy-start | bytes 30724
  41.7 42.4 %copy-start.13 = (s32[1,2560]{1,0:T(1,128)S(1)}, s32[1,2560]{1,0:T(1,128)}, u32[]{:S(2)}) copy-start(s32[1,2560]{1,0:T(1,128)} %param.40) | copy-start | bytes 30724
  101.3 2.3 %copy-start.3 = (bf16[512,512]{1,0:T(8,128)(2,1)S(1)}, bf16[512,512]{1,0:T(8,128)(2,1)}, u32[]{:S(2)}) copy-start(bf16[512,512]{1,0:T(8,128)(2,1)} %all_gather.24) | copy-start | bytes 1572868
  101.3 2.6 %copy-start.23 = (s32[1,16]{1,0:T(1,128)S(1)}, s32[1,16]{1,0:T(1,128)}, u32[]{:S(2)}) copy-start(s32[1,16]{1,0:T(1,128)} %param.37) | copy-start | bytes 196
  137.3 25.3 %copy-start.2 = (bf16[512,512]{1,0:T(8,128)(2,1)S(1)}, bf16[512,512]{1,0:T(8,128)(2,1)}, u32[]{:S(2)}) copy-start(bf16[512,512]{1,0:T(8,128)(2,1)} %all_gather.28) | copy-start | bytes 1572868
  166.6 3.9 %copy-start.20 = (bf16[512,512]{1,0:T(8,128)(2,1)S(1)}, bf16[512,512]{1,0:T(8,128)(2,1)}, u32[]{:S(2)}) copy-start(bf16[512,512]{1,0:T(8,128)(2,1)} %param.54) | copy-start | bytes 1572868
  174.6 9.1 %collective-permute-start.2 = (bf16[256,512]{1,0:T(8,128)(2,1)}, bf16[256,512]{1,0:T(8,128)(2,1)}, u32[]{:S(2)}, u32[]{:S(2)}) collective-permute-start(bf16[256,512]{1,0:T(8,128)(2,1)} %convolution_convert_fusion.2), channel_id=1, source_target_pairs={{0,1},{1,2},{2,3},{3,4},{4,5},{5,6},{6,7},{7,8},{8,9},{9,10},{10,1... | collective-permute-start | bytes 786440 | tf_op jit(solution)/shard_map/ppermute | solution.py:17
  179.2 10.1 %collective-permute-start.3 = (bf16[256,512]{1,0:T(8,128)(2,1)}, bf16[256,512]{1,0:T(8,128)(2,1)}, u32[]{:S(2)}, u32[]{:S(2)}) collective-permute-start(bf16[256,512]{1,0:T(8,128)(2,1)} %convolution_convert_fusion.1), channel_id=1, source_target_pairs={{1,0},{2,1},{3,2},{4,3},{5,4},{6,5},{7,6},{8,7},{9,8},{10,9},{11,1... | collective-permute-start | bytes 786440 | tf_op jit(solution)/shard_map/ppermute | solution.py:17
  181.1 8.2 %copy-start.4 = (bf16[512,512]{1,0:T(8,128)(2,1)S(1)}, bf16[512,512]{1,0:T(8,128)(2,1)}, u32[]{:S(2)}) copy-start(bf16[512,512]{1,0:T(8,128)(2,1)} %param.55) | copy-start | bytes 1572868
  189.3 4.2 %copy-start.21 = (bf16[512,84]{0,1:T(8,128)(2,1)S(1)}, bf16[512,84]{0,1:T(8,128)(2,1)}, u32[]{:S(2)}) copy-start(bf16[512,84]{0,1:T(8,128)(2,1)} %param.57) | copy-start | bytes 258052
  (8 other events, 11.5 us)
Sparse Core Ops, SparseCore 0:
  9.0 37.1 all-gather.2
  47.8 37.3 all-gather.4
where the time goes:
time: 205 us; the launch traced here: 204 us
  blocking collectives  110 us (54%)
  matrix products  46.4 us (23%)
  between operations  16.5 us (8%)
  starting transfers between devices  11.7 us (6%)
  other arithmetic  10.4 us (5%)
  local copies, waits for them, and re-layouts  5.78 us (3%)
  waiting for transfers between devices  3.44 us (2%)
    all_gather x1, blocking collectives, shards(): lax.all_gather(pick_rows(value_local, published), 'space', axis=0, tiled=...  33.1 us
    all_gather x1, blocking collectives, shards(): lax.all_gather(pick_rows(key_local, published), 'space', axis=0, tiled=True)  22.6 us
    all_gather x1, blocking collectives, shards(): lax.all_gather(w_key, 'member', axis=0, tiled=True)  15.2 us
    all_gather x1, blocking collectives, shards(): lax.all_gather(w_project, 'member', axis=0, tiled=True)  14.3 us
    all_gather x1, blocking collectives, shards(): lax.all_gather(w_value, 'member', axis=0, tiled=True)  14 us
    ppermute x4, starting transfers between devices, from_behind(): return lax.ppermute(block, axis, route)  11.7 us
    all_gather x1, blocking collectives, shards(): lax.all_gather(w_query, 'member', axis=0, tiled=True)  10.9 us
    dot_general x6, matrix products, adjacency(): lax.dot_general(dst_hot, src_hot, (((0,), (0,)), ((), ())), preferred_ele...  8.65 us
  transfers between devices with their start and end apart: 6, of which 1 were waited for; matrix products, arithmetic and copies ran while one was open for 24% of the time, Pallas kernels for 0%

commit v1 on v0

v1 whole, which is shorter than its diff:
```python
import functools
import math

import jax
import jax.numpy as jnp
from jax import lax
from jax.experimental import pallas as pl
from jax.experimental.pallas import tpu as pltpu
from jax.sharding import PartitionSpec as P

DH = 128
EPS = 1e-05
BF = jnp.bfloat16
F32 = jnp.float32

ANY = pl.BlockSpec(memory_space=pl.ANY)
VMEM = pl.BlockSpec(memory_space=pltpu.VMEM)
SMEM = pl.BlockSpec(memory_space=pltpu.SMEM)


def dot(a, b):
    return jnp.dot(a, b, preferred_element_type=F32)


def dot_nt(a, b):
    return lax.dot_general(a, b, (((1,), (1,)), ((), ())), preferred_element_type=F32)


def silu(v):
    return v / (1.0 + jnp.exp(-v))


def hot_rows(row, count):
    ids = lax.broadcasted_iota(jnp.int32, (count, row.shape[1]), 0)
    return jnp.where(ids == row, 1.0, 0.0).astype(BF)


def live(row, length):
    slot = lax.broadcasted_iota(jnp.int32, row.shape, 1)
    return jnp.where(slot < length, row, -1)


def layer_norm(values, gain):
    centred = values - jnp.mean(values, axis=-1, keepdims=True)
    spread = jnp.mean(centred * centred, axis=-1, keepdims=True)
    return centred * lax.rsqrt(spread + EPS) * gain


def call(body, outs, ins, operands, scratch=(), flops=0, nbytes=0, name=None):
    return pl.pallas_call(
        body,
        out_shape=[jax.ShapeDtypeStruct(s, d) for s, d in outs],
        in_specs=ins,
        out_specs=[VMEM] * len(outs),
        scratch_shapes=list(scratch),
        name=name,
        cost_estimate=pl.CostEstimate(flops=flops, bytes_accessed=nbytes, transcendentals=0),
    )(*operands)


def around(bands):
    band = lax.axis_index("space")
    return band, jnp.minimum(band + 1, bands - 1), jnp.maximum(band - 1, 0)


def pick_body(
    bands, x_ref, src_ref, back_ref, wq, wk, wv, wp, wu, wd, up_ref, down_ref, a_ref, b_ref, sem
):
    band, upper, lower = around(bands)
    half = band % 2
    heads = wp.shape[0] // 2
    deep = wd.shape[0] // 2
    width = wp.shape[1]
    blocks = wu.shape[1] // width
    top = pl.multiple_of(half * heads, heads)
    low = pl.multiple_of(half * deep, deep)
    copies = []
    for i, w in enumerate((wq, wk, wv)):
        copies.append((w, a_ref.at[:, i * width : (i + 1) * width]))
    copies.append((wp.at[pl.ds(top, heads)], b_ref.at[0:heads]))
    copies.append((wd.at[pl.ds(low, deep)], b_ref.at[heads : heads + deep]))
    for i in range(blocks):
        at = heads + deep + i * heads
        copies.append(
            (wu.at[pl.ds(top, heads), i * width : (i + 1) * width], b_ref.at[at : at + heads])
        )
    copies = [pltpu.make_async_copy(s, d, sem.at[i]) for i, (s, d) in enumerate(copies)]
    for copy in copies:
        copy.start()
    x = x_ref[...]
    rows = x.shape[0]
    slots = src_ref.shape[1]
    eye = lax.broadcasted_iota(jnp.int32, (slots, slots), 0) == lax.broadcasted_iota(
        jnp.int32, (slots, slots), 1
    )
    for out, at in ((up_ref, upper), (down_ref, lower)):
        wanted = src_ref[pl.ds(at, 1), :].astype(F32)
        column = jnp.sum(jnp.where(eye, wanted, 0.0), axis=1, keepdims=True).astype(jnp.int32)
        ids = lax.broadcasted_iota(jnp.int32, (slots, rows), 1)
        picker = jnp.where(ids == column, 1.0, 0.0).astype(BF)
        out[0:slots, :] = dot(picker, x).astype(BF)
        back = back_ref[pl.ds(at, 1), :].astype(F32)
        out[slots:, :] = jnp.broadcast_to(back, (out.shape[0] - slots, slots)).astype(BF)
    for copy in copies:
        copy.wait()


def embed_body(bands, x_ref, we_ref, src_ref, dst_ref, len_ref, latent_ref, agg_ref):
    band, _, _ = around(bands)
    latent = silu(dot(x_ref[...], we_ref[...])).astype(BF)
    latent_ref[...] = latent
    mesh_rows = agg_ref.shape[0]
    src_hot = hot_rows(src_ref[...], x_ref.shape[0])
    dst_hot = hot_rows(live(dst_ref[...], len_ref[band]), mesh_rows)
    links = dot_nt(dst_hot, src_hot).astype(BF)
    agg_ref[...] = dot(links, latent)


def mesh_body(
    bands,
    agg_ref,
    below_ref,
    above_ref,
    dst_ref,
    len_ref,
    we_ref,
    ws_ref,
    wm_ref,
    static_ref,
    gain_ref,
    rows_ref,
    state_ref,
    normed_ref,
    halo_ref,
    wide,
    own,
):
    band, upper, lower = around(bands)
    total = agg_ref[...]
    mesh_rows = total.shape[0]
    slots = dst_ref.shape[1]
    for ref, at, there in ((below_ref, lower, band > 0), (above_ref, upper, band < bands - 1)):
        count = jnp.where(there, len_ref[at], 0)
        latent = silu(dot(ref[0:slots, :], we_ref[...])).astype(BF)
        dst_hot = hot_rows(live(dst_ref[pl.ds(at, 1), :], count), mesh_rows)
        total = total + dot(dst_hot, latent)
    agg = dot(total.astype(BF), ws_ref[...]).astype(BF)
    state = (static_ref[...].astype(F32) + silu(dot(agg, wm_ref[...]))).astype(BF)
    state_ref[...] = state
    normed = layer_norm(state.astype(F32), gain_ref[...]).astype(BF)
    normed_ref[...] = normed
    wide[...] = normed.astype(F32)
    published = own.shape[0]
    for j in range(published):
        own[j : j + 1, :] = wide[pl.ds(rows_ref[0, j], 1), :]
    halo = own[...].astype(BF)
    for b in range(bands):
        halo_ref[b * published : (b + 1) * published, :] = halo


def attend_body(
    normed_ref, far_ref, nbr_ref, wq, wk, wv, a1, a2, a3, out_ref, w_ref, rep_ref, sem
):
    me = lax.axis_index("member")
    part, width = wq.shape
    copies = []
    for i, w in enumerate((wq, wk, wv)):
        at = pl.multiple_of(me * part, part)
        copies.append((w, w_ref.at[pl.ds(at, part), i * width : (i + 1) * width]))
    for d, a in ((1, a1), (2, a2), (3, a3)):
        at = pl.multiple_of(((me - d) % 4) * part, part)
        copies.append((a, w_ref.at[pl.ds(at, part)]))
    copies = [pltpu.make_async_copy(s, d, sem.at[i]) for i, (s, d) in enumerate(copies)]
    for copy in copies:
        copy.start()
    normed = normed_ref[...]
    mesh_rows = normed.shape[0]
    table = mesh_rows + far_ref.shape[0]
    labels = jnp.transpose(nbr_ref[...], (1, 0))
    ids = lax.broadcasted_iota(jnp.int32, (mesh_rows, table), 1)
    rows = lax.broadcasted_iota(jnp.int32, (mesh_rows, 1), 0)
    repeats = jnp.where(ids == rows, 1.0, 0.0)
    for k in range(labels.shape[1]):
        repeats = repeats + jnp.where(ids == labels[:, k : k + 1], 1.0, 0.0)
    rep_ref[...] = repeats
    for copy in copies:
        copy.wait()
    own = dot(normed, w_ref[...]).astype(BF)
    far = dot(far_ref[...], w_ref[:, width:]).astype(BF)
    for h in range(width // DH):
        at = h * DH
        q = own[:, at : at + DH]
        k = jnp.concatenate(
            [own[:, width + at : width + at + DH], far[:, at : at + DH]], axis=0
        )
        v = jnp.concatenate(
            [own[:, 2 * width + at : 2 * width + at + DH], far[:, width + at : width + at + DH]],
            axis=0,
        )
        repeats = rep_ref[...]
        present = repeats > 0.0
        scores = jnp.where(present, dot_nt(q, k) / math.sqrt(DH), -jnp.inf)
        top = jnp.max(scores, axis=-1, keepdims=True)
        weights = repeats * jnp.exp(scores - top)
        probs = (weights / jnp.sum(weights, axis=-1, keepdims=True)).astype(BF)
        out_ref[:, at : at + DH] = dot(probs, v).astype(BF)


def mlp_body(
    att_ref,
    state_ref,
    gain_ref,
    wr_ref,
    wp,
    wu,
    wd,
    b1,
    b2,
    b3,
    s1,
    s2,
    s3,
    out_ref,
    p_ref,
    u_ref,
    d_ref,
    sem,
):
    me = lax.axis_index("member")
    half = lax.axis_index("space") % 2
    part, width = wp.shape
    deep = wd.shape[0]
    blocks = wu.shape[1] // width
    hp, hd = part // 2, deep // 2
    at_p = pl.multiple_of(me * part, part)
    at_d = pl.multiple_of(me * deep, deep)
    proj = [(wp, p_ref.at[pl.ds(at_p, part)])]
    up = [(wu, u_ref.at[pl.ds(at_p, part)])]
    down = [(wd, d_ref.at[pl.ds(at_d, deep)])]
    for d, b, s in ((1, b1, s1), (2, b2, s2), (3, b3, s3)):
        home = (me - d) % 4
        for ref, side in ((b, half), (s, 1 - half)):
            at_p = pl.multiple_of(home * part + side * hp, hp)
            at_d = pl.multiple_of(home * deep + side * hd, hd)
            proj.append((ref.at[0:hp], p_ref.at[pl.ds(at_p, hp)]))
            down.append((ref.at[hp : hp + hd], d_ref.at[pl.ds(at_d, hd)]))
            for i in range(blocks):
                at = hp + hd + i * hp
                up.append(
                    (
                        ref.at[at : at + hp],
                        u_ref.at[pl.ds(at_p, hp), i * width : (i + 1) * width],
                    )
                )
    count = 0
    groups = []
    for group in (proj, up, down):
        copies = []
        for s, d in group:
            copies.append(pltpu.make_async_copy(s, d, sem.at[count]))
            count += 1
        groups.append(copies)
        for copy in copies:
            copy.start()
    for copy in groups[0]:
        copy.wait()
    after = state_ref[...].astype(F32) + dot(att_ref[...], p_ref[...])
    normed = layer_norm(after, gain_ref[...]).astype(BF)
    for copy in groups[1]:
        copy.wait()
    expanded = silu(dot(normed, u_ref[...])).astype(BF)
    for copy in groups[2]:
        copy.wait()
    mesh_out = (after + dot(expanded, d_ref[...])).astype(BF)
    out_ref[...] = dot(mesh_out, wr_ref[...]).astype(BF)


def links_body(
    bands, rows, back_ref, src_ref, dst_ref, far_dst_ref, len_ref, below_ref, above_ref,
    latent_ref, ws_ref, lo_ref, hi_ref, grid_ref, pre_ref,
):
    band, upper, lower = around(bands)
    mesh_rows = back_ref.shape[0]
    slots = far_dst_ref.shape[1]
    pre_ref[...] = dot(latent_ref[...], ws_ref[...])
    src_hot = hot_rows(src_ref[...], mesh_rows)
    dst_hot = hot_rows(live(dst_ref[...], len_ref[band]), rows)
    links = dot_nt(dst_hot, src_hot).astype(BF)
    grid_ref[...] = dot(links, back_ref[...])
    for ref, out, at, there in (
        (below_ref, lo_ref, lower, band > 0),
        (above_ref, hi_ref, upper, band < bands - 1),
    ):
        count = jnp.where(there, len_ref[at], 0)
        src = ref[slots : slots + 1, :].astype(F32).astype(jnp.int32)
        src_hot = hot_rows(src, mesh_rows)
        dst_hot = hot_rows(live(far_dst_ref[pl.ds(at, 1), :], count), rows)
        out[...] = dot_nt(dst_hot, src_hot).astype(BF)


def final_body(grid_ref, pre_ref, lo_ref, hi_ref, below_ref, above_ref, wg_ref, wo_ref, out_ref):
    total = grid_ref[...] + dot(lo_ref[...], below_ref[...]) + dot(hi_ref[...], above_ref[...])
    updated = silu(dot(total.astype(BF), wg_ref[...]) + pre_ref[...]).astype(BF)
    out_ref[...] = dot_nt(wo_ref[...], updated).astype(BF)


def shards(
    grid_in,
    mesh_embed,
    g2m_src,
    g2m_dst,
    g2m_own_src,
    g2m_own_dst,
    g2m_len,
    mesh_nbr,
    halo_rows,
    m2g_src,
    m2g_dst,
    m2g_own_src,
    m2g_own_dst,
    m2g_len,
    w_embed,
    w_send,
    w_mesh,
    attn_gain,
    w_query,
    w_key,
    w_value,
    w_project,
    mlp_gain,
    w_up,
    w_down,
    w_return,
    w_grid,
    w_skip,
    w_out,
):
    x = grid_in[0]
    rows, channels = x.shape
    mesh_rows, width = mesh_embed.shape
    bands = lax.axis_size("space")
    slots = g2m_src.shape[2]
    part = w_query.shape[0]
    deep = w_down.shape[0]
    hidden = w_up.shape[1]
    published = halo_rows.shape[1]
    lane = -(-slots // 256) * 256
    g2m_count = g2m_len.reshape(-1)
    m2g_count = m2g_len.reshape(-1)
    bind = functools.partial

    up, down, pack_a, pack_b = call(
        bind(pick_body, bands),
        [
            ((slots + 16, channels), BF),
            ((slots + 16, channels), BF),
            ((part, 3 * width), BF),
            ((part // 2 + deep // 2 + part // 2 * (hidden // width), width), BF),
        ],
        [VMEM] * 3 + [ANY] * 6,
        (x, g2m_src[0], m2g_src[0], w_query, w_key, w_value, w_project, w_up, w_down),
        [pltpu.SemaphoreType.DMA((16,))],
        flops=int(3e8),
        nbytes=int(3e6),
        name="pick",
    )
    forward = [(i, i + 1) for i in range(bands - 1)]
    backward = [(i + 1, i) for i in range(bands - 1)]
    swap = [(i, i ^ 1) for i in range(bands)]

    def turn(block, d):
        return lax.ppermute(block, "member", [(i, (i + d) % 4) for i in range(4)])

    below = lax.ppermute(up, "space", forward)
    above = lax.ppermute(down, "space", backward)
    a1, a3, a2 = turn(pack_a, 1), turn(pack_a, 3), turn(pack_a, 2)
    latent, agg = call(
        bind(embed_body, bands),
        [((rows, width), BF), ((mesh_rows, width), F32)],
        [VMEM] * 4 + [SMEM],
        (x, w_embed, g2m_own_src, g2m_own_dst, g2m_count),
        flops=int(3e9),
        nbytes=int(3e6),
        name="embed",
    )
    pack_b, agg = lax.optimization_barrier((pack_b, agg))
    b1, b3, b2 = turn(pack_b, 1), turn(pack_b, 3), turn(pack_b, 2)
    state, normed, halo = call(
        bind(mesh_body, bands),
        [((mesh_rows, width), BF), ((mesh_rows, width), BF), ((bands * published, width), BF)],
        [VMEM] * 4 + [SMEM] + [VMEM] * 5 + [SMEM],
        (
            agg,
            below,
            above,
            g2m_dst[0],
            g2m_count,
            w_embed,
            w_send,
            w_mesh,
            mesh_embed,
            attn_gain.reshape(1, width),
            halo_rows,
        ),
        [pltpu.VMEM((mesh_rows, width), F32), pltpu.VMEM((published, width), F32)],
        flops=int(1e9),
        nbytes=int(3e6),
        name="mesh",
    )
    far = lax.all_to_all(halo, "space", 0, 0, tiled=True)
    (attended,) = call(
        attend_body,
        [((mesh_rows, width), BF)],
        [VMEM] * 3 + [ANY] * 6,
        (normed, far, mesh_nbr.T, w_query, w_key, w_value, a1, a2, a3),
        [
            pltpu.VMEM((width, 3 * width), BF),
            pltpu.VMEM((mesh_rows, mesh_rows + bands * published), F32),
            pltpu.SemaphoreType.DMA((8,)),
        ],
        flops=int(4e9),
        nbytes=int(4e6),
        name="attend",
    )
    s1, s2, s3 = (lax.ppermute(b, "space", swap) for b in (b1, b2, b3))
    (back,) = call(
        mlp_body,
        [((mesh_rows, width), BF)],
        [VMEM] * 4 + [ANY] * 9,
        (
            attended,
            state,
            mlp_gain.reshape(1, width),
            w_return,
            w_project,
            w_up,
            w_down,
            b1,
            b2,
            b3,
            s1,
            s2,
            s3,
        ),
        [
            pltpu.VMEM((4 * part, width), BF),
            pltpu.VMEM((4 * part, hidden), BF),
            pltpu.VMEM((4 * deep, width), BF),
            pltpu.SemaphoreType.DMA((48,)),
        ],
        flops=int(2e9),
        nbytes=int(6e6),
        name="mlp",
    )
    back_below = lax.ppermute(back, "space", forward)
    back_above = lax.ppermute(back, "space", backward)
    lo, hi, grid_agg, pre = call(
        bind(links_body, bands, rows),
        [
            ((rows, mesh_rows), BF),
            ((rows, mesh_rows), BF),
            ((rows, width), F32),
            ((rows, width), F32),
        ],
        [VMEM] * 4 + [SMEM] + [VMEM] * 4,
        (back, m2g_own_src, m2g_own_dst, m2g_dst[0], m2g_count, below, above, latent, w_skip),
        flops=int(4e9),
        nbytes=int(8e6),
        name="links",
    )
    (result,) = call(
        final_body,
        [((w_out.shape[1], rows), BF)],
        [VMEM] * 8,
        (grid_agg, pre, lo, hi, back_below, back_above, w_grid, w_out.T),
        flops=int(2e9),
        nbytes=int(8e6),
        name="final",
    )
    return result[None]


def solution(mesh):
    placed = (
        P("member", "space", None),
        P("space", None),
        P("space", None, None),
        P("space", None, None),
        P("space", None),
        P("space", None),
        P(None, "space"),
        P("space", None),
        P("space", None),
        P("space", None, None),
        P("space", None, None),
        P("space", None),
        P("space", None),
        P(None, "space"),
        P(),
        P(),
        P(),
        P(),
        P("member", None),
        P("member", None),
        P("member", None),
        P("member", None),
        P(),
        P("member", None),
        P("member", None),
        P(),
        P(),
        P(),
        P(),
    )
    return jax.shard_map(
        shards, mesh=mesh, in_specs=placed, out_specs=P("member", None, "space"), check_vma=False
    )
```

time: 205 us -> 108 us (0.53)
  blocking collectives: 110 us -> 0 us
  matrix products: 46.4 us -> 0 us
  Pallas kernels: 0 us -> 37.8 us
  waiting for transfers between devices: 3.44 us -> 36.8 us
  between operations: 16.5 us -> 0.19 us
  starting transfers between devices: 11.7 us -> 27.2 us
  other arithmetic: 10.4 us -> 0 us
    all_gather x6 -> x0, blocking collectives: 110 us -> none  [the longest x1 33.1 us: shards(): lax.all_gather(pick_rows(value_local, published), 'space', axis=0, tiled=...]
    dot_general x29 -> x0, matrix products: 46.4 us -> none  [the longest x6 8.65 us: adjacency(): lax.dot_general(dst_hot, src_hot, (((0,), (0,)), ((), ())), preferred_ele...]
    pallas_call x0 -> x7, Pallas kernels: none -> 37.8 us  [call(): pl.pallas_call(body, out_shape=[jax.ShapeDtypeStruct(s, d) for s, d in ou...]
    ppermute x4 -> x13, waiting for transfers between devices: 2.69 us -> 36.8 us  [the longest x6 29.1 us: turn(): return lax.ppermute(block, 'member', [(i, (i + d) % 4) for i in range(4)])]
    ppermute x4 -> x13, starting transfers between devices: 11.7 us -> 19.8 us  [the longest x6 6.68 us: turn(): return lax.ppermute(block, 'member', [(i, (i + d) % 4) for i in range(4)])]
    all_to_all x0 -> x1, starting transfers between devices: none -> 7.4 us  [shards(): far = lax.all_to_all(halo, 'space', 0, 0, tiled=True)]
    lt x12 -> x0, other arithmetic: 5.09 us -> none  [the longest x8 5.07 us: adjacency(): live_slot = start + lax.broadcasted_iota(jnp.int32, (block, 1), 0) < length]
    unnamed x52 -> x28, local copies, waits for them, and re-layouts: 1.17 us -> 4.66 us
  transfers between devices with their start and end apart: 6 -> 14, of which waited for: 1 -> 4; matrix products, arithmetic and copies ran while one was open for 24% -> 0% of each run, Pallas kernels for 0% -> 22%
where the time goes in v1:
time: 108 us; the launch traced here: 107 us
  Pallas kernels  37.8 us (35%)
  waiting for transfers between devices  36.8 us (34%)
  starting transfers between devices  27.2 us (25%)
  local copies, waits for them, and re-layouts  4.66 us (4%)
    pallas_call x7, Pallas kernels, call(): pl.pallas_call(body, out_shape=[jax.ShapeDtypeStruct(s, d) for s, d in ou...  37.8 us
    ppermute x6, waiting for transfers between devices, turn(): return lax.ppermute(block, 'member', [(i, (i + d) % 4) for i in range(4)])  29.1 us
    all_to_all x1, starting transfers between devices, shards(): far = lax.all_to_all(halo, 'space', 0, 0, tiled=True)  7.4 us
    ppermute x6, starting transfers between devices, turn(): return lax.ppermute(block, 'member', [(i, (i + d) % 4) for i in range(4)])  6.68 us
    ppermute x1, waiting for transfers between devices, shards(): above = lax.ppermute(down, 'space', backward)  6.56 us
    unnamed x28, local copies, waits for them, and re-layouts  4.66 us
    ppermute x1, starting transfers between devices, shards(): back_below = lax.ppermute(back, 'space', forward)  4.22 us
    ppermute x1, starting transfers between devices, shards(): below = lax.ppermute(up, 'space', forward)  4.02 us
  transfers between devices with their start and end apart: 14, of which 4 were waited for; matrix products, arithmetic and copies ran while one was open for 0% of the time, Pallas kernels for 22%

profile of v1, /device:TPU:7, one launch (start us, length us, event | category | flops | bytes accessed | tf_op | source)
XLA Modules:
  0.0 106.6 jit_solution(9384378388439024108)
XLA Ops:
  0.0 3.5 %pick.1 = (bf16[272,256]{1,0:T(8,128)(2,1)}, bf16[272,256]{1,0:T(8,128)(2,1)}, bf16[128,1536]{1,0:T(8,128)(2,1)}, bf16[576,512]{1,0:T(8,128)(2,1)}) custom-call(bf16[1024,256]{1,0:T(8,128)(2,1)} %bitcast.16, s32[32,256]{1,0:T(8,128)} %bitcast.18, s32[32,256]{1,0:T(8,128)} %bitcast.19, bf16[128,512]{1,0:T(8,128)(2,1)} %wq.3, bf16[128,512]{1,0:T(8,128)(2,1)} %wk.3, ...), custom_call_target="tpu_custom_call" | custom-call | flops 300000000 | bytes 3000000 | tf_op jit(solution)/shard_map/pick/pallas_call | solution.py:50
  3.5 4.0 %collective-permute-start = (bf16[272,256]{1,0:T(8,128)(2,1)}, bf16[272,256]{1,0:T(8,128)(2,1)S(1)}, u32[]{:S(2)}, u32[]{:S(2)}) collective-permute-start(bf16[272,256]{1,0:T(8,128)(2,1)} %get-tuple-element.23), channel_id=1, source_target_pairs={{0,1},{1,2},{2,3},{3,4},{4,5},{5,6},{6,7},{7,8},{8,9},{9,10},{10,1... | collective-permute-start | bytes 417800 | tf_op jit(solution)/shard_map/ppermute | solution.py:374
  7.5 3.9 %embed.1 = (bf16[1024,512]{1,0:T(8,128)(2,1)}, f32[256,512]{1,0:T(8,128)}) custom-call(bf16[1024,256]{1,0:T(8,128)(2,1)} %bitcast.17, bf16[256,512]{1,0:T(8,128)(2,1)} %we_ref.3, s32[1,1536]{1,0:T(1,128)} %src_ref.2, s32[1,1536]{1,0:T(1,128)} %dst_ref.2, s32[32]{0:T(128)} %bitcast.26), custom_call_target="tpu_custom_call" | custom-call | flops 3000000000 | bytes 3000000 | tf_op jit(solution)/shard_map/embed/pallas_call | solution.py:50
  11.4 2.7 %collective-permute-start.7 = (bf16[576,512]{1,0:T(8,128)(2,1)S(1)}, bf16[576,512]{1,0:T(8,128)(2,1)S(1)}, u32[]{:S(2)}, u32[]{:S(2)}) collective-permute-start(bf16[576,512]{1,0:T(8,128)(2,1)S(1)} %copy-done.4), channel_id=1, source_target_pairs={{0,96},{32,0},{64,32},{96,64},{1,97},{33,1},{65,33},{97,65},{2,98}... | collective-permute-start | bytes 1769480 | tf_op jit(solution)/shard_map/ppermute | solution.py:372
  14.1 1.6 %collective-permute-start.6 = (bf16[576,512]{1,0:T(8,128)(2,1)S(1)}, bf16[576,512]{1,0:T(8,128)(2,1)S(1)}, u32[]{:S(2)}, u32[]{:S(2)}) collective-permute-start(bf16[576,512]{1,0:T(8,128)(2,1)S(1)} %copy-done.4), channel_id=1, source_target_pairs={{0,64},{32,96},{64,0},{96,32},{1,65},{33,97},{65,1},{97,33},{2,66}... | collective-permute-start | bytes 1769480 | tf_op jit(solution)/shard_map/ppermute | solution.py:372
  15.8 1.6 %collective-permute-start.2 = (bf16[128,1536]{1,0:T(8,128)(2,1)}, bf16[128,1536]{1,0:T(8,128)(2,1)S(1)}, u32[]{:S(2)}, u32[]{:S(2)}) collective-permute-start(bf16[128,1536]{1,0:T(8,128)(2,1)} %get-tuple-element.27), channel_id=1, source_target_pairs={{0,32},{32,64},{64,96},{96,0},{1,33},{33,65},{65,97},{97,1},{2,34}... | collective-permute-start | bytes 1179656 | tf_op jit(solution)/shard_map/ppermute | solution.py:372
  17.4 1.9 %collective-permute-start.1 = (bf16[272,256]{1,0:T(8,128)(2,1)S(1)}, bf16[272,256]{1,0:T(8,128)(2,1)S(1)}, u32[]{:S(2)}, u32[]{:S(2)}) collective-permute-start(bf16[272,256]{1,0:T(8,128)(2,1)S(1)} %copy-done.13), channel_id=1, source_target_pairs={{1,0},{2,1},{3,2},{4,3},{5,4},{6,5},{7,6},{8,7},{9,8},{10,9},{11,1... | collective-permute-start | bytes 417800 | tf_op jit(solution)/shard_map/ppermute | solution.py:375
  19.3 6.6 %collective-permute-done.1.above_ref = bf16[272,256]{1,0:T(8,128)(2,1)S(1)} collective-permute-done((bf16[272,256]{1,0:T(8,128)(2,1)S(1)}, bf16[272,256]{1,0:T(8,128)(2,1)S(1)}, u32[]{:S(2)}, u32[]{:S(2)}) %collective-permute-start.1) | collective-permute-done | bytes 139296 | tf_op jit(solution)/shard_map/ppermute | solution.py:375
  26.5 4.1 %mesh.1 = (bf16[256,512]{1,0:T(8,128)(2,1)}, bf16[256,512]{1,0:T(8,128)(2,1)}, bf16[512,512]{1,0:T(8,128)(2,1)}) custom-call(f32[256,512]{1,0:T(8,128)} %get-tuple-element.22.agg_ref, bf16[272,256]{1,0:T(8,128)(2,1)} %copy-done.11, bf16[272,256]{1,0:T(8,128)(2,1)} %copy-done.12, s32[32,256]{1,0:T(8,128)} %bitcast.21, s32[32]{0:T(128)} %bitcast.27, ...), custom_call_target="tpu_custom_call" | custom-call | flops 1000000000 | bytes 3000000 | tf_op jit(solution)/shard_map/mesh/pallas_call | solution.py:50
  30.7 7.4 %all-to-all-start = ((bf16[32,16,512]{2,1,0:T(8,128)(2,1)}), bf16[32,16,512]{2,1,0:T(8,128)(2,1)S(1)}, u32[]{:S(2)}, u32[]{:S(2)}) async-start(bf16[32,16,512]{2,1,0:T(8,128)(2,1)} %bitcast.15), calls=%async_computation | async-start | bytes 1048576 | tf_op jit(solution)/shard_map/all_to_all | solution.py:410
  38.8 20.4 %collective-permute-done.2.a1 = bf16[128,1536]{1,0:T(8,128)(2,1)S(1)} collective-permute-done((bf16[128,1536]{1,0:T(8,128)(2,1)}, bf16[128,1536]{1,0:T(8,128)(2,1)S(1)}, u32[]{:S(2)}, u32[]{:S(2)}) %collective-permute-start.2) | collective-permute-done | bytes 393248 | tf_op jit(solution)/shard_map/ppermute | solution.py:372
  59.2 0.7 copy-done.7
  60.8 0.7 copy-done.8
  61.5 8.7 %collective-permute-done.4.a3 = bf16[128,1536]{1,0:T(8,128)(2,1)} collective-permute-done((bf16[128,1536]{1,0:T(8,128)(2,1)}, bf16[128,1536]{1,0:T(8,128)(2,1)}, u32[]{:S(2)}, u32[]{:S(2)}) %collective-permute-start.4) | collective-permute-done | bytes 393248 | tf_op jit(solution)/shard_map/ppermute | solution.py:372
  70.2 0.8 copy-done
  71.0 8.6 %attend.1.att_ref = bf16[256,512]{1,0:T(8,128)(2,1)} custom-call(bf16[256,512]{1,0:T(8,128)(2,1)} %get-tuple-element.25.normed_ref, bf16[512,512]{1,0:T(8,128)(2,1)} %bitcast.14, s32[32,256]{1,0:T(8,128)} %bitcast.22, bf16[128,512]{1,0:T(8,128)(2,1)} %wq.3, bf16[128,512]{1,0:T(8,128)(2,1)} %wk.3, bf16[128,512]{1,0:T(8,128)(2,1)} %wv.3, ...), custom_call_target="tpu_custom_call" | custom-call | flops 4000000000 | bytes 4000000 | tf_op jit(solution)/shard_map/attend/pallas_call | solution.py:50
  79.7 0.8 copy-done.5
  80.6 5.8 %mlp.1.back_ref = bf16[256,512]{1,0:T(8,128)(2,1)} custom-call(bf16[256,512]{1,0:T(8,128)(2,1)} %attend.1.att_ref, bf16[256,512]{1,0:T(8,128)(2,1)} %get-tuple-element.28.state_ref, f32[1,512]{1,0:T(1,128)} %bitcast.25, bf16[512,512]{1,0:T(8,128)(2,1)} %wr_ref.1, bf16[128,512]{1,0:T(8,128)(2,1)} %wp.3, bf16[128,2048]{1,0:T(8,128)(2,1)} %wu.3, ...), custom_call_target="tpu_custom_call" | custom-call | flops 2000000000 | bytes 6000000 | tf_op jit(solution)/shard_map/mlp/pallas_call | solution.py:50
  86.5 4.2 %collective-permute-start.11 = (bf16[256,512]{1,0:T(8,128)(2,1)}, bf16[256,512]{1,0:T(8,128)(2,1)S(1)}, u32[]{:S(2)}, u32[]{:S(2)}) collective-permute-start(bf16[256,512]{1,0:T(8,128)(2,1)} %mlp.1.back_ref), channel_id=1, source_target_pairs={{0,1},{1,2},{2,3},{3,4},{4,5},{5,6},{6,7},{7,8},{8,9},{9,10},{10,1... | collective-permute-start | bytes 786440 | tf_op jit(solution)/shard_map/ppermute | solution.py:455
  90.7 2.1 %collective-permute-start.12 = (bf16[256,512]{1,0:T(8,128)(2,1)}, bf16[256,512]{1,0:T(8,128)(2,1)S(1)}, u32[]{:S(2)}, u32[]{:S(2)}) collective-permute-start(bf16[256,512]{1,0:T(8,128)(2,1)} %mlp.1.back_ref), channel_id=1, source_target_pairs={{1,0},{2,1},{3,2},{4,3},{5,4},{6,5},{7,6},{8,7},{9,8},{10,9},{11,1... | collective-permute-start | bytes 786440 | tf_op jit(solution)/shard_map/ppermute | solution.py:456
  92.8 6.7 %links.1 = (bf16[1024,256]{1,0:T(8,128)(2,1)}, bf16[1024,256]{1,0:T(8,128)(2,1)}, f32[1024,512]{1,0:T(8,128)}, f32[1024,512]{1,0:T(8,128)}) custom-call(bf16[256,512]{1,0:T(8,128)(2,1)} %mlp.1.back_ref, s32[1,2560]{1,0:T(1,128)} %src_ref.3, s32[1,2560]{1,0:T(1,128)} %dst_ref.3, s32[32,256]{1,0:T(8,128)} %bitcast.23, s32[32]{0:T(128)} %bitcast.28, ...), custom_call_target="tpu_custom_call" | custom-call | flops 4000000000 | bytes 8000000 | tf_op jit(solution)/shard_map/links/pallas_call | solution.py:50
  99.6 1.1 %collective-permute-done.12.above_ref = bf16[256,512]{1,0:T(8,128)(2,1)S(1)} collective-permute-done((bf16[256,512]{1,0:T(8,128)(2,1)}, bf16[256,512]{1,0:T(8,128)(2,1)S(1)}, u32[]{:S(2)}, u32[]{:S(2)}) %collective-permute-start.12) | collective-permute-done | bytes 262176 | tf_op jit(solution)/shard_map/ppermute | solution.py:456
  100.7 0.7 copy-done.10
  101.4 5.2 %final.1 = bf16[84,1024]{1,0:T(8,128)(2,1)} custom-call(f32[1024,512]{1,0:T(8,128)} %get-tuple-element.31.grid_ref, f32[1024,512]{1,0:T(8,128)} %get-tuple-element.32.pre_ref, bf16[1024,256]{1,0:T(8,128)(2,1)} %get-tuple-element.33.lo_ref, bf16[1024,256]{1,0:T(8,128)(2,1)} %get-tuple-element.34.hi_ref, bf16[256,512]{1,0:T(8,128)(2,1)} %copy-done.9, ...), custom_call_target="tpu_custom_call" | custom-call | flops 2000000000 | bytes 8000000 | tf_op jit(solution)/shard_map/final/pallas_call | solution.py:50
  (39 shorter events, 2.4 us)
Async XLA Ops:
  3.5 13.9 %collective-permute-start = (bf16[272,256]{1,0:T(8,128)(2,1)}, bf16[272,256]{1,0:T(8,128)(2,1)S(1)}, u32[]{:S(2)}, u32[]{:S(2)}) collective-permute-start(bf16[272,256]{1,0:T(8,128)(2,1)} %get-tuple-element.23), channel_id=1, source_target_pairs={{0,1},{1,2},{2,3},{3,4},{4,5},{5,6},{6,7},{7,8},{8,9},{9,10},{10,1... | collective-permute-start | bytes 417800 | tf_op jit(solution)/shard_map/ppermute | solution.py:374
  7.5 3.9 %copy-start.4 = (bf16[576,512]{1,0:T(8,128)(2,1)S(1)}, bf16[576,512]{1,0:T(8,128)(2,1)}, u32[]{:S(2)}) copy-start(bf16[576,512]{1,0:T(8,128)(2,1)} %get-tuple-element.29) | copy-start | bytes 1769476
  7.5 9.9 %copy-start.13 = (bf16[272,256]{1,0:T(8,128)(2,1)S(1)}, bf16[272,256]{1,0:T(8,128)(2,1)}, u32[]{:S(2)}) copy-start(bf16[272,256]{1,0:T(8,128)(2,1)} %get-tuple-element.24) | copy-start | bytes 417796
  11.4 48.6 %collective-permute-start.7 = (bf16[576,512]{1,0:T(8,128)(2,1)S(1)}, bf16[576,512]{1,0:T(8,128)(2,1)S(1)}, u32[]{:S(2)}, u32[]{:S(2)}) collective-permute-start(bf16[576,512]{1,0:T(8,128)(2,1)S(1)} %copy-done.4), channel_id=1, source_target_pairs={{0,96},{32,0},{64,32},{96,64},{1,97},{33,1},{65,33},{97,65},{2,98}... | collective-permute-start | bytes 1769480 | tf_op jit(solution)/shard_map/ppermute | solution.py:372
  14.1 45.8 %collective-permute-start.5 = (bf16[576,512]{1,0:T(8,128)(2,1)S(1)}, bf16[576,512]{1,0:T(8,128)(2,1)S(1)}, u32[]{:S(2)}, u32[]{:S(2)}) collective-permute-start(bf16[576,512]{1,0:T(8,128)(2,1)S(1)} %copy-done.4), channel_id=1, source_target_pairs={{0,32},{32,64},{64,96},{96,0},{1,33},{33,65},{65,97},{97,1},{2,34}... | collective-permute-start | bytes 1769480 | tf_op jit(solution)/shard_map/ppermute | solution.py:372
  14.1 46.3 %collective-permute-start.6 = (bf16[576,512]{1,0:T(8,128)(2,1)S(1)}, bf16[576,512]{1,0:T(8,128)(2,1)S(1)}, u32[]{:S(2)}, u32[]{:S(2)}) collective-permute-start(bf16[576,512]{1,0:T(8,128)(2,1)S(1)} %copy-done.4), channel_id=1, source_target_pairs={{0,64},{32,96},{64,0},{96,32},{1,65},{33,97},{65,1},{97,33},{2,66}... | collective-permute-start | bytes 1769480 | tf_op jit(solution)/shard_map/ppermute | solution.py:372
  15.8 43.4 %collective-permute-start.2 = (bf16[128,1536]{1,0:T(8,128)(2,1)}, bf16[128,1536]{1,0:T(8,128)(2,1)S(1)}, u32[]{:S(2)}, u32[]{:S(2)}) collective-permute-start(bf16[128,1536]{1,0:T(8,128)(2,1)} %get-tuple-element.27), channel_id=1, source_target_pairs={{0,32},{32,64},{64,96},{96,0},{1,33},{33,65},{65,97},{97,1},{2,34}... | collective-permute-start | bytes 1179656 | tf_op jit(solution)/shard_map/ppermute | solution.py:372
  17.4 8.5 %copy-start.11 = (bf16[272,256]{1,0:T(8,128)(2,1)}, bf16[272,256]{1,0:T(8,128)(2,1)S(1)}, u32[]{:S(2)}) copy-start(bf16[272,256]{1,0:T(8,128)(2,1)S(1)} %collective-permute-done.below_ref) | copy-start | bytes 417796
  17.4 8.5 %collective-permute-start.1 = (bf16[272,256]{1,0:T(8,128)(2,1)S(1)}, bf16[272,256]{1,0:T(8,128)(2,1)S(1)}, u32[]{:S(2)}, u32[]{:S(2)}) collective-permute-start(bf16[272,256]{1,0:T(8,128)(2,1)S(1)} %copy-done.13), channel_id=1, source_target_pairs={{1,0},{2,1},{3,2},{4,3},{5,4},{6,5},{7,6},{8,7},{9,8},{10,9},{11,1... | collective-permute-start | bytes 417800 | tf_op jit(solution)/shard_map/ppermute | solution.py:375
  30.7 39.5 %all-to-all-start = ((bf16[32,16,512]{2,1,0:T(8,128)(2,1)}), bf16[32,16,512]{2,1,0:T(8,128)(2,1)S(1)}, u32[]{:S(2)}, u32[]{:S(2)}) async-start(bf16[32,16,512]{2,1,0:T(8,128)(2,1)} %bitcast.15), calls=%async_computation | async-start | bytes 1048576 | tf_op jit(solution)/shard_map/all_to_all | solution.py:410
  38.1 22.7 %collective-permute-start.3 = (bf16[128,1536]{1,0:T(8,128)(2,1)}, bf16[128,1536]{1,0:T(8,128)(2,1)S(1)}, u32[]{:S(2)}, u32[]{:S(2)}) collective-permute-start(bf16[128,1536]{1,0:T(8,128)(2,1)} %get-tuple-element.27), channel_id=1, source_target_pairs={{0,64},{32,96},{64,0},{96,32},{1,65},{33,97},{65,1},{97,33},{2,66}... | collective-permute-start | bytes 1179656 | tf_op jit(solution)/shard_map/ppermute | solution.py:372
  59.2 11.0 %collective-permute-start.4 = (bf16[128,1536]{1,0:T(8,128)(2,1)}, bf16[128,1536]{1,0:T(8,128)(2,1)}, u32[]{:S(2)}, u32[]{:S(2)}) collective-permute-start(bf16[128,1536]{1,0:T(8,128)(2,1)} %get-tuple-element.27), channel_id=1, source_target_pairs={{0,96},{32,0},{64,32},{96,64},{1,97},{33,1},{65,33},{97,65},{2,98}... | collective-permute-start | bytes 1179656 | tf_op jit(solution)/shard_map/ppermute | solution.py:372
  60.0 19.6 %copy-start.1 = (bf16[576,512]{1,0:T(8,128)(2,1)}, bf16[576,512]{1,0:T(8,128)(2,1)S(1)}, u32[]{:S(2)}) copy-start(bf16[576,512]{1,0:T(8,128)(2,1)S(1)} %collective-permute-done.7.b3) | copy-start | bytes 1769476
  60.0 19.7 %collective-permute-start.10 = (bf16[576,512]{1,0:T(8,128)(2,1)S(1)}, bf16[576,512]{1,0:T(8,128)(2,1)S(1)}, u32[]{:S(2)}, u32[]{:S(2)}) collective-permute-start(bf16[576,512]{1,0:T(8,128)(2,1)S(1)} %collective-permute-done.7.b3), channel_id=1, source_target_pairs={{0,1},{1,0},{2,3},{3,2},{4,5},{5,4},{6,7},{7,6},{8,9},{9,8},{10,11... | collective-permute-start | bytes 1769480 | tf_op jit(solution)/shard_map/ppermute | solution.py:425
  60.0 19.6 %copy-start.2 = (bf16[576,512]{1,0:T(8,128)(2,1)}, bf16[576,512]{1,0:T(8,128)(2,1)S(1)}, u32[]{:S(2)}) copy-start(bf16[576,512]{1,0:T(8,128)(2,1)S(1)} %collective-permute-done.5.b1) | copy-start | bytes 1769476
  60.0 19.6 %collective-permute-start.8 = (bf16[576,512]{1,0:T(8,128)(2,1)S(1)}, bf16[576,512]{1,0:T(8,128)(2,1)}, u32[]{:S(2)}, u32[]{:S(2)}) collective-permute-start(bf16[576,512]{1,0:T(8,128)(2,1)S(1)} %collective-permute-done.5.b1), channel_id=1, source_target_pairs={{0,1},{1,0},{2,3},{3,2},{4,5},{5,4},{6,7},{7,6},{8,9},{9,8},{10,11... | collective-permute-start | bytes 1769480 | tf_op jit(solution)/shard_map/ppermute | solution.py:425
  60.5 19.1 %copy-start.3 = (bf16[576,512]{1,0:T(8,128)(2,1)}, bf16[576,512]{1,0:T(8,128)(2,1)S(1)}, u32[]{:S(2)}) copy-start(bf16[576,512]{1,0:T(8,128)(2,1)S(1)} %collective-permute-done.6.b2) | copy-start | bytes 1769476
  60.5 19.2 %collective-permute-start.9 = (bf16[576,512]{1,0:T(8,128)(2,1)S(1)}, bf16[576,512]{1,0:T(8,128)(2,1)S(1)}, u32[]{:S(2)}, u32[]{:S(2)}) collective-permute-start(bf16[576,512]{1,0:T(8,128)(2,1)S(1)} %collective-permute-done.6.b2), channel_id=1, source_target_pairs={{0,1},{1,0},{2,3},{3,2},{4,5},{5,4},{6,7},{7,6},{8,9},{9,8},{10,11... | collective-permute-start | bytes 1769480 | tf_op jit(solution)/shard_map/ppermute | solution.py:425
  70.2 0.8 copy-start
  79.6 0.8 copy-start.5
  79.7 1.0 copy-start.6
  86.5 13.1 %collective-permute-start.11 = (bf16[256,512]{1,0:T(8,128)(2,1)}, bf16[256,512]{1,0:T(8,128)(2,1)S(1)}, u32[]{:S(2)}, u32[]{:S(2)}) collective-permute-start(bf16[256,512]{1,0:T(8,128)(2,1)} %mlp.1.back_ref), channel_id=1, source_target_pairs={{0,1},{1,2},{2,3},{3,4},{4,5},{5,6},{6,7},{7,8},{8,9},{9,10},{10,1... | collective-permute-start | bytes 786440 | tf_op jit(solution)/shard_map/ppermute | solution.py:455
  90.7 10.0 %collective-permute-start.12 = (bf16[256,512]{1,0:T(8,128)(2,1)}, bf16[256,512]{1,0:T(8,128)(2,1)S(1)}, u32[]{:S(2)}, u32[]{:S(2)}) collective-permute-start(bf16[256,512]{1,0:T(8,128)(2,1)} %mlp.1.back_ref), channel_id=1, source_target_pairs={{1,0},{2,1},{3,2},{4,3},{5,4},{6,5},{7,6},{8,7},{9,8},{10,9},{11,1... | collective-permute-start | bytes 786440 | tf_op jit(solution)/shard_map/ppermute | solution.py:456
  99.6 1.1 %copy-start.9 = (bf16[256,512]{1,0:T(8,128)(2,1)}, bf16[256,512]{1,0:T(8,128)(2,1)S(1)}, u32[]{:S(2)}) copy-start(bf16[256,512]{1,0:T(8,128)(2,1)S(1)} %collective-permute-done.11.below_ref) | copy-start | bytes 786436
  (4 other events, 2.9 us)

commit v2 on v1

v2 whole, which is shorter than its diff:
```python
import functools
import math

import jax
import jax.numpy as jnp
from jax import lax
from jax.experimental import pallas as pl
from jax.experimental.pallas import tpu as pltpu
from jax.sharding import PartitionSpec as P

DH = 128
EPS = 1e-05
BF = jnp.bfloat16
F32 = jnp.float32

HBM = pl.BlockSpec(memory_space=pltpu.HBM)
VMEM = pl.BlockSpec(memory_space=pltpu.VMEM)
SMEM = pl.BlockSpec(memory_space=pltpu.SMEM)


def dot(a, b):
    return jnp.dot(a, b, preferred_element_type=F32)


def dot_nt(a, b):
    return lax.dot_general(a, b, (((1,), (1,)), ((), ())), preferred_element_type=F32)


def silu(v):
    return v / (1.0 + jnp.exp(-v))


def hot_rows(row, count):
    ids = lax.broadcasted_iota(jnp.int32, (count, row.shape[1]), 0)
    return jnp.where(ids == row, 1.0, 0.0).astype(BF)


def live(row, length):
    slot = lax.broadcasted_iota(jnp.int32, row.shape, 1)
    return jnp.where(slot < length, row, -1)


def layer_norm(values, gain):
    centred = values - jnp.mean(values, axis=-1, keepdims=True)
    spread = jnp.mean(centred * centred, axis=-1, keepdims=True)
    return centred * lax.rsqrt(spread + EPS) * gain


def call(body, outs, operands, scratch=(), flops=0, nbytes=0, mib=24):
    specs = {"h": HBM, "v": VMEM, "d": VMEM, "s": SMEM}
    spaces = {"h": pltpu.HBM, "v": pltpu.VMEM}
    arrays = [
        pltpu.with_memory_space_constraint(a, spaces[w]) if w in spaces else a for w, a in operands
    ]
    kinds = {"h": pltpu.HBM, "v": pltpu.VMEM, "d": jax.ShapeDtypeStruct}
    shapes = [kinds[w](s, d) for w, s, d in outs]
    return pl.pallas_call(
        body,
        out_shape=shapes,
        in_specs=[specs[w] for w, _ in operands],
        out_specs=[specs[w] for w, _, _ in outs],
        scratch_shapes=list(scratch),
        compiler_params=pltpu.CompilerParams(vmem_limit_bytes=mib * 2**20),
        cost_estimate=pl.CostEstimate(flops=flops, bytes_accessed=nbytes, transcendentals=0),
    )(*arrays)


def around(bands):
    band = lax.axis_index("space")
    return band, jnp.minimum(band + 1, bands - 1), jnp.maximum(band - 1, 0)


def pick_body(
    bands, x_hbm, src_hbm, back_hbm, wq, wk, wv, wp, wu, wd, we_hbm, own_hbm, land_hbm,
    up_ref, down_ref, pack_ref, x_ref, we_ref, own_ref, land_ref, src_ref, back_ref, sem,
):
    band, upper, lower = around(bands)
    half = band % 2
    copies = [(src_hbm, src_ref), (back_hbm, back_ref), (x_hbm, x_ref)]
    copies += half_weights((wq, wk, wv, wp), wu, wd, half, pack_ref)
    copies += [(we_hbm, we_ref), (own_hbm, own_ref), (land_hbm, land_ref)]
    copies = start_all(copies, sem)
    for copy in copies[:3]:
        copy.wait()
    x = x_ref[...]
    rows = x.shape[0]
    slots = src_ref.shape[1]
    eye = lax.broadcasted_iota(jnp.int32, (slots, slots), 0) == lax.broadcasted_iota(
        jnp.int32, (slots, slots), 1
    )
    for out, at in ((up_ref, upper), (down_ref, lower)):
        wanted = src_ref[pl.ds(at, 1), :].astype(F32)
        column = jnp.sum(jnp.where(eye, wanted, 0.0), axis=1, keepdims=True).astype(jnp.int32)
        ids = lax.broadcasted_iota(jnp.int32, (slots, rows), 1)
        picker = jnp.where(ids == column, 1.0, 0.0).astype(BF)
        out[0:slots, :] = dot(picker, x).astype(BF)
        back = back_ref[pl.ds(at, 1), :].astype(F32)
        out[slots:, :] = jnp.broadcast_to(back, (out.shape[0] - slots, slots)).astype(BF)
    for copy in copies[3:]:
        copy.wait()


def start_all(pairs, sem, first=0):
    copies = [pltpu.make_async_copy(s, d, sem.at[first + i]) for i, (s, d) in enumerate(pairs)]
    for copy in copies:
        copy.start()
    return copies


def half_weights(square, wu, wd, half, pack_ref):
    _, piece, width = pack_ref.shape
    top = pl.multiple_of(half * piece, piece)
    deep = wd.shape[0] // 2
    count = len(square)
    pairs = [(w.at[pl.ds(top, piece)], pack_ref.at[i]) for i, w in enumerate(square)]
    pairs.append((wd.at[pl.ds(half * deep, deep)], pack_ref.at[count : count + deep]))
    for i in range(wu.shape[1] // width):
        pairs.append(
            (
                wu.at[pl.ds(top, piece), i * width : (i + 1) * width],
                pack_ref.at[count + deep + i],
            )
        )
    return pairs


def embed_body(bands, count, x_ref, we_ref, src_ref, dst_ref, len_ref, *refs):
    far, (latent_hbm, agg_ref), near, (latent_ref, sem) = (
        refs[:count],
        refs[count : count + 2],
        refs[count + 2 : -2],
        refs[-2:],
    )
    copies = start_all(list(zip(far, near)), sem)
    band, _, _ = around(bands)
    latent = silu(dot(x_ref[...], we_ref[...])).astype(BF)
    latent_ref[...] = latent
    copies += start_all([(latent_ref, latent_hbm)], sem, count)
    mesh_rows = agg_ref.shape[0]
    src_hot = hot_rows(src_ref[...], x_ref.shape[0])
    dst_hot = hot_rows(live(dst_ref[...], len_ref[band]), mesh_rows)
    links = dot_nt(dst_hot, src_hot).astype(BF)
    agg_ref[...] = dot(links, latent)
    for copy in copies:
        copy.wait()


def mesh_body(
    bands,
    agg_ref,
    below_ref,
    above_ref,
    dst_ref,
    len_ref,
    we_ref,
    ws_ref,
    wm_ref,
    static_ref,
    gain_ref,
    rows_ref,
    state_ref,
    normed_ref,
    halo_ref,
    wide,
    own,
):
    band, upper, lower = around(bands)
    total = agg_ref[...]
    mesh_rows = total.shape[0]
    slots = dst_ref.shape[1]
    for ref, at, there in ((below_ref, lower, band > 0), (above_ref, upper, band < bands - 1)):
        count = jnp.where(there, len_ref[at], 0)
        latent = silu(dot(ref[0:slots, :], we_ref[...])).astype(BF)
        dst_hot = hot_rows(live(dst_ref[pl.ds(at, 1), :], count), mesh_rows)
        total = total + dot(dst_hot, latent)
    agg = dot(total.astype(BF), ws_ref[...]).astype(BF)
    state = (static_ref[...].astype(F32) + silu(dot(agg, wm_ref[...]))).astype(BF)
    state_ref[...] = state
    normed = layer_norm(state.astype(F32), gain_ref[...]).astype(BF)
    normed_ref[...] = normed
    wide[...] = normed.astype(F32)
    published = own.shape[0]
    for j in range(published):
        own[j : j + 1, :] = wide[pl.ds(rows_ref[0, j], 1), :]
    halo = own[...].astype(BF)
    for b in range(bands):
        halo_ref[b * published : (b + 1) * published, :] = halo


def fill_body(
    bands, src_ref, dst_ref, far_dst_ref, len_ref, below_ref, above_ref, nbr_ref,
    links_hbm, rep_ref, links_ref, sem,
):
    band, upper, lower = around(bands)
    mesh_rows, table = rep_ref.shape
    rows = links_ref.shape[1]
    slots = far_dst_ref.shape[1]
    src_hot = hot_rows(src_ref[...], mesh_rows)
    dst_hot = hot_rows(live(dst_ref[...], len_ref[band]), rows)
    links_ref[0] = dot_nt(dst_hot, src_hot).astype(BF)
    for i, (ref, at, there) in enumerate(
        ((below_ref, lower, band > 0), (above_ref, upper, band < bands - 1))
    ):
        count = jnp.where(there, len_ref[at], 0)
        src = ref[slots : slots + 1, :].astype(F32).astype(jnp.int32)
        src_hot = hot_rows(src, mesh_rows)
        dst_hot = hot_rows(live(far_dst_ref[pl.ds(at, 1), :], count), rows)
        links_ref[i + 1] = dot_nt(dst_hot, src_hot).astype(BF)
    copies = start_all([(links_ref, links_hbm)], sem)
    labels = jnp.transpose(nbr_ref[...], (1, 0))
    ids = lax.broadcasted_iota(jnp.int32, (mesh_rows, table), 1)
    own = lax.broadcasted_iota(jnp.int32, (mesh_rows, 1), 0)
    repeats = jnp.where(ids == own, 1.0, 0.0)
    for k in range(labels.shape[1]):
        repeats = repeats + jnp.where(ids == labels[:, k : k + 1], 1.0, 0.0)
    rep_ref[...] = repeats
    for copy in copies:
        copy.wait()


def layer_body(
    normed_ref, far_ref, rep_ref, state_ref, gain_hbm, wr_hbm, wg_hbm, wq, wk, wv, wp, wu, wd,
    b1, b2, b3, s1, s2, s3, out_ref, m_ref, u_ref, d_ref, att_ref, gain_ref, wr_ref, wg_ref, sem,
):
    me = lax.axis_index("member")
    half = lax.axis_index("space") % 2
    square = (wq, wk, wv, wp)
    count = len(square)
    part, width = wq.shape
    piece = part // 2
    deep = wd.shape[0] // 2
    blocks = wu.shape[1] // width
    home = pl.multiple_of(me * part, part)
    heads = [(w, m_ref.at[i, pl.ds(home, part)]) for i, w in enumerate(square)]
    ups = [
        (wu.at[:, i * width : (i + 1) * width], u_ref.at[i, pl.ds(home, part)])
        for i in range(blocks)
    ]
    downs = [(wd, d_ref.at[pl.ds(me * 2 * deep, 2 * deep)])]
    for d, b, s in ((1, b1, s1), (3, b3, s3), (2, b2, s2)):
        source = (me - d) % 4
        for ref, side in ((b, half), (s, 1 - half)):
            at = pl.multiple_of(source * part + side * piece, piece)
            low = (source * 2 + side) * deep
            heads.append((ref.at[0:count], m_ref.at[:, pl.ds(at, piece)]))
            ups.append((ref.at[count + deep :], u_ref.at[:, pl.ds(at, piece)]))
            downs.append((ref.at[count : count + deep], d_ref.at[pl.ds(low, deep)]))
    heads = start_all(heads, sem)
    ups = start_all(ups, sem, len(heads))
    downs += [(wr_hbm, wr_ref), (wg_hbm, wg_ref)]
    heads_gain = start_all([(gain_hbm, gain_ref)], sem, len(heads) + len(ups) + len(downs))
    downs = start_all(downs, sem, len(heads) + len(ups))
    for copy in heads + heads_gain:
        copy.wait()
    normed = normed_ref[...]
    far = far_ref[...]
    queries = dot(normed, m_ref[0]).astype(BF)
    keys = jnp.concatenate([dot(normed, m_ref[1]).astype(BF), dot(far, m_ref[1]).astype(BF)], 0)
    values = jnp.concatenate([dot(normed, m_ref[2]).astype(BF), dot(far, m_ref[2]).astype(BF)], 0)
    for h in range(width // DH):
        at = slice(h * DH, (h + 1) * DH)
        repeats = rep_ref[...]
        scores = dot_nt(queries[:, at], keys[:, at]) / math.sqrt(DH)
        scores = jnp.where(repeats > 0.0, scores, -jnp.inf)
        top = jnp.max(scores, axis=-1, keepdims=True)
        weights = repeats * jnp.exp(scores - top)
        probs = (weights / jnp.sum(weights, axis=-1, keepdims=True)).astype(BF)
        att_ref[:, at] = dot(probs, values[:, at]).astype(BF)
    after = state_ref[...].astype(F32) + dot(att_ref[...], m_ref[3])
    normed = layer_norm(after, gain_ref[...]).astype(BF)
    for copy in ups + downs:
        copy.wait()
    total = after
    span = width // piece
    for i in range(blocks):
        expanded = silu(dot(normed, u_ref[i])).astype(BF)
        down = d_ref[i * span : (i + 1) * span].reshape(width, width)
        total = total + dot(expanded, down)
    back = dot(total.astype(BF), wr_ref[...]).astype(BF)
    out_ref[...] = dot(back, wg_ref[...]).astype(BF)


def part_body(
    back_ref, links_hbm, latent_hbm, ws_hbm, wo_hbm,
    out_ref, far_ref, wo_ref, own_ref, latent_ref, ws_ref, sem,
):
    copies = [(latent_hbm, latent_ref), (ws_hbm, ws_ref), (links_hbm.at[0], own_ref)]
    copies += [(links_hbm.at[1:3], far_ref), (wo_hbm, wo_ref)]
    copies = start_all(copies, sem)
    copies[0].wait()
    copies[1].wait()
    total = dot(latent_ref[...], ws_ref[...])
    copies[2].wait()
    out_ref[...] = total + dot(own_ref[...], back_ref[...])
    copies[3].wait()
    copies[4].wait()


def final_body(part_ref, links_ref, below_ref, above_ref, wo_ref, out_ref):
    total = part_ref[...] + dot(links_ref[0], below_ref[...])
    total = total + dot(links_ref[1], above_ref[...])
    out_ref[...] = dot_nt(wo_ref[...], silu(total).astype(BF)).astype(BF)


def shards(
    grid_in,
    mesh_embed,
    g2m_src,
    g2m_dst,
    g2m_own_src,
    g2m_own_dst,
    g2m_len,
    mesh_nbr,
    halo_rows,
    m2g_src,
    m2g_dst,
    m2g_own_src,
    m2g_own_dst,
    m2g_len,
    w_embed,
    w_send,
    w_mesh,
    attn_gain,
    w_query,
    w_key,
    w_value,
    w_project,
    mlp_gain,
    w_up,
    w_down,
    w_return,
    w_grid,
    w_skip,
    w_out,
):
    x = grid_in[0]
    rows, channels = x.shape
    mesh_rows, width = mesh_embed.shape
    bands = lax.axis_size("space")
    slots = g2m_src.shape[2]
    part = w_query.shape[0]
    piece = part // 2
    hidden = w_up.shape[1]
    published = halo_rows.shape[1]
    table = mesh_rows + bands * published
    g2m_count = g2m_len.reshape(-1)
    m2g_count = m2g_len.reshape(-1)
    w_deep = w_down.reshape(-1, piece, width)
    deep = w_deep.shape[0] // 2
    blocks = hidden // width
    square = (w_query, w_key, w_value, w_project)
    bind = functools.partial
    forward = [(i, i + 1) for i in range(bands - 1)]
    backward = [(i + 1, i) for i in range(bands - 1)]
    swap = [(i, i ^ 1) for i in range(bands)]

    def turn(block, d):
        return lax.ppermute(block, "member", [(i, (i + d) % 4) for i in range(4)])

    def like(a):
        return "v", a.shape, a.dtype

    def tag(where, *arrays):
        return [(where, a) for a in arrays]

    up, down, pack, x, w_embed, g2m_own_src, g2m_own_dst = call(
        bind(pick_body, bands),
        [
            ("v", (slots + 16, channels), BF),
            ("v", (slots + 16, channels), BF),
            ("v", (4 + deep + blocks, piece, width), BF),
            *map(like, (x, w_embed, g2m_own_src, g2m_own_dst)),
        ],
        tag("h", x, g2m_src[0], m2g_src[0], *square, w_up, w_deep, w_embed, g2m_own_src)
        + tag("h", g2m_own_dst),
        [
            pltpu.VMEM(g2m_src.shape[1:], jnp.int32),
            pltpu.VMEM(m2g_src.shape[1:], jnp.int32),
            pltpu.SemaphoreType.DMA((20,)),
        ],
        flops=int(3e8),
        nbytes=int(3e6),
    )
    below = lax.ppermute(up, "space", forward)
    above = lax.ppermute(down, "space", backward)
    b1, b3, b2 = turn(pack, 1), turn(pack, 3), turn(pack, 2)
    ahead = [
        g2m_dst[0],
        w_send,
        w_mesh,
        mesh_embed,
        attn_gain.reshape(1, width),
        m2g_own_src,
        m2g_own_dst,
        m2g_dst[0],
        mesh_nbr.T,
    ]
    latent, agg, *ahead = call(
        bind(embed_body, bands, len(ahead)),
        [("h", (rows, width), BF), ("v", (mesh_rows, width), F32), *map(like, ahead)],
        tag("v", x, w_embed, g2m_own_src, g2m_own_dst) + tag("s", g2m_count) + tag("h", *ahead),
        [pltpu.VMEM((rows, width), BF), pltpu.SemaphoreType.DMA((len(ahead) + 1,))],
        flops=int(3e9),
        nbytes=int(3e6),
    )
    state, normed, halo = call(
        bind(mesh_body, bands),
        [
            ("v", (mesh_rows, width), BF),
            ("v", (mesh_rows, width), BF),
            ("d", (bands * published, width), BF),
        ],
        tag("v", agg)
        + tag("d", below, above)
        + tag("v", ahead[0])
        + tag("s", g2m_count)
        + tag("v", w_embed, *ahead[1:5])
        + tag("s", halo_rows),
        [pltpu.VMEM((mesh_rows, width), F32), pltpu.VMEM((published, width), F32)],
        flops=int(1e9),
        nbytes=int(3e6),
    )
    far = lax.all_to_all(halo, "space", 0, 0, tiled=True)
    links, repeats = call(
        bind(fill_body, bands),
        [("h", (3, rows, mesh_rows), BF), ("v", (mesh_rows, table), F32)],
        tag("v", *ahead[5:8])
        + tag("s", m2g_count)
        + tag("d", below, above)
        + tag("v", ahead[8]),
        [pltpu.VMEM((3, rows, mesh_rows), BF), pltpu.SemaphoreType.DMA((1,))],
        flops=int(4e9),
        nbytes=int(8e6),
    )
    s1, s3, s2 = (lax.ppermute(b, "space", swap) for b in (b1, b3, b2))
    (back,) = call(
        layer_body,
        [("v", (mesh_rows, width), BF)],
        tag("v", normed)
        + tag("d", far)
        + tag("v", repeats, state)
        + tag("h", mlp_gain.reshape(1, width), w_return, w_grid)
        + tag("h", *square, w_up, w_deep, b1, b2, b3, s1, s2, s3),
        [
            pltpu.VMEM((4, 4 * part, width), BF),
            pltpu.VMEM((blocks, 4 * part, width), BF),
            pltpu.VMEM((8 * deep, piece, width), BF),
            pltpu.VMEM((mesh_rows, width), BF),
            pltpu.VMEM((1, width), F32),
            pltpu.VMEM((width, width), BF),
            pltpu.VMEM((width, width), BF),
            pltpu.SemaphoreType.DMA((40,)),
        ],
        flops=int(5e9),
        nbytes=int(6e6),
    )
    back_below = lax.ppermute(back, "space", forward)
    back_above = lax.ppermute(back, "space", backward)
    part, far_links, w_last = call(
        part_body,
        [("v", (rows, width), F32), ("v", (2, rows, mesh_rows), BF), like(w_out.T)],
        tag("v", back) + tag("h", links, latent, w_skip, w_out.T),
        [
            pltpu.VMEM((rows, mesh_rows), BF),
            pltpu.VMEM((rows, width), BF),
            pltpu.VMEM((width, width), BF),
            pltpu.SemaphoreType.DMA((5,)),
        ],
        flops=int(1e9),
        nbytes=int(2e6),
    )
    (result,) = call(
        final_body,
        [("d", (w_out.shape[1], rows), BF)],
        tag("v", part, far_links) + tag("d", back_below, back_above) + tag("v", w_last),
        flops=int(2e9),
        nbytes=int(8e6),
    )
    return result[None]


def solution(mesh):
    placed = (
        P("member", "space", None),
        P("space", None),
        P("space", None, None),
        P("space", None, None),
        P("space", None),
        P("space", None),
        P(None, "space"),
        P("space", None),
        P("space", None),
        P("space", None, None),
        P("space", None, None),
        P("space", None),
        P("space", None),
        P(None, "space"),
        P(),
        P(),
        P(),
        P(),
        P("member", None),
        P("member", None),
        P("member", None),
        P("member", None),
        P(),
        P("member", None),
        P("member", None),
        P(),
        P(),
        P(),
        P(),
    )
    return jax.shard_map(
        shards, mesh=mesh, in_specs=placed, out_specs=P("member", None, "space"), check_vma=False
    )
```

time: 108 us -> 89.3 us (0.83)
  Pallas kernels: 37.8 us -> 27 us
  local copies, waits for them, and re-layouts: 4.66 us -> 0.02 us
  waiting for transfers between devices: 36.8 us -> 33.8 us
    pallas_call x7, Pallas kernels: 37.8 us -> 27 us  [call(): pl.pallas_call(body, out_shape=shapes, in_specs=[specs[w] for w, _ in ope...]
    ppermute x1, waiting for transfers between devices: 6.56 us -> 0.01 us  [shards(): above = lax.ppermute(down, 'space', backward)]
    unnamed x28 -> x8, local copies, waits for them, and re-layouts: 4.66 us -> 0.02 us
    ppermute x6 -> x3, waiting for transfers between devices: 29.1 us -> 24.6 us  [turn(): return lax.ppermute(block, 'member', [(i, (i + d) % 4) for i in range(4)])]
    ppermute x1, waiting for transfers between devices: 1.13 us -> 5.32 us  [shards(): back_above = lax.ppermute(back, 'space', backward)]
    all_to_all x1, waiting for transfers between devices: 0.01 us -> 3.89 us  [shards(): far = lax.all_to_all(halo, 'space', 0, 0, tiled=True)]
    ppermute x3, starting transfers between devices: 0.78 us -> 3 us  [shards(): s1, s3, s2 = (lax.ppermute(b, 'space', swap) for b in (b1, b3, b2))]
    ppermute x6 -> x3, starting transfers between devices: 6.68 us -> 5.05 us  [turn(): return lax.ppermute(block, 'member', [(i, (i + d) % 4) for i in range(4)])]
  transfers between devices with their start and end apart: 14 -> 11, of which waited for: 4 -> 4; matrix products, arithmetic and copies ran while one was open for 0% -> 0% of each run, Pallas kernels for 22% -> 17%
where the time goes in v2:
time: 89.3 us; the launch traced here: 89 us
  waiting for transfers between devices  33.8 us (38%)
  starting transfers between devices  28 us (31%)
  Pallas kernels  27 us (30%)
    pallas_call x7, Pallas kernels, call(): pl.pallas_call(body, out_shape=shapes, in_specs=[specs[w] for w, _ in ope...  27 us
    ppermute x3, waiting for transfers between devices, turn(): return lax.ppermute(block, 'member', [(i, (i + d) % 4) for i in range(4)])  24.6 us
    all_to_all x1, starting transfers between devices, shards(): far = lax.all_to_all(halo, 'space', 0, 0, tiled=True)  8.51 us
    ppermute x1, waiting for transfers between devices, shards(): back_above = lax.ppermute(back, 'space', backward)  5.32 us
    ppermute x3, starting transfers between devices, turn(): return lax.ppermute(block, 'member', [(i, (i + d) % 4) for i in range(4)])  5.05 us
    ppermute x1, starting transfers between devices, shards(): below = lax.ppermute(up, 'space', forward)  4.85 us
    all_to_all x1, waiting for transfers between devices, shards(): far = lax.all_to_all(halo, 'space', 0, 0, tiled=True)  3.89 us
    ppermute x3, starting transfers between devices, shards(): s1, s3, s2 = (lax.ppermute(b, 'space', swap) for b in (b1, b3, b2))  3 us
  transfers between devices with their start and end apart: 11, of which 4 were waited for; matrix products, arithmetic and copies ran while one was open for 0% of the time, Pallas kernels for 17%

profile of v2, /device:TPU:7, one launch (start us, length us, event | category | flops | bytes accessed | tf_op | source)
XLA Modules:
  0.0 89.0 jit_solution(1177142805756077434)
XLA Ops:
  0.0 1.8 %shard_map.271 = (bf16[272,256]{1,0:T(8,128)(2,1)S(1)}, bf16[272,256]{1,0:T(8,128)(2,1)S(1)}, bf16[12,64,512]{2,1,0:T(8,128)(2,1)S(1)}, bf16[1024,256]{1,0:T(8,1...) custom-call(bf16[1024,256]{1,0:T(8,128)(2,1)} %bitcast.19, ...), custom_call_target="tpu_custom_call" | custom-call | flops 300000000 | bytes 3000000 | tf_op jit(solution)/shard_map/pallas_call | solution.py:57
  1.8 1.4 %collective-permute-start.2 = (bf16[12,64,512]{2,1,0:T(8,128)(2,1)S(1)}, bf16[12,64,512]{2,1,0:T(8,128)(2,1)S(1)}, u32[]{:S(2)}, u32[]{:S(2)}) collective-permute-start(bf16[12,64,512]{2,1,0:T(8,128)(2,1)S(1)} %get-tuple-element.51), channel_id=1, source_target_pairs={{0,32},{32,64},{64,96},{96,0},{1,33},{33,65},{65,97},{97,1},{2,34}... | collective-permute-start | bytes 2359304 | tf_op jit(solution)/shard_map/ppermute | solution.py:358
  3.2 2.6 %collective-permute-start.3 = (bf16[12,64,512]{2,1,0:T(8,128)(2,1)S(1)}, bf16[12,64,512]{2,1,0:T(8,128)(2,1)}, u32[]{:S(2)}, u32[]{:S(2)}) collective-permute-start(bf16[12,64,512]{2,1,0:T(8,128)(2,1)S(1)} %get-tuple-element.51), channel_id=1, source_target_pairs={{0,64},{32,96},{64,0},{96,32},{1,65},{33,97},{65,1},{97,33},{2,66}... | collective-permute-start | bytes 2359304 | tf_op jit(solution)/shard_map/ppermute | solution.py:358
  5.8 1.1 %collective-permute-start.4 = (bf16[12,64,512]{2,1,0:T(8,128)(2,1)S(1)}, bf16[12,64,512]{2,1,0:T(8,128)(2,1)}, u32[]{:S(2)}, u32[]{:S(2)}) collective-permute-start(bf16[12,64,512]{2,1,0:T(8,128)(2,1)S(1)} %get-tuple-element.51), channel_id=1, source_target_pairs={{0,96},{32,0},{64,32},{96,64},{1,97},{33,1},{65,33},{97,65},{2,98}... | collective-permute-start | bytes 2359304 | tf_op jit(solution)/shard_map/ppermute | solution.py:358
  6.9 4.8 %collective-permute-start = (bf16[272,256]{1,0:T(8,128)(2,1)S(1)}, bf16[272,256]{1,0:T(8,128)(2,1)S(1)}, u32[]{:S(2)}, u32[]{:S(2)}) collective-permute-start(bf16[272,256]{1,0:T(8,128)(2,1)S(1)} %get-tuple-element.36), channel_id=1, source_target_pairs={{0,1},{1,2},{2,3},{3,4},{4,5},{5,6},{6,7},{7,8},{8,9},{9,10},{10,1... | collective-permute-start | bytes 417800 | tf_op jit(solution)/shard_map/ppermute | solution.py:384
  11.7 1.9 %collective-permute-start.1 = (bf16[272,256]{1,0:T(8,128)(2,1)S(1)}, bf16[272,256]{1,0:T(8,128)(2,1)S(1)}, u32[]{:S(2)}, u32[]{:S(2)}) collective-permute-start(bf16[272,256]{1,0:T(8,128)(2,1)S(1)} %get-tuple-element.37), channel_id=1, source_target_pairs={{1,0},{2,1},{3,2},{4,3},{5,4},{6,5},{7,6},{8,7},{9,8},{10,9},{11,1... | collective-permute-start | bytes 417800 | tf_op jit(solution)/shard_map/ppermute | solution.py:385
  13.7 8.0 %collective-permute-done.2.b1 = bf16[12,64,512]{2,1,0:T(8,128)(2,1)S(1)} collective-permute-done((bf16[12,64,512]{2,1,0:T(8,128)(2,1)S(1)}, bf16[12,64,512]{2,1,0:T(8,128)(2,1)S(1)}, u32[]{:S(2)}, u32[]{:S(2)}) %collective-permute-start.2) | collective-permute-done | bytes 786464 | tf_op jit(solution)/shard_map/ppermute | solution.py:358
  21.6 1.5 %collective-permute-start.5 = (bf16[12,64,512]{2,1,0:T(8,128)(2,1)S(1)}, bf16[12,64,512]{2,1,0:T(8,128)(2,1)}, u32[]{:S(2)}, u32[]{:S(2)}) collective-permute-start(bf16[12,64,512]{2,1,0:T(8,128)(2,1)S(1)} %collective-permute-done.2.b1), channel_id=1, source_target_pairs={{0,1},{1,0},{2,3},{3,2},{4,5},{5,4},{6,7},{7,6},{8,9},{9,8},{10,11... | collective-permute-start | bytes 2359304 | tf_op jit(solution)/shard_map/ppermute | solution.py:435
  23.1 16.6 %collective-permute-done.3.b2 = bf16[12,64,512]{2,1,0:T(8,128)(2,1)} collective-permute-done((bf16[12,64,512]{2,1,0:T(8,128)(2,1)S(1)}, bf16[12,64,512]{2,1,0:T(8,128)(2,1)}, u32[]{:S(2)}, u32[]{:S(2)}) %collective-permute-start.3) | collective-permute-done | bytes 786464 | tf_op jit(solution)/shard_map/ppermute | solution.py:358
  39.7 1.5 %collective-permute-start.6 = (bf16[12,64,512]{2,1,0:T(8,128)(2,1)}, bf16[12,64,512]{2,1,0:T(8,128)(2,1)}, u32[]{:S(2)}, u32[]{:S(2)}) collective-permute-start(bf16[12,64,512]{2,1,0:T(8,128)(2,1)} %collective-permute-done.3.b2), channel_id=1, source_target_pairs={{0,1},{1,0},{2,3},{3,2},{4,5},{5,4},{6,7},{7,6},{8,9},{9,8},{10,11... | collective-permute-start | bytes 2359304 | tf_op jit(solution)/shard_map/ppermute | solution.py:435
  41.3 0.0 collective-permute-start.7
  41.3 0.0 copy-start.1
  41.3 2.9 %shard_map.272 = (bf16[1024,512]{1,0:T(8,128)(2,1)}, f32[256,512]{1,0:T(8,128)S(1)}, s32[32,256]{1,0:T(8,128)S(1)}, bf16[512,512]{1,0:T(8,128)(2,1)S(1)}, bf16[5...) custom-call(bf16[1024,256]{1,0:T(8,128)(2,1)S(1)} %get-tuple-element, ...), custom_call_target="tpu_custom_call" | custom-call | flops 3000000000 | bytes 3000000 | tf_op jit(solution)/shard_map/pallas_call | solution.py:57
  44.2 0.0 copy-start.2
  44.2 3.0 %shard_map.273 = (bf16[256,512]{1,0:T(8,128)(2,1)S(1)}, bf16[256,512]{1,0:T(8,128)(2,1)S(1)}, bf16[512,512]{1,0:T(8,128)(2,1)}) custom-call(f32[256,512]{1,0:T(8,128)S(1)} %get-tuple-element.35.agg_ref, bf16[272,256]{1,0:T(8,128)(2,1)S(1)} %collective-permute-done.below_ref, bf16[272,256]{1,0:T(8,128)(2,1)S(1)} %collective-permute-done.1.above_ref, ...), custom_call_target="tpu_custom_call" | custom-call | flops 1000000000 | bytes 3000000 | tf_op jit(solution)/shard_map/pallas_call | solution.py:57
  47.2 8.5 %all-to-all-start = ((bf16[32,16,512]{2,1,0:T(8,128)(2,1)}), bf16[32,16,512]{2,1,0:T(8,128)(2,1)S(1)}, u32[]{:S(2)}, u32[]{:S(2)}) async-start(bf16[32,16,512]{2,1,0:T(8,128)(2,1)} %bitcast.9), calls=%async_computation | async-start | bytes 1048576 | tf_op jit(solution)/shard_map/all_to_all | solution.py:423
  55.7 6.3 %shard_map.274 = (bf16[3,1024,256]{2,1,0:T(8,128)(2,1)}, f32[256,768]{1,0:T(8,128)S(1)}) custom-call(s32[1,2560]{1,0:T(1,128)S(1)} %get-tuple-element.45.src_ref, s32[1,2560]{1,0:T(1,128)S(1)} %get-tuple-element.46.dst_ref, s32[32,256]{1,0:T(8,128)S(1)} %get-tuple-element.47.far_dst_ref, s32[32]{0:T(128)S(1)} %bitcast.18, ...), custom_call_target="tpu_custom_call" | custom-call | flops 4000000000 | bytes 8000000 | tf_op jit(solution)/shard_map/pallas_call | solution.py:57
  62.1 3.9 %all-to-all-done = bf16[32,16,512]{2,1,0:T(8,128)(2,1)S(1)} async-done(((bf16[32,16,512]{2,1,0:T(8,128)(2,1)}), bf16[32,16,512]{2,1,0:T(8,128)(2,1)S(1)}, u32[]{:S(2)}, u32[]{:S(2)}) %all-to-all-start) | async-done | bytes 524320 | tf_op jit(solution)/shard_map/all_to_all | solution.py:423
  66.0 8.5 %shard_map.275.back_ref = bf16[256,512]{1,0:T(8,128)(2,1)S(1)} custom-call(bf16[256,512]{1,0:T(8,128)(2,1)S(1)} %get-tuple-element.43.normed_ref, bf16[512,512]{1,0:T(8,128)(2,1)S(1)} %bitcast.15, f32[256,768]{1,0:T(8,128)S(1)} %get-tuple-element.49.rep_ref, bf16[256,512]{1,0:T(8,128)(2,1)S(1)} %get-tuple-element.50.state_ref, f32[1,512]{1,0:T(1,128)} %bitcast.29, ...), custom_call_target="tpu_custom_call" | custom-call | flops 5000000000 | bytes 6000000 | tf_op jit(solution)/shard_map/pallas_call | solution.py:57
  74.5 2.8 %collective-permute-start.8 = (bf16[256,512]{1,0:T(8,128)(2,1)S(1)}, bf16[256,512]{1,0:T(8,128)(2,1)S(1)}, u32[]{:S(2)}, u32[]{:S(2)}) collective-permute-start(bf16[256,512]{1,0:T(8,128)(2,1)S(1)} %shard_map.275.back_ref), channel_id=1, source_target_pairs={{0,1},{1,2},{2,3},{3,4},{4,5},{5,6},{6,7},{7,8},{8,9},{9,10},{10,1... | collective-permute-start | bytes 786440 | tf_op jit(solution)/shard_map/ppermute | solution.py:457
  77.3 1.9 %collective-permute-start.9 = (bf16[256,512]{1,0:T(8,128)(2,1)S(1)}, bf16[256,512]{1,0:T(8,128)(2,1)S(1)}, u32[]{:S(2)}, u32[]{:S(2)}) collective-permute-start(bf16[256,512]{1,0:T(8,128)(2,1)S(1)} %shard_map.275.back_ref), channel_id=1, source_target_pairs={{1,0},{2,1},{3,2},{4,3},{5,4},{6,5},{7,6},{8,7},{9,8},{10,9},{11,1... | collective-permute-start | bytes 786440 | tf_op jit(solution)/shard_map/ppermute | solution.py:458
  79.2 2.5 %shard_map.276 = (f32[1024,512]{1,0:T(8,128)S(1)}, bf16[2,1024,256]{2,1,0:T(8,128)(2,1)S(1)}, bf16[84,512]{1,0:T(8,128)(2,1)S(1)}) custom-call(bf16[256,512]{1,0:T(8,128)(2,1)S(1)} %shard_map.275.back_ref, bf16[3,1024,256]{2,1,0:T(8,128)(2,1)} %get-tuple-element.52.links_hbm, bf16[1024,512]{1,0:T(8,128)(2,1)} %get-tuple-element.53.latent_hbm, ...), custom_call_target="tpu_custom_call" | custom-call | flops 1000000000 | bytes 2000000 | tf_op jit(solution)/shard_map/pallas_call | solution.py:57
  81.8 5.3 %collective-permute-done.9.above_ref = bf16[256,512]{1,0:T(8,128)(2,1)S(1)} collective-permute-done((bf16[256,512]{1,0:T(8,128)(2,1)S(1)}, bf16[256,512]{1,0:T(8,128)(2,1)S(1)}, u32[]{:S(2)}, u32[]{:S(2)}) %collective-permute-start.9) | collective-permute-done | bytes 262176 | tf_op jit(solution)/shard_map/ppermute | solution.py:458
  87.1 1.9 %shard_map.277 = bf16[84,1024]{1,0:T(8,128)(2,1)} custom-call(f32[1024,512]{1,0:T(8,128)S(1)} %get-tuple-element.54.part_ref, bf16[2,1024,256]{2,1,0:T(8,128)(2,1)S(1)} %get-tuple-element.55.links_ref, bf16[256,512]{1,0:T(8,128)(2,1)S(1)} %collective-permute-done.8.below_ref, bf16[256,512]{1,0:T(8,128)(2,1)S(1)} %collective-permute-done.9.above_ref, ...), custom_call_target="tpu_custom_call" | custom-call | flops 2000000000 | bytes 8000000 | tf_op jit(solution)/shard_map/pallas_call | solution.py:57
  (13 shorter events, 0.0 us)
Async XLA Ops:
  0.0 41.3 %copy-start = (s32[32,1]{0,1:T(1,128)S(1)}, s32[32,1]{0,1:T(1,128)}, u32[]{:S(2)}) copy-start(s32[32,1]{0,1:T(1,128)} %param.35) | copy-start | bytes 388
  1.8 19.8 %collective-permute-start.2 = (bf16[12,64,512]{2,1,0:T(8,128)(2,1)S(1)}, bf16[12,64,512]{2,1,0:T(8,128)(2,1)S(1)}, u32[]{:S(2)}, u32[]{:S(2)}) collective-permute-start(bf16[12,64,512]{2,1,0:T(8,128)(2,1)S(1)} %get-tuple-element.51), channel_id=1, source_target_pairs={{0,32},{32,64},{64,96},{96,0},{1,33},{33,65},{65,97},{97,1},{2,34}... | collective-permute-start | bytes 2359304 | tf_op jit(solution)/shard_map/ppermute | solution.py:358
  3.2 36.5 %collective-permute-start.3 = (bf16[12,64,512]{2,1,0:T(8,128)(2,1)S(1)}, bf16[12,64,512]{2,1,0:T(8,128)(2,1)}, u32[]{:S(2)}, u32[]{:S(2)}) collective-permute-start(bf16[12,64,512]{2,1,0:T(8,128)(2,1)S(1)} %get-tuple-element.51), channel_id=1, source_target_pairs={{0,64},{32,96},{64,0},{96,32},{1,65},{33,97},{65,1},{97,33},{2,66}... | collective-permute-start | bytes 2359304 | tf_op jit(solution)/shard_map/ppermute | solution.py:358
  5.8 35.5 %collective-permute-start.4 = (bf16[12,64,512]{2,1,0:T(8,128)(2,1)S(1)}, bf16[12,64,512]{2,1,0:T(8,128)(2,1)}, u32[]{:S(2)}, u32[]{:S(2)}) collective-permute-start(bf16[12,64,512]{2,1,0:T(8,128)(2,1)S(1)} %get-tuple-element.51), channel_id=1, source_target_pairs={{0,96},{32,0},{64,32},{96,64},{1,97},{33,1},{65,33},{97,65},{2,98}... | collective-permute-start | bytes 2359304 | tf_op jit(solution)/shard_map/ppermute | solution.py:358
  6.9 37.3 %collective-permute-start = (bf16[272,256]{1,0:T(8,128)(2,1)S(1)}, bf16[272,256]{1,0:T(8,128)(2,1)S(1)}, u32[]{:S(2)}, u32[]{:S(2)}) collective-permute-start(bf16[272,256]{1,0:T(8,128)(2,1)S(1)} %get-tuple-element.36), channel_id=1, source_target_pairs={{0,1},{1,2},{2,3},{3,4},{4,5},{5,6},{6,7},{7,8},{8,9},{9,10},{10,1... | collective-permute-start | bytes 417800 | tf_op jit(solution)/shard_map/ppermute | solution.py:384
  11.7 32.5 %collective-permute-start.1 = (bf16[272,256]{1,0:T(8,128)(2,1)S(1)}, bf16[272,256]{1,0:T(8,128)(2,1)S(1)}, u32[]{:S(2)}, u32[]{:S(2)}) collective-permute-start(bf16[272,256]{1,0:T(8,128)(2,1)S(1)} %get-tuple-element.37), channel_id=1, source_target_pairs={{1,0},{2,1},{3,2},{4,3},{5,4},{6,5},{7,6},{8,7},{9,8},{10,9},{11,1... | collective-permute-start | bytes 417800 | tf_op jit(solution)/shard_map/ppermute | solution.py:385
  21.6 22.5 %copy-start.3 = (bf16[12,64,512]{2,1,0:T(8,128)(2,1)}, bf16[12,64,512]{2,1,0:T(8,128)(2,1)S(1)}, u32[]{:S(2)}) copy-start(bf16[12,64,512]{2,1,0:T(8,128)(2,1)S(1)} %collective-permute-done.2.b1) | copy-start | bytes 2359300
  21.6 44.3 %collective-permute-start.5 = (bf16[12,64,512]{2,1,0:T(8,128)(2,1)S(1)}, bf16[12,64,512]{2,1,0:T(8,128)(2,1)}, u32[]{:S(2)}, u32[]{:S(2)}) collective-permute-start(bf16[12,64,512]{2,1,0:T(8,128)(2,1)S(1)} %collective-permute-done.2.b1), channel_id=1, source_target_pairs={{0,1},{1,0},{2,3},{3,2},{4,5},{5,4},{6,7},{7,6},{8,9},{9,8},{10,11... | collective-permute-start | bytes 2359304 | tf_op jit(solution)/shard_map/ppermute | solution.py:435
  39.7 26.3 %collective-permute-start.6 = (bf16[12,64,512]{2,1,0:T(8,128)(2,1)}, bf16[12,64,512]{2,1,0:T(8,128)(2,1)}, u32[]{:S(2)}, u32[]{:S(2)}) collective-permute-start(bf16[12,64,512]{2,1,0:T(8,128)(2,1)} %collective-permute-done.3.b2), channel_id=1, source_target_pairs={{0,1},{1,0},{2,3},{3,2},{4,5},{5,4},{6,7},{7,6},{8,9},{9,8},{10,11... | collective-permute-start | bytes 2359304 | tf_op jit(solution)/shard_map/ppermute | solution.py:435
  41.3 24.7 %collective-permute-start.7 = (bf16[12,64,512]{2,1,0:T(8,128)(2,1)}, bf16[12,64,512]{2,1,0:T(8,128)(2,1)}, u32[]{:S(2)}, u32[]{:S(2)}) collective-permute-start(bf16[12,64,512]{2,1,0:T(8,128)(2,1)} %collective-permute-done.4.b3), channel_id=1, source_target_pairs={{0,1},{1,0},{2,3},{3,2},{4,5},{5,4},{6,7},{7,6},{8,9},{9,8},{10,11... | collective-permute-start | bytes 2359304 | tf_op jit(solution)/shard_map/ppermute | solution.py:435
  41.3 2.9 %copy-start.1 = (s32[1,16]{1,0:T(1,128)S(1)}, s32[1,16]{1,0:T(1,128)}, u32[]{:S(2)}) copy-start(s32[1,16]{1,0:T(1,128)} %rows_ref.1) | copy-start | bytes 196
  44.2 11.5 %copy-start.2 = (s32[32,1]{0,1:T(1,128)S(1)}, s32[32,1]{0,1:T(1,128)}, u32[]{:S(2)}) copy-start(s32[32,1]{0,1:T(1,128)} %param.42) | copy-start | bytes 388
  47.2 18.8 %all-to-all-start = ((bf16[32,16,512]{2,1,0:T(8,128)(2,1)}), bf16[32,16,512]{2,1,0:T(8,128)(2,1)S(1)}, u32[]{:S(2)}, u32[]{:S(2)}) async-start(bf16[32,16,512]{2,1,0:T(8,128)(2,1)} %bitcast.9), calls=%async_computation | async-start | bytes 1048576 | tf_op jit(solution)/shard_map/all_to_all | solution.py:423
  74.5 7.2 %collective-permute-start.8 = (bf16[256,512]{1,0:T(8,128)(2,1)S(1)}, bf16[256,512]{1,0:T(8,128)(2,1)S(1)}, u32[]{:S(2)}, u32[]{:S(2)}) collective-permute-start(bf16[256,512]{1,0:T(8,128)(2,1)S(1)} %shard_map.275.back_ref), channel_id=1, source_target_pairs={{0,1},{1,2},{2,3},{3,4},{4,5},{5,6},{6,7},{7,8},{8,9},{9,10},{10,1... | collective-permute-start | bytes 786440 | tf_op jit(solution)/shard_map/ppermute | solution.py:457
  77.3 9.8 %collective-permute-start.9 = (bf16[256,512]{1,0:T(8,128)(2,1)S(1)}, bf16[256,512]{1,0:T(8,128)(2,1)S(1)}, u32[]{:S(2)}, u32[]{:S(2)}) collective-permute-start(bf16[256,512]{1,0:T(8,128)(2,1)S(1)} %shard_map.275.back_ref), channel_id=1, source_target_pairs={{1,0},{2,1},{3,2},{4,3},{5,4},{6,5},{7,6},{8,7},{9,8},{10,9},{11,1... | collective-permute-start | bytes 786440 | tf_op jit(solution)/shard_map/ppermute | solution.py:458

commit v3 on v2

--- a/solution.py
+++ b/solution.py
@@ -67,17 +67,19 @@
 
 def around(bands):
     band = lax.axis_index("space")
-    return band, jnp.minimum(band + 1, bands - 1), jnp.maximum(band - 1, 0)
+    odd = band % 2
+    cross = band - 1 + 2 * odd
+    there = (cross >= 0) & (cross < bands)
+    return band, band + 1 - 2 * odd, jnp.clip(cross, 0, bands - 1), there
 
 
 def pick_body(
     bands, x_hbm, src_hbm, back_hbm, wq, wk, wv, wp, wu, wd, we_hbm, own_hbm, land_hbm,
-    up_ref, down_ref, pack_ref, x_ref, we_ref, own_ref, land_ref, src_ref, back_ref, sem,
+    near_ref, cross_ref, a_ref, b_ref, x_ref, we_ref, own_ref, land_ref, src_ref, back_ref, sem,
 ):
-    band, upper, lower = around(bands)
-    half = band % 2
+    band, near, cross, _ = around(bands)
     copies = [(src_hbm, src_ref), (back_hbm, back_ref), (x_hbm, x_ref)]
-    copies += half_weights((wq, wk, wv, wp), wu, wd, half, pack_ref)
+    copies += half_weights((wq, wk, wv, wp), wu, wd, band % 2, a_ref, b_ref)
     copies += [(we_hbm, we_ref), (own_hbm, own_ref), (land_hbm, land_ref)]
     copies = start_all(copies, sem)
     for copy in copies[:3]:
@@ -88,7 +90,7 @@
     eye = lax.broadcasted_iota(jnp.int32, (slots, slots), 0) == lax.broadcasted_iota(
         jnp.int32, (slots, slots), 1
     )
-    for out, at in ((up_ref, upper), (down_ref, lower)):
+    for out, at in ((near_ref, near), (cross_ref, cross)):
         wanted = src_ref[pl.ds(at, 1), :].astype(F32)
         column = jnp.sum(jnp.where(eye, wanted, 0.0), axis=1, keepdims=True).astype(jnp.int32)
         ids = lax.broadcasted_iota(jnp.int32, (slots, rows), 1)
@@ -107,24 +109,23 @@
     return copies
 
 
-def half_weights(square, wu, wd, half, pack_ref):
-    _, piece, width = pack_ref.shape
+def half_weights(square, wu, wd, half, a_ref, b_ref):
+    _, piece, width = a_ref.shape
     top = pl.multiple_of(half * piece, piece)
-    deep = wd.shape[0] // 2
+    deep = wd.shape[0] // 4
+    low = half * 2 * deep
     count = len(square)
-    pairs = [(w.at[pl.ds(top, piece)], pack_ref.at[i]) for i, w in enumerate(square)]
-    pairs.append((wd.at[pl.ds(half * deep, deep)], pack_ref.at[count : count + deep]))
+    pairs = [(w.at[pl.ds(top, piece)], a_ref.at[i]) for i, w in enumerate(square)]
+    pairs.append((wd.at[pl.ds(low, deep)], a_ref.at[count:]))
+    pairs.append((wd.at[pl.ds(low + deep, deep)], b_ref.at[0:deep]))
     for i in range(wu.shape[1] // width):
         pairs.append(
-            (
-                wu.at[pl.ds(top, piece), i * width : (i + 1) * width],
-                pack_ref.at[count + deep + i],
-            )
+            (wu.at[pl.ds(top, piece), i * width : (i + 1) * width], b_ref.at[deep + i])
         )
     return pairs
 
 
-def embed_body(bands, count, x_ref, we_ref, src_ref, dst_ref, len_ref, *refs):
+def embed_body(count, x_ref, we_ref, src_ref, dst_ref, len_ref, *refs):
     far, (latent_hbm, agg_ref), near, (latent_ref, sem) = (
         refs[:count],
         refs[count : count + 2],
@@ -132,7 +133,7 @@
         refs[-2:],
     )
     copies = start_all(list(zip(far, near)), sem)
-    band, _, _ = around(bands)
+    band = lax.axis_index("space")
     latent = silu(dot(x_ref[...], we_ref[...])).astype(BF)
     latent_ref[...] = latent
     copies += start_all([(latent_ref, latent_hbm)], sem, count)
@@ -148,8 +149,8 @@
 def mesh_body(
     bands,
     agg_ref,
-    below_ref,
-    above_ref,
+    near_ref,
+    cross_ref,
     dst_ref,
     len_ref,
     we_ref,
@@ -164,12 +165,12 @@
     wide,
     own,
 ):
-    band, upper, lower = around(bands)
+    _, near, cross, there = around(bands)
     total = agg_ref[...]
     mesh_rows = total.shape[0]
     slots = dst_ref.shape[1]
-    for ref, at, there in ((below_ref, lower, band > 0), (above_ref, upper, band < bands - 1)):
-        count = jnp.where(there, len_ref[at], 0)
+    for ref, at, some in ((near_ref, near, True), (cross_ref, cross, there)):
+        count = jnp.where(some, len_ref[at], 0)
         latent = silu(dot(ref[0:slots, :], we_ref[...])).astype(BF)
         dst_hot = hot_rows(live(dst_ref[pl.ds(at, 1), :], count), mesh_rows)
         total = total + dot(dst_hot, latent)
@@ -188,20 +189,18 @@
 
 
 def fill_body(
-    bands, src_ref, dst_ref, far_dst_ref, len_ref, below_ref, above_ref, nbr_ref,
+    bands, src_ref, dst_ref, far_dst_ref, len_ref, near_ref, cross_ref, nbr_ref,
     links_hbm, rep_ref, links_ref, sem,
 ):
-    band, upper, lower = around(bands)
+    band, near, cross, there = around(bands)
     mesh_rows, table = rep_ref.shape
     rows = links_ref.shape[1]
     slots = far_dst_ref.shape[1]
     src_hot = hot_rows(src_ref[...], mesh_rows)
     dst_hot = hot_rows(live(dst_ref[...], len_ref[band]), rows)
     links_ref[0] = dot_nt(dst_hot, src_hot).astype(BF)
-    for i, (ref, at, there) in enumerate(
-        ((below_ref, lower, band > 0), (above_ref, upper, band < bands - 1))
-    ):
-        count = jnp.where(there, len_ref[at], 0)
+    for i, (ref, at, some) in enumerate(((near_ref, near, True), (cross_ref, cross, there))):
+        count = jnp.where(some, len_ref[at], 0)
         src = ref[slots : slots + 1, :].astype(F32).astype(jnp.int32)
         src_hot = hot_rows(src, mesh_rows)
         dst_hot = hot_rows(live(far_dst_ref[pl.ds(at, 1), :], count), rows)
@@ -219,16 +218,17 @@
 
 
 def layer_body(
-    normed_ref, far_ref, rep_ref, state_ref, gain_hbm, wr_hbm, wg_hbm, wq, wk, wv, wp, wu, wd,
-    b1, b2, b3, s1, s2, s3, out_ref, m_ref, u_ref, d_ref, att_ref, gain_ref, wr_ref, wg_ref, sem,
+    normed_ref, far_ref, rep_ref, state_ref, gain_hbm, wr_hbm, wg_hbm, wq, wk, wv, wp, wu, wd, *refs
 ):
+    pieces, refs = refs[:12], refs[12:]
+    out_ref, m_ref, u_ref, d_ref, att_ref, gain_ref, wr_ref, wg_ref, sem = refs
     me = lax.axis_index("member")
     half = lax.axis_index("space") % 2
     square = (wq, wk, wv, wp)
     count = len(square)
     part, width = wq.shape
     piece = part // 2
-    deep = wd.shape[0] // 2
+    deep = wd.shape[0] // 4
     blocks = wu.shape[1] // width
     home = pl.multiple_of(me * part, part)
     heads = [(w, m_ref.at[i, pl.ds(home, part)]) for i, w in enumerate(square)]
@@ -236,15 +236,16 @@
         (wu.at[:, i * width : (i + 1) * width], u_ref.at[i, pl.ds(home, part)])
         for i in range(blocks)
     ]
-    downs = [(wd, d_ref.at[pl.ds(me * 2 * deep, 2 * deep)])]
-    for d, b, s in ((1, b1, s1), (3, b3, s3), (2, b2, s2)):
-        source = (me - d) % 4
-        for ref, side in ((b, half), (s, 1 - half)):
+    downs = [(wd, d_ref.at[pl.ds(me * 4 * deep, 4 * deep)])]
+    for j, d in enumerate((1, 3, 2)):
+        source = me ^ d
+        for side, (a, b) in ((half, pieces[2 * j : 2 * j + 2]), (1 - half, pieces[2 * j + 6 : 2 * j + 8])):
             at = pl.multiple_of(source * part + side * piece, piece)
-            low = (source * 2 + side) * deep
-            heads.append((ref.at[0:count], m_ref.at[:, pl.ds(at, piece)]))
-            ups.append((ref.at[count + deep :], u_ref.at[:, pl.ds(at, piece)]))
-            downs.append((ref.at[count : count + deep], d_ref.at[pl.ds(low, deep)]))
+            low = (source * 2 + side) * 2 * deep
+            heads.append((a.at[0:count], m_ref.at[:, pl.ds(at, piece)]))
+            ups.append((b.at[deep:], u_ref.at[:, pl.ds(at, piece)]))
+            downs.append((a.at[count:], d_ref.at[pl.ds(low, deep)]))
+            downs.append((b.at[0:deep], d_ref.at[pl.ds(low + deep, deep)]))
     heads = start_all(heads, sem)
     ups = start_all(ups, sem, len(heads))
     downs += [(wr_hbm, wr_ref), (wg_hbm, wg_ref)]
@@ -296,9 +297,9 @@
     copies[4].wait()
 
 
-def final_body(part_ref, links_ref, below_ref, above_ref, wo_ref, out_ref):
-    total = part_ref[...] + dot(links_ref[0], below_ref[...])
-    total = total + dot(links_ref[1], above_ref[...])
+def final_body(part_ref, links_ref, near_ref, cross_ref, wo_ref, out_ref):
+    total = part_ref[...] + dot(links_ref[0], near_ref[...])
+    total = total + dot(links_ref[1], cross_ref[...])
     out_ref[...] = dot_nt(wo_ref[...], silu(total).astype(BF)).astype(BF)
 
 
@@ -346,16 +347,18 @@
     g2m_count = g2m_len.reshape(-1)
     m2g_count = m2g_len.reshape(-1)
     w_deep = w_down.reshape(-1, piece, width)
-    deep = w_deep.shape[0] // 2
+    deep = w_deep.shape[0] // 4
     blocks = hidden // width
     square = (w_query, w_key, w_value, w_project)
     bind = functools.partial
-    forward = [(i, i + 1) for i in range(bands - 1)]
-    backward = [(i + 1, i) for i in range(bands - 1)]
     swap = [(i, i ^ 1) for i in range(bands)]
+    chain = [(i, j) for i in range(bands) for j in (i - 1 + i % 2 * 2,) if 0 <= j < bands]
 
     def turn(block, d):
-        return lax.ppermute(block, "member", [(i, (i + d) % 4) for i in range(4)])
+        return lax.ppermute(block, "member", [(i, i ^ d) for i in range(4)])
+
+    def pass_on(block, route):
+        return lax.ppermute(block, "space", route)
 
     def like(a):
         return "v", a.shape, a.dtype
@@ -363,12 +366,13 @@
     def tag(where, *arrays):
         return [(where, a) for a in arrays]
 
-    up, down, pack, x, w_embed, g2m_own_src, g2m_own_dst = call(
+    near, cross, own_a, own_b, x, w_embed, g2m_own_src, g2m_own_dst = call(
         bind(pick_body, bands),
         [
             ("v", (slots + 16, channels), BF),
             ("v", (slots + 16, channels), BF),
-            ("v", (4 + deep + blocks, piece, width), BF),
+            ("v", (4 + deep, piece, width), BF),
+            ("v", (deep + blocks, piece, width), BF),
             *map(like, (x, w_embed, g2m_own_src, g2m_own_dst)),
         ],
         tag("h", x, g2m_src[0], m2g_src[0], *square, w_up, w_deep, w_embed, g2m_own_src)
@@ -381,9 +385,14 @@
         flops=int(3e8),
         nbytes=int(3e6),
     )
-    below = lax.ppermute(up, "space", forward)
-    above = lax.ppermute(down, "space", backward)
-    b1, b3, b2 = turn(pack, 1), turn(pack, 3), turn(pack, 2)
+    a1 = turn(own_a, 1)
+    b3 = turn(own_b, 3)
+    near = pass_on(near, swap)
+    cross = pass_on(cross, chain)
+    b1 = turn(own_b, 1)
+    a3 = turn(own_a, 3)
+    a2 = turn(a1, 3)
+    b2 = turn(b3, 1)
     ahead = [
         g2m_dst[0],
         w_send,
@@ -396,7 +405,7 @@
         mesh_nbr.T,
     ]
     latent, agg, *ahead = call(
-        bind(embed_body, bands, len(ahead)),
+        bind(embed_body, len(ahead)),
         [("h", (rows, width), BF), ("v", (mesh_rows, width), F32), *map(like, ahead)],
         tag("v", x, w_embed, g2m_own_src, g2m_own_dst) + tag("s", g2m_count) + tag("h", *ahead),
         [pltpu.VMEM((rows, width), BF), pltpu.SemaphoreType.DMA((len(ahead) + 1,))],
@@ -411,7 +420,7 @@
             ("d", (bands * published, width), BF),
         ],
         tag("v", agg)
-        + tag("d", below, above)
+        + tag("d", near, cross)
         + tag("v", ahead[0])
         + tag("s", g2m_count)
         + tag("v", w_embed, *ahead[1:5])
@@ -426,13 +435,14 @@
         [("h", (3, rows, mesh_rows), BF), ("v", (mesh_rows, table), F32)],
         tag("v", *ahead[5:8])
         + tag("s", m2g_count)
-        + tag("d", below, above)
+        + tag("d", near, cross)
         + tag("v", ahead[8]),
         [pltpu.VMEM((3, rows, mesh_rows), BF), pltpu.SemaphoreType.DMA((1,))],
         flops=int(4e9),
         nbytes=int(8e6),
     )
-    s1, s3, s2 = (lax.ppermute(b, "space", swap) for b in (b1, b3, b2))
+    fetched = a1, b1, a3, b3, a2, b2
+    shared = [pass_on(w, swap) for w in fetched]
     (back,) = call(
         layer_body,
         [("v", (mesh_rows, width), BF)],
@@ -440,22 +450,22 @@
         + tag("d", far)
         + tag("v", repeats, state)
         + tag("h", mlp_gain.reshape(1, width), w_return, w_grid)
-        + tag("h", *square, w_up, w_deep, b1, b2, b3, s1, s2, s3),
+        + tag("h", *square, w_up, w_deep, *fetched, *shared),
         [
             pltpu.VMEM((4, 4 * part, width), BF),
             pltpu.VMEM((blocks, 4 * part, width), BF),
-            pltpu.VMEM((8 * deep, piece, width), BF),
+            pltpu.VMEM((16 * deep, piece, width), BF),
             pltpu.VMEM((mesh_rows, width), BF),
             pltpu.VMEM((1, width), F32),
             pltpu.VMEM((width, width), BF),
             pltpu.VMEM((width, width), BF),
-            pltpu.SemaphoreType.DMA((40,)),
+            pltpu.SemaphoreType.DMA((64,)),
         ],
         flops=int(5e9),
         nbytes=int(6e6),
     )
-    back_below = lax.ppermute(back, "space", forward)
-    back_above = lax.ppermute(back, "space", backward)
+    back_near = pass_on(back, swap)
+    back_cross = pass_on(back, chain)
     part, far_links, w_last = call(
         part_body,
         [("v", (rows, width), F32), ("v", (2, rows, mesh_rows), BF), like(w_out.T)],
@@ -472,7 +482,7 @@
     (result,) = call(
         final_body,
         [("d", (w_out.shape[1], rows), BF)],
-        tag("v", part, far_links) + tag("d", back_below, back_above) + tag("v", w_last),
+        tag("v", part, far_links) + tag("d", back_near, back_cross) + tag("v", w_last),
         flops=int(2e9),
         nbytes=int(8e6),
     )

time: 89.3 us -> 64.9 us (0.73)
  waiting for transfers between devices: 33.8 us -> 9.33 us
  starting transfers between devices: 28 us -> 27 us
    ppermute x10 -> x16, waiting for transfers between devices: 29.9 us -> 6.99 us  [the longest x10 4.61 us: pass_on(): return lax.ppermute(block, 'space', route)]
    all_to_all x1, waiting for transfers between devices: 3.89 us -> 2.34 us  [shards(): far = lax.all_to_all(halo, 'space', 0, 0, tiled=True)]
    ppermute x10 -> x16, starting transfers between devices: 19.5 us -> 18.6 us  [the longest x10 11.3 us: pass_on(): return lax.ppermute(block, 'space', route)]
  transfers between devices with their start and end apart: 11 -> 17, of which waited for: 4 -> 4; matrix products, arithmetic and copies ran while one was open for 0% -> 0% of each run, Pallas kernels for 17% -> 23%
where the time goes in v3:
time: 64.9 us; the launch traced here: 64.5 us
  Pallas kernels  27.2 us (42%)
  starting transfers between devices  27 us (42%)
  waiting for transfers between devices  9.33 us (14%)
  local copies, waits for them, and re-layouts  0.77 us (1%)
    pallas_call x7, Pallas kernels, call(): pl.pallas_call(body, out_shape=shapes, in_specs=[specs[w] for w, _ in ope...  27.2 us
    ppermute x10, starting transfers between devices, pass_on(): return lax.ppermute(block, 'space', route)  11.3 us
    all_to_all x1, starting transfers between devices, shards(): far = lax.all_to_all(halo, 'space', 0, 0, tiled=True)  8.41 us
    ppermute x6, starting transfers between devices, turn(): return lax.ppermute(block, 'member', [(i, i ^ d) for i in range(4)])  7.33 us
    ppermute x10, waiting for transfers between devices, pass_on(): return lax.ppermute(block, 'space', route)  4.61 us
    ppermute x6, waiting for transfers between devices, turn(): return lax.ppermute(block, 'member', [(i, i ^ d) for i in range(4)])  2.38 us
    all_to_all x1, waiting for transfers between devices, shards(): far = lax.all_to_all(halo, 'space', 0, 0, tiled=True)  2.34 us
  transfers between devices with their start and end apart: 17, of which 4 were waited for; matrix products, arithmetic and copies ran while one was open for 0% of the time, Pallas kernels for 23%

profile of v3, /device:TPU:7, one launch (start us, length us, event | category | flops | bytes accessed | tf_op | source)
XLA Modules:
  0.0 64.5 jit_solution(1749626682954664351)
XLA Ops:
  0.0 1.8 %shard_map.271 = (bf16[272,256]{1,0:T(8,128)(2,1)S(1)}, bf16[272,256]{1,0:T(8,128)(2,1)S(1)}, bf16[6,64,512]{2,1,0:T(8,128)(2,1)S(1)}, bf16[6,64,512]{2,1,0:T(8,...) custom-call(bf16[1024,256]{1,0:T(8,128)(2,1)} %bitcast.19, ...), custom_call_target="tpu_custom_call" | custom-call | flops 300000000 | bytes 3000000 | tf_op jit(solution)/shard_map/pallas_call | solution.py:57
  1.8 2.8 %collective-permute-start.5 = (bf16[6,64,512]{2,1,0:T(8,128)(2,1)S(1)}, bf16[6,64,512]{2,1,0:T(8,128)(2,1)S(1)}, u32[]{:S(2)}, u32[]{:S(2)}) collective-permute-start(bf16[6,64,512]{2,1,0:T(8,128)(2,1)S(1)} %get-tuple-element.53), channel_id=1, source_target_pairs={{0,96},{32,64},{64,32},{96,0},{1,97},{33,65},{65,33},{97,1},{2,98}... | collective-permute-start | bytes 1179656 | tf_op jit(solution)/shard_map/ppermute | solution.py:358
  4.6 1.1 %collective-permute-start = (bf16[272,256]{1,0:T(8,128)(2,1)S(1)}, bf16[272,256]{1,0:T(8,128)(2,1)S(1)}, u32[]{:S(2)}, u32[]{:S(2)}) collective-permute-start(bf16[272,256]{1,0:T(8,128)(2,1)S(1)} %get-tuple-element.37), channel_id=1, source_target_pairs={{0,1},{1,0},{2,3},{3,2},{4,5},{5,4},{6,7},{7,6},{8,9},{9,8},{10,11... | collective-permute-start | bytes 417800 | tf_op jit(solution)/shard_map/ppermute | solution.py:361
  5.7 3.3 %collective-permute-start.1 = (bf16[272,256]{1,0:T(8,128)(2,1)S(1)}, bf16[272,256]{1,0:T(8,128)(2,1)S(1)}, u32[]{:S(2)}, u32[]{:S(2)}) collective-permute-start(bf16[272,256]{1,0:T(8,128)(2,1)S(1)} %get-tuple-element.38), channel_id=1, source_target_pairs={{1,2},{2,1},{3,4},{4,3},{5,6},{6,5},{7,8},{8,7},{9,10},{10,9},{11,... | collective-permute-start | bytes 417800 | tf_op jit(solution)/shard_map/ppermute | solution.py:361
  9.1 0.9 %collective-permute-start.4 = (bf16[6,64,512]{2,1,0:T(8,128)(2,1)S(1)}, bf16[6,64,512]{2,1,0:T(8,128)(2,1)S(1)}, u32[]{:S(2)}, u32[]{:S(2)}) collective-permute-start(bf16[6,64,512]{2,1,0:T(8,128)(2,1)S(1)} %get-tuple-element.52), channel_id=1, source_target_pairs={{0,96},{32,64},{64,32},{96,0},{1,97},{33,65},{65,33},{97,1},{2,98}... | collective-permute-start | bytes 1179656 | tf_op jit(solution)/shard_map/ppermute | solution.py:358
  9.9 0.9 %collective-permute-start.3 = (bf16[6,64,512]{2,1,0:T(8,128)(2,1)S(1)}, bf16[6,64,512]{2,1,0:T(8,128)(2,1)}, u32[]{:S(2)}, u32[]{:S(2)}) collective-permute-start(bf16[6,64,512]{2,1,0:T(8,128)(2,1)S(1)} %get-tuple-element.53), channel_id=1, source_target_pairs={{0,32},{32,0},{64,96},{96,64},{1,33},{33,1},{65,97},{97,65},{2,34}... | collective-permute-start | bytes 1179656 | tf_op jit(solution)/shard_map/ppermute | solution.py:358
  10.9 2.4 %collective-permute-done.5.refs_3_ = bf16[6,64,512]{2,1,0:T(8,128)(2,1)S(1)} collective-permute-done((bf16[6,64,512]{2,1,0:T(8,128)(2,1)S(1)}, bf16[6,64,512]{2,1,0:T(8,128)(2,1)S(1)}, u32[]{:S(2)}, u32[]{:S(2)}) %collective-permute-start.5) | collective-permute-done | bytes 393248 | tf_op jit(solution)/shard_map/ppermute | solution.py:358
  13.2 1.0 %collective-permute-done.1.cross_ref = bf16[272,256]{1,0:T(8,128)(2,1)S(1)} collective-permute-done((bf16[272,256]{1,0:T(8,128)(2,1)S(1)}, bf16[272,256]{1,0:T(8,128)(2,1)S(1)}, u32[]{:S(2)}, u32[]{:S(2)}) %collective-permute-start.1) | collective-permute-done | bytes 139296 | tf_op jit(solution)/shard_map/ppermute | solution.py:361
  14.2 1.7 %collective-permute-start.11 = (bf16[6,64,512]{2,1,0:T(8,128)(2,1)S(1)}, bf16[6,64,512]{2,1,0:T(8,128)(2,1)}, u32[]{:S(2)}, u32[]{:S(2)}) collective-permute-start(bf16[6,64,512]{2,1,0:T(8,128)(2,1)S(1)} %collective-permute-done.5.refs_3_), channel_id=1, source_target_pairs={{0,1},{1,0},{2,3},{3,2},{4,5},{5,4},{6,7},{7,6},{8,9},{9,8},{10,11... | collective-permute-start | bytes 1179656 | tf_op jit(solution)/shard_map/ppermute | solution.py:361
  15.9 2.7 %collective-permute-start.6 = (bf16[6,64,512]{2,1,0:T(8,128)(2,1)S(1)}, bf16[6,64,512]{2,1,0:T(8,128)(2,1)}, u32[]{:S(2)}, u32[]{:S(2)}) collective-permute-start(bf16[6,64,512]{2,1,0:T(8,128)(2,1)S(1)} %collective-permute-done.2.refs_0_), channel_id=1, source_target_pairs={{0,96},{32,64},{64,32},{96,0},{1,97},{33,65},{65,33},{97,1},{2,98}... | collective-permute-start | bytes 1179656 | tf_op jit(solution)/shard_map/ppermute | solution.py:358
  18.6 2.9 %shard_map.272 = (bf16[1024,512]{1,0:T(8,128)(2,1)}, f32[256,512]{1,0:T(8,128)S(1)}, s32[32,256]{1,0:T(8,128)S(1)}, bf16[512,512]{1,0:T(8,128)(2,1)S(1)}, bf16[5...) custom-call(bf16[1024,256]{1,0:T(8,128)(2,1)S(1)} %get-tuple-element, ...), custom_call_target="tpu_custom_call" | custom-call | flops 3000000000 | bytes 3000000 | tf_op jit(solution)/shard_map/pallas_call | solution.py:57
  21.5 3.0 %shard_map.273 = (bf16[256,512]{1,0:T(8,128)(2,1)S(1)}, bf16[256,512]{1,0:T(8,128)(2,1)S(1)}, bf16[512,512]{1,0:T(8,128)(2,1)}) custom-call(f32[256,512]{1,0:T(8,128)S(1)} %get-tuple-element.36.agg_ref, bf16[272,256]{1,0:T(8,128)(2,1)S(1)} %collective-permute-done.near_ref, bf16[272,256]{1,0:T(8,128)(2,1)S(1)} %collective-permute-done.1.cross_ref, ...), custom_call_target="tpu_custom_call" | custom-call | flops 1000000000 | bytes 3000000 | tf_op jit(solution)/shard_map/pallas_call | solution.py:57
  24.5 8.4 %all-to-all-start = ((bf16[32,16,512]{2,1,0:T(8,128)(2,1)}), bf16[32,16,512]{2,1,0:T(8,128)(2,1)S(1)}, u32[]{:S(2)}, u32[]{:S(2)}) async-start(bf16[32,16,512]{2,1,0:T(8,128)(2,1)} %bitcast.9), calls=%async_computation | async-start | bytes 1048576 | tf_op jit(solution)/shard_map/all_to_all | solution.py:432
  33.0 0.5 collective-permute-start.8
  33.6 0.4 collective-permute-start.9
  34.1 0.4 collective-permute-start.13
  34.5 6.4 %shard_map.274 = (bf16[3,1024,256]{2,1,0:T(8,128)(2,1)}, f32[256,768]{1,0:T(8,128)S(1)}) custom-call(s32[1,2560]{1,0:T(1,128)S(1)} %get-tuple-element.46.src_ref, s32[1,2560]{1,0:T(1,128)S(1)} %get-tuple-element.47.dst_ref, s32[32,256]{1,0:T(8,128)S(1)} %get-tuple-element.48.far_dst_ref, s32[32]{0:T(128)S(1)} %bitcast.18, ...), custom_call_target="tpu_custom_call" | custom-call | flops 4000000000 | bytes 8000000 | tf_op jit(solution)/shard_map/pallas_call | solution.py:57
  40.8 2.3 %all-to-all-done = bf16[32,16,512]{2,1,0:T(8,128)(2,1)S(1)} async-done(((bf16[32,16,512]{2,1,0:T(8,128)(2,1)}), bf16[32,16,512]{2,1,0:T(8,128)(2,1)S(1)}, u32[]{:S(2)}, u32[]{:S(2)}) %all-to-all-start) | async-done | bytes 524320 | tf_op jit(solution)/shard_map/all_to_all | solution.py:432
  43.2 0.7 %copy-done.6 = bf16[6,64,512]{2,1,0:T(8,128)(2,1)} copy-done((bf16[6,64,512]{2,1,0:T(8,128)(2,1)}, bf16[6,64,512]{2,1,0:T(8,128)(2,1)S(1)}, u32[]{:S(2)}) %copy-start.6) | copy-done | bytes 393240
  44.0 8.7 %shard_map.275.back_ref = bf16[256,512]{1,0:T(8,128)(2,1)S(1)} custom-call(bf16[256,512]{1,0:T(8,128)(2,1)S(1)} %get-tuple-element.44.normed_ref, bf16[512,512]{1,0:T(8,128)(2,1)S(1)} %bitcast.15, f32[256,768]{1,0:T(8,128)S(1)} %get-tuple-element.50.rep_ref, bf16[256,512]{1,0:T(8,128)(2,1)S(1)} %get-tuple-element.51.state_ref, f32[1,512]{1,0:T(1,128)} %bitcast.29, ...), custom_call_target="tpu_custom_call" | custom-call | flops 5000000000 | bytes 6000000 | tf_op jit(solution)/shard_map/pallas_call | solution.py:57
  52.8 3.6 %collective-permute-start.15 = (bf16[256,512]{1,0:T(8,128)(2,1)S(1)}, bf16[256,512]{1,0:T(8,128)(2,1)S(1)}, u32[]{:S(2)}, u32[]{:S(2)}) collective-permute-start(bf16[256,512]{1,0:T(8,128)(2,1)S(1)} %shard_map.275.back_ref), channel_id=1, source_target_pairs={{1,2},{2,1},{3,4},{4,3},{5,6},{6,5},{7,8},{8,7},{9,10},{10,9},{11,... | collective-permute-start | bytes 786440 | tf_op jit(solution)/shard_map/ppermute | solution.py:361
  56.4 2.5 %shard_map.276 = (f32[1024,512]{1,0:T(8,128)S(1)}, bf16[2,1024,256]{2,1,0:T(8,128)(2,1)S(1)}, bf16[84,512]{1,0:T(8,128)(2,1)S(1)}) custom-call(bf16[256,512]{1,0:T(8,128)(2,1)S(1)} %shard_map.275.back_ref, bf16[3,1024,256]{2,1,0:T(8,128)(2,1)} %get-tuple-element.54.links_hbm, bf16[1024,512]{1,0:T(8,128)(2,1)} %get-tuple-element.55.latent_hbm, ...), custom_call_target="tpu_custom_call" | custom-call | flops 1000000000 | bytes 2000000 | tf_op jit(solution)/shard_map/pallas_call | solution.py:57
  58.9 3.6 %collective-permute-done.15.cross_ref = bf16[256,512]{1,0:T(8,128)(2,1)S(1)} collective-permute-done((bf16[256,512]{1,0:T(8,128)(2,1)S(1)}, bf16[256,512]{1,0:T(8,128)(2,1)S(1)}, u32[]{:S(2)}, u32[]{:S(2)}) %collective-permute-start.15) | collective-permute-done | bytes 262176 | tf_op jit(solution)/shard_map/ppermute | solution.py:361
  62.6 1.9 %shard_map.277 = bf16[84,1024]{1,0:T(8,128)(2,1)} custom-call(f32[1024,512]{1,0:T(8,128)S(1)} %get-tuple-element.56.part_ref, bf16[2,1024,256]{2,1,0:T(8,128)(2,1)S(1)} %get-tuple-element.57.links_ref, bf16[256,512]{1,0:T(8,128)(2,1)S(1)} %collective-permute-done.14.near_ref, bf16[256,512]{1,0:T(8,128)(2,1)S(1)} %collective-permute-done.15.cross_ref, ...), custom_call_target="tpu_custom_call" | custom-call | flops 2000000000 | bytes 8000000 | tf_op jit(solution)/shard_map/pallas_call | solution.py:57
  (31 shorter events, 0.4 us)
Async XLA Ops:
  0.0 18.6 %copy-start = (s32[32,1]{0,1:T(1,128)S(1)}, s32[32,1]{0,1:T(1,128)}, u32[]{:S(2)}) copy-start(s32[32,1]{0,1:T(1,128)} %param.35) | copy-start | bytes 388
  1.8 11.4 %collective-permute-start.5 = (bf16[6,64,512]{2,1,0:T(8,128)(2,1)S(1)}, bf16[6,64,512]{2,1,0:T(8,128)(2,1)S(1)}, u32[]{:S(2)}, u32[]{:S(2)}) collective-permute-start(bf16[6,64,512]{2,1,0:T(8,128)(2,1)S(1)} %get-tuple-element.53), channel_id=1, source_target_pairs={{0,96},{32,64},{64,32},{96,0},{1,97},{33,65},{65,33},{97,1},{2,98}... | collective-permute-start | bytes 1179656 | tf_op jit(solution)/shard_map/ppermute | solution.py:358
  4.6 11.2 %collective-permute-start.2 = (bf16[6,64,512]{2,1,0:T(8,128)(2,1)S(1)}, bf16[6,64,512]{2,1,0:T(8,128)(2,1)S(1)}, u32[]{:S(2)}, u32[]{:S(2)}) collective-permute-start(bf16[6,64,512]{2,1,0:T(8,128)(2,1)S(1)} %get-tuple-element.52), channel_id=1, source_target_pairs={{0,32},{32,0},{64,96},{96,64},{1,33},{33,1},{65,97},{97,65},{2,34}... | collective-permute-start | bytes 1179656 | tf_op jit(solution)/shard_map/ppermute | solution.py:358
  4.6 5.3 %collective-permute-start = (bf16[272,256]{1,0:T(8,128)(2,1)S(1)}, bf16[272,256]{1,0:T(8,128)(2,1)S(1)}, u32[]{:S(2)}, u32[]{:S(2)}) collective-permute-start(bf16[272,256]{1,0:T(8,128)(2,1)S(1)} %get-tuple-element.37), channel_id=1, source_target_pairs={{0,1},{1,0},{2,3},{3,2},{4,5},{5,4},{6,7},{7,6},{8,9},{9,8},{10,11... | collective-permute-start | bytes 417800 | tf_op jit(solution)/shard_map/ppermute | solution.py:361
  5.7 8.5 %collective-permute-start.1 = (bf16[272,256]{1,0:T(8,128)(2,1)S(1)}, bf16[272,256]{1,0:T(8,128)(2,1)S(1)}, u32[]{:S(2)}, u32[]{:S(2)}) collective-permute-start(bf16[272,256]{1,0:T(8,128)(2,1)S(1)} %get-tuple-element.38), channel_id=1, source_target_pairs={{1,2},{2,1},{3,4},{4,3},{5,6},{6,5},{7,8},{8,7},{9,10},{10,9},{11,... | collective-permute-start | bytes 417800 | tf_op jit(solution)/shard_map/ppermute | solution.py:361
  9.1 23.9 %collective-permute-start.4 = (bf16[6,64,512]{2,1,0:T(8,128)(2,1)S(1)}, bf16[6,64,512]{2,1,0:T(8,128)(2,1)S(1)}, u32[]{:S(2)}, u32[]{:S(2)}) collective-permute-start(bf16[6,64,512]{2,1,0:T(8,128)(2,1)S(1)} %get-tuple-element.52), channel_id=1, source_target_pairs={{0,96},{32,64},{64,32},{96,0},{1,97},{33,65},{65,33},{97,1},{2,98}... | collective-permute-start | bytes 1179656 | tf_op jit(solution)/shard_map/ppermute | solution.py:358
  9.9 23.5 %collective-permute-start.3 = (bf16[6,64,512]{2,1,0:T(8,128)(2,1)S(1)}, bf16[6,64,512]{2,1,0:T(8,128)(2,1)}, u32[]{:S(2)}, u32[]{:S(2)}) collective-permute-start(bf16[6,64,512]{2,1,0:T(8,128)(2,1)S(1)} %get-tuple-element.53), channel_id=1, source_target_pairs={{0,32},{32,0},{64,96},{96,64},{1,33},{33,1},{65,97},{97,65},{2,34}... | collective-permute-start | bytes 1179656 | tf_op jit(solution)/shard_map/ppermute | solution.py:358
  13.2 8.3 %copy-start.3 = (bf16[6,64,512]{2,1,0:T(8,128)(2,1)}, bf16[6,64,512]{2,1,0:T(8,128)(2,1)S(1)}, u32[]{:S(2)}) copy-start(bf16[6,64,512]{2,1,0:T(8,128)(2,1)S(1)} %collective-permute-done.5.refs_3_) | copy-start | bytes 1179652
  13.2 20.7 %collective-permute-start.7 = (bf16[6,64,512]{2,1,0:T(8,128)(2,1)S(1)}, bf16[6,64,512]{2,1,0:T(8,128)(2,1)}, u32[]{:S(2)}, u32[]{:S(2)}) collective-permute-start(bf16[6,64,512]{2,1,0:T(8,128)(2,1)S(1)} %collective-permute-done.5.refs_3_), channel_id=1, source_target_pairs={{0,32},{32,0},{64,96},{96,64},{1,33},{33,1},{65,97},{97,65},{2,34}... | collective-permute-start | bytes 1179656 | tf_op jit(solution)/shard_map/ppermute | solution.py:358
  14.2 19.9 %collective-permute-start.11 = (bf16[6,64,512]{2,1,0:T(8,128)(2,1)S(1)}, bf16[6,64,512]{2,1,0:T(8,128)(2,1)}, u32[]{:S(2)}, u32[]{:S(2)}) collective-permute-start(bf16[6,64,512]{2,1,0:T(8,128)(2,1)S(1)} %collective-permute-done.5.refs_3_), channel_id=1, source_target_pairs={{0,1},{1,0},{2,3},{3,2},{4,5},{5,4},{6,7},{7,6},{8,9},{9,8},{10,11... | collective-permute-start | bytes 1179656 | tf_op jit(solution)/shard_map/ppermute | solution.py:361
  15.9 17.1 %copy-start.4 = (bf16[6,64,512]{2,1,0:T(8,128)(2,1)}, bf16[6,64,512]{2,1,0:T(8,128)(2,1)S(1)}, u32[]{:S(2)}) copy-start(bf16[6,64,512]{2,1,0:T(8,128)(2,1)S(1)} %collective-permute-done.2.refs_0_) | copy-start | bytes 1179652
  15.9 17.7 %collective-permute-start.6 = (bf16[6,64,512]{2,1,0:T(8,128)(2,1)S(1)}, bf16[6,64,512]{2,1,0:T(8,128)(2,1)}, u32[]{:S(2)}, u32[]{:S(2)}) collective-permute-start(bf16[6,64,512]{2,1,0:T(8,128)(2,1)S(1)} %collective-permute-done.2.refs_0_), channel_id=1, source_target_pairs={{0,96},{32,64},{64,32},{96,0},{1,97},{33,65},{65,33},{97,1},{2,98}... | collective-permute-start | bytes 1179656 | tf_op jit(solution)/shard_map/ppermute | solution.py:358
  18.6 2.9 %copy-start.1 = (s32[1,16]{1,0:T(1,128)S(1)}, s32[1,16]{1,0:T(1,128)}, u32[]{:S(2)}) copy-start(s32[1,16]{1,0:T(1,128)} %rows_ref.1) | copy-start | bytes 196
  21.5 13.0 %copy-start.2 = (s32[32,1]{0,1:T(1,128)S(1)}, s32[32,1]{0,1:T(1,128)}, u32[]{:S(2)}) copy-start(s32[32,1]{0,1:T(1,128)} %param.42) | copy-start | bytes 388
  24.5 18.7 %all-to-all-start = ((bf16[32,16,512]{2,1,0:T(8,128)(2,1)}), bf16[32,16,512]{2,1,0:T(8,128)(2,1)S(1)}, u32[]{:S(2)}, u32[]{:S(2)}) async-start(bf16[32,16,512]{2,1,0:T(8,128)(2,1)} %bitcast.9), calls=%async_computation | async-start | bytes 1048576 | tf_op jit(solution)/shard_map/all_to_all | solution.py:432
  33.0 7.9 %copy-start.5 = (bf16[6,64,512]{2,1,0:T(8,128)(2,1)}, bf16[6,64,512]{2,1,0:T(8,128)(2,1)S(1)}, u32[]{:S(2)}) copy-start(bf16[6,64,512]{2,1,0:T(8,128)(2,1)S(1)} %collective-permute-done.4.refs_2_) | copy-start | bytes 1179652
  33.0 10.2 %collective-permute-start.8 = (bf16[6,64,512]{2,1,0:T(8,128)(2,1)S(1)}, bf16[6,64,512]{2,1,0:T(8,128)(2,1)}, u32[]{:S(2)}, u32[]{:S(2)}) collective-permute-start(bf16[6,64,512]{2,1,0:T(8,128)(2,1)S(1)} %collective-permute-done.2.refs_0_), channel_id=1, source_target_pairs={{0,1},{1,0},{2,3},{3,2},{4,5},{5,4},{6,7},{7,6},{8,9},{9,8},{10,11... | collective-permute-start | bytes 1179656 | tf_op jit(solution)/shard_map/ppermute | solution.py:361
  33.4 9.8 %collective-permute-start.10 = (bf16[6,64,512]{2,1,0:T(8,128)(2,1)S(1)}, bf16[6,64,512]{2,1,0:T(8,128)(2,1)}, u32[]{:S(2)}, u32[]{:S(2)}) collective-permute-start(bf16[6,64,512]{2,1,0:T(8,128)(2,1)S(1)} %collective-permute-done.4.refs_2_), channel_id=1, source_target_pairs={{0,1},{1,0},{2,3},{3,2},{4,5},{5,4},{6,7},{7,6},{8,9},{9,8},{10,11... | collective-permute-start | bytes 1179656 | tf_op jit(solution)/shard_map/ppermute | solution.py:361
  33.6 9.6 %collective-permute-start.9 = (bf16[6,64,512]{2,1,0:T(8,128)(2,1)}, bf16[6,64,512]{2,1,0:T(8,128)(2,1)}, u32[]{:S(2)}, u32[]{:S(2)}) collective-permute-start(bf16[6,64,512]{2,1,0:T(8,128)(2,1)} %collective-permute-done.3.refs_1_), channel_id=1, source_target_pairs={{0,1},{1,0},{2,3},{3,2},{4,5},{5,4},{6,7},{7,6},{8,9},{9,8},{10,11... | collective-permute-start | bytes 1179656 | tf_op jit(solution)/shard_map/ppermute | solution.py:361
  34.0 9.2 %collective-permute-start.12 = (bf16[6,64,512]{2,1,0:T(8,128)(2,1)}, bf16[6,64,512]{2,1,0:T(8,128)(2,1)}, u32[]{:S(2)}, u32[]{:S(2)}) collective-permute-start(bf16[6,64,512]{2,1,0:T(8,128)(2,1)} %collective-permute-done.6.refs_4_), channel_id=1, source_target_pairs={{0,1},{1,0},{2,3},{3,2},{4,5},{5,4},{6,7},{7,6},{8,9},{9,8},{10,11... | collective-permute-start | bytes 1179656 | tf_op jit(solution)/shard_map/ppermute | solution.py:361
  34.1 9.1 %collective-permute-start.13 = (bf16[6,64,512]{2,1,0:T(8,128)(2,1)}, bf16[6,64,512]{2,1,0:T(8,128)(2,1)S(1)}, u32[]{:S(2)}, u32[]{:S(2)}) collective-permute-start(bf16[6,64,512]{2,1,0:T(8,128)(2,1)} %collective-permute-done.7.refs_5_), channel_id=1, source_target_pairs={{0,1},{1,0},{2,3},{3,2},{4,5},{5,4},{6,7},{7,6},{8,9},{9,8},{10,11... | collective-permute-start | bytes 1179656 | tf_op jit(solution)/shard_map/ppermute | solution.py:361
  43.2 0.8 %copy-start.6 = (bf16[6,64,512]{2,1,0:T(8,128)(2,1)}, bf16[6,64,512]{2,1,0:T(8,128)(2,1)S(1)}, u32[]{:S(2)}) copy-start(bf16[6,64,512]{2,1,0:T(8,128)(2,1)S(1)} %collective-permute-done.13.refs_11_) | copy-start | bytes 1179652
  52.7 6.3 %collective-permute-start.14 = (bf16[256,512]{1,0:T(8,128)(2,1)S(1)}, bf16[256,512]{1,0:T(8,128)(2,1)S(1)}, u32[]{:S(2)}, u32[]{:S(2)}) collective-permute-start(bf16[256,512]{1,0:T(8,128)(2,1)S(1)} %shard_map.275.back_ref), channel_id=1, source_target_pairs={{0,1},{1,0},{2,3},{3,2},{4,5},{5,4},{6,7},{7,6},{8,9},{9,8},{10,11... | collective-permute-start | bytes 786440 | tf_op jit(solution)/shard_map/ppermute | solution.py:361
  52.8 9.8 %collective-permute-start.15 = (bf16[256,512]{1,0:T(8,128)(2,1)S(1)}, bf16[256,512]{1,0:T(8,128)(2,1)S(1)}, u32[]{:S(2)}, u32[]{:S(2)}) collective-permute-start(bf16[256,512]{1,0:T(8,128)(2,1)S(1)} %shard_map.275.back_ref), channel_id=1, source_target_pairs={{1,2},{2,1},{3,4},{4,3},{5,6},{6,5},{7,8},{8,7},{9,10},{10,9},{11,... | collective-permute-start | bytes 786440 | tf_op jit(solution)/shard_map/ppermute | solution.py:361

commit v4 on v3

--- a/solution.py
+++ b/solution.py
@@ -10,9 +10,11 @@
 
 DH = 128
 EPS = 1e-05
+LOG2E = math.log2(math.e)
 BF = jnp.bfloat16
 F32 = jnp.float32
 
+ANY = pl.BlockSpec(memory_space=pl.ANY)
 HBM = pl.BlockSpec(memory_space=pltpu.HBM)
 VMEM = pl.BlockSpec(memory_space=pltpu.VMEM)
 SMEM = pl.BlockSpec(memory_space=pltpu.SMEM)
@@ -27,7 +29,8 @@
 
 
 def silu(v):
-    return v / (1.0 + jnp.exp(-v))
+    half = 0.5 * v
+    return half + half * jnp.tanh(half)
 
 
 def hot_rows(row, count):
@@ -47,7 +50,7 @@
 
 
 def call(body, outs, operands, scratch=(), flops=0, nbytes=0, mib=24):
-    specs = {"h": HBM, "v": VMEM, "d": VMEM, "s": SMEM}
+    specs = {"h": HBM, "v": VMEM, "d": VMEM, "s": SMEM, "a": ANY}
     spaces = {"h": pltpu.HBM, "v": pltpu.VMEM}
     arrays = [
         pltpu.with_memory_space_constraint(a, spaces[w]) if w in spaces else a for w, a in operands
@@ -212,7 +215,7 @@
     repeats = jnp.where(ids == own, 1.0, 0.0)
     for k in range(labels.shape[1]):
         repeats = repeats + jnp.where(ids == labels[:, k : k + 1], 1.0, 0.0)
-    rep_ref[...] = repeats
+    rep_ref[...] = repeats.astype(BF)
     for copy in copies:
         copy.wait()
 
@@ -221,7 +224,7 @@
     normed_ref, far_ref, rep_ref, state_ref, gain_hbm, wr_hbm, wg_hbm, wq, wk, wv, wp, wu, wd, *refs
 ):
     pieces, refs = refs[:12], refs[12:]
-    out_ref, m_ref, u_ref, d_ref, att_ref, gain_ref, wr_ref, wg_ref, sem = refs
+    out_ref, m_ref, u_ref, d_ref, att_ref, bias_ref, gain_ref, wr_ref, wg_ref, sem = refs
     me = lax.axis_index("member")
     half = lax.axis_index("space") % 2
     square = (wq, wk, wv, wp)
@@ -251,6 +254,7 @@
     downs += [(wr_hbm, wr_ref), (wg_hbm, wg_ref)]
     heads_gain = start_all([(gain_hbm, gain_ref)], sem, len(heads) + len(ups) + len(downs))
     downs = start_all(downs, sem, len(heads) + len(ups))
+    bias_ref[...] = jnp.log(rep_ref[...].astype(F32)) * LOG2E
     for copy in heads + heads_gain:
         copy.wait()
     normed = normed_ref[...]
@@ -260,13 +264,10 @@
     values = jnp.concatenate([dot(normed, m_ref[2]).astype(BF), dot(far, m_ref[2]).astype(BF)], 0)
     for h in range(width // DH):
         at = slice(h * DH, (h + 1) * DH)
-        repeats = rep_ref[...]
-        scores = dot_nt(queries[:, at], keys[:, at]) / math.sqrt(DH)
-        scores = jnp.where(repeats > 0.0, scores, -jnp.inf)
-        top = jnp.max(scores, axis=-1, keepdims=True)
-        weights = repeats * jnp.exp(scores - top)
-        probs = (weights / jnp.sum(weights, axis=-1, keepdims=True)).astype(BF)
-        att_ref[:, at] = dot(probs, values[:, at]).astype(BF)
+        scores = dot_nt(queries[:, at], keys[:, at]) * (LOG2E / math.sqrt(DH)) + bias_ref[...]
+        weights = jnp.exp2(scores - jnp.max(scores, axis=-1, keepdims=True))
+        total = jnp.sum(weights, axis=-1, keepdims=True)
+        att_ref[:, at] = (dot(weights.astype(BF), values[:, at]) / total).astype(BF)
     after = state_ref[...].astype(F32) + dot(att_ref[...], m_ref[3])
     normed = layer_norm(after, gain_ref[...]).astype(BF)
     for copy in ups + downs:
@@ -352,13 +353,18 @@
     square = (w_query, w_key, w_value, w_project)
     bind = functools.partial
     swap = [(i, i ^ 1) for i in range(bands)]
-    chain = [(i, j) for i in range(bands) for j in (i - 1 + i % 2 * 2,) if 0 <= j < bands]
+    chain = []
+    for m in range(4):
+        for i in range(bands):
+            j = i - 1 + i % 2 * 2
+            chain.append((m * bands + i, m * bands + j if 0 <= j < bands else (m ^ 1) * bands + i))
 
     def turn(block, d):
         return lax.ppermute(block, "member", [(i, i ^ d) for i in range(4)])
 
     def pass_on(block, route):
-        return lax.ppermute(block, "space", route)
+        axes = "space" if len(route) == bands else ("member", "space")
+        return lax.ppermute(block, axes, route)
 
     def like(a):
         return "v", a.shape, a.dtype
@@ -417,7 +423,7 @@
         [
             ("v", (mesh_rows, width), BF),
             ("v", (mesh_rows, width), BF),
-            ("d", (bands * published, width), BF),
+            ("v", (bands * published, width), BF),
         ],
         tag("v", agg)
         + tag("d", near, cross)
@@ -432,7 +438,7 @@
     far = lax.all_to_all(halo, "space", 0, 0, tiled=True)
     links, repeats = call(
         bind(fill_body, bands),
-        [("h", (3, rows, mesh_rows), BF), ("v", (mesh_rows, table), F32)],
+        [("h", (3, rows, mesh_rows), BF), ("v", (mesh_rows, table), BF)],
         tag("v", *ahead[5:8])
         + tag("s", m2g_count)
         + tag("d", near, cross)
@@ -450,12 +456,15 @@
         + tag("d", far)
         + tag("v", repeats, state)
         + tag("h", mlp_gain.reshape(1, width), w_return, w_grid)
-        + tag("h", *square, w_up, w_deep, *fetched, *shared),
+        + tag("h", *square, w_up, w_deep)
+        + tag("h", *fetched)
+        + [("v" if i in (0, 2, 3) else "h", w) for i, w in enumerate(shared)],
         [
             pltpu.VMEM((4, 4 * part, width), BF),
             pltpu.VMEM((blocks, 4 * part, width), BF),
             pltpu.VMEM((16 * deep, piece, width), BF),
             pltpu.VMEM((mesh_rows, width), BF),
+            pltpu.VMEM((mesh_rows, table), F32),
             pltpu.VMEM((1, width), F32),
             pltpu.VMEM((width, width), BF),
             pltpu.VMEM((width, width), BF),

time: 64.9 us -> 62.3 us (0.960)
  starting transfers between devices: 27 us -> 24 us
  waiting for transfers between devices: 9.33 us -> 10.6 us
  Pallas kernels: 27.2 us -> 26.2 us
    ppermute x10, starting transfers between devices: 11.3 us -> 8.66 us  [pass_on(): return lax.ppermute(block, axes, route)]
    ppermute x6, waiting for transfers between devices: 2.38 us -> 4.46 us  [turn(): return lax.ppermute(block, 'member', [(i, i ^ d) for i in range(4)])]
    pallas_call x7, Pallas kernels: 27.2 us -> 26.2 us  [call(): pl.pallas_call(body, out_shape=shapes, in_specs=[specs[w] for w, _ in ope...]
    ppermute x10, waiting for transfers between devices: 4.61 us -> 3.75 us  [pass_on(): return lax.ppermute(block, axes, route)]
  transfers between devices with their start and end apart: 17 -> 17, of which waited for: 4 -> 3; matrix products, arithmetic and copies ran while one was open for 0% -> 0% of each run, Pallas kernels for 23% -> 24%
where the time goes in v4:
time: 62.3 us; the launch traced here: 61.6 us
  Pallas kernels  26.2 us (42%)
  starting transfers between devices  24 us (39%)
  waiting for transfers between devices  10.6 us (17%)
  local copies, waits for them, and re-layouts  0.77 us (1%)
    pallas_call x7, Pallas kernels, call(): pl.pallas_call(body, out_shape=shapes, in_specs=[specs[w] for w, _ in ope...  26.2 us
    ppermute x10, starting transfers between devices, pass_on(): return lax.ppermute(block, axes, route)  8.66 us
    all_to_all x1, starting transfers between devices, shards(): far = lax.all_to_all(halo, 'space', 0, 0, tiled=True)  8.38 us
    ppermute x6, starting transfers between devices, turn(): return lax.ppermute(block, 'member', [(i, i ^ d) for i in range(4)])  6.95 us
    ppermute x6, waiting for transfers between devices, turn(): return lax.ppermute(block, 'member', [(i, i ^ d) for i in range(4)])  4.46 us
    ppermute x10, waiting for transfers between devices, pass_on(): return lax.ppermute(block, axes, route)  3.75 us
    all_to_all x1, waiting for transfers between devices, shards(): far = lax.all_to_all(halo, 'space', 0, 0, tiled=True)  2.37 us
  transfers between devices with their start and end apart: 17, of which 3 were waited for; matrix products, arithmetic and copies ran while one was open for 0% of the time, Pallas kernels for 24%

profile of v4, /device:TPU:7, one launch (start us, length us, event | category | flops | bytes accessed | tf_op | source)
XLA Modules:
  0.0 61.6 jit_solution(14772226546892823323)
XLA Ops:
  0.0 1.8 %shard_map.271 = (bf16[272,256]{1,0:T(8,128)(2,1)S(1)}, bf16[272,256]{1,0:T(8,128)(2,1)S(1)}, bf16[6,64,512]{2,1,0:T(8,128)(2,1)S(1)}, bf16[6,64,512]{2,1,0:T(8,...) custom-call(bf16[1024,256]{1,0:T(8,128)(2,1)} %bitcast.19, ...), custom_call_target="tpu_custom_call" | custom-call | flops 300000000 | bytes 3000000 | tf_op jit(solution)/shard_map/pallas_call | solution.py:60
  1.8 2.8 %collective-permute-start.5 = (bf16[6,64,512]{2,1,0:T(8,128)(2,1)S(1)}, bf16[6,64,512]{2,1,0:T(8,128)(2,1)S(1)}, u32[]{:S(2)}, u32[]{:S(2)}) collective-permute-start(bf16[6,64,512]{2,1,0:T(8,128)(2,1)S(1)} %get-tuple-element.53), channel_id=1, source_target_pairs={{0,96},{32,64},{64,32},{96,0},{1,97},{33,65},{65,33},{97,1},{2,98}... | collective-permute-start | bytes 1179656 | tf_op jit(solution)/shard_map/ppermute | solution.py:363
  4.6 1.1 %collective-permute-start = (bf16[272,256]{1,0:T(8,128)(2,1)S(1)}, bf16[272,256]{1,0:T(8,128)(2,1)S(1)}, u32[]{:S(2)}, u32[]{:S(2)}) collective-permute-start(bf16[272,256]{1,0:T(8,128)(2,1)S(1)} %get-tuple-element.37), channel_id=1, source_target_pairs={{0,1},{1,0},{2,3},{3,2},{4,5},{5,4},{6,7},{7,6},{8,9},{9,8},{10,11... | collective-permute-start | bytes 417800 | tf_op jit(solution)/shard_map/ppermute | solution.py:367
  5.7 1.4 %collective-permute-start.1 = (bf16[272,256]{1,0:T(8,128)(2,1)S(1)}, bf16[272,256]{1,0:T(8,128)(2,1)S(1)}, u32[]{:S(2)}, u32[]{:S(2)}) collective-permute-start(bf16[272,256]{1,0:T(8,128)(2,1)S(1)} %get-tuple-element.38), channel_id=1, source_target_pairs={{0,32},{1,2},{2,1},{3,4},{4,3},{5,6},{6,5},{7,8},{8,7},{9,10},{10,... | collective-permute-start | bytes 417800 | tf_op jit(solution)/shard_map/ppermute | solution.py:367
  7.2 0.8 %collective-permute-start.4 = (bf16[6,64,512]{2,1,0:T(8,128)(2,1)S(1)}, bf16[6,64,512]{2,1,0:T(8,128)(2,1)}, u32[]{:S(2)}, u32[]{:S(2)}) collective-permute-start(bf16[6,64,512]{2,1,0:T(8,128)(2,1)S(1)} %get-tuple-element.52), channel_id=1, source_target_pairs={{0,96},{32,64},{64,32},{96,0},{1,97},{33,65},{65,33},{97,1},{2,98}... | collective-permute-start | bytes 1179656 | tf_op jit(solution)/shard_map/ppermute | solution.py:363
  7.9 0.8 %collective-permute-start.3 = (bf16[6,64,512]{2,1,0:T(8,128)(2,1)S(1)}, bf16[6,64,512]{2,1,0:T(8,128)(2,1)}, u32[]{:S(2)}, u32[]{:S(2)}) collective-permute-start(bf16[6,64,512]{2,1,0:T(8,128)(2,1)S(1)} %get-tuple-element.53), channel_id=1, source_target_pairs={{0,32},{32,0},{64,96},{96,64},{1,33},{33,1},{65,97},{97,65},{2,34}... | collective-permute-start | bytes 1179656 | tf_op jit(solution)/shard_map/ppermute | solution.py:363
  8.8 4.4 %collective-permute-done.5.refs_3_ = bf16[6,64,512]{2,1,0:T(8,128)(2,1)S(1)} collective-permute-done((bf16[6,64,512]{2,1,0:T(8,128)(2,1)S(1)}, bf16[6,64,512]{2,1,0:T(8,128)(2,1)S(1)}, u32[]{:S(2)}, u32[]{:S(2)}) %collective-permute-start.5) | collective-permute-done | bytes 393248 | tf_op jit(solution)/shard_map/ppermute | solution.py:363
  13.3 2.8 %collective-permute-start.11 = (bf16[6,64,512]{2,1,0:T(8,128)(2,1)S(1)}, bf16[6,64,512]{2,1,0:T(8,128)(2,1)S(1)}, u32[]{:S(2)}, u32[]{:S(2)}) collective-permute-start(bf16[6,64,512]{2,1,0:T(8,128)(2,1)S(1)} %collective-permute-done.5.refs_3_), channel_id=1, source_target_pairs={{0,1},{1,0},{2,3},{3,2},{4,5},{5,4},{6,7},{7,6},{8,9},{9,8},{10,11... | collective-permute-start | bytes 1179656 | tf_op jit(solution)/shard_map/ppermute | solution.py:367
  16.1 2.5 %collective-permute-start.6 = (bf16[6,64,512]{2,1,0:T(8,128)(2,1)}, bf16[6,64,512]{2,1,0:T(8,128)(2,1)}, u32[]{:S(2)}, u32[]{:S(2)}) collective-permute-start(bf16[6,64,512]{2,1,0:T(8,128)(2,1)} %collective-permute-done.2.refs_0_), channel_id=1, source_target_pairs={{0,96},{32,64},{64,32},{96,0},{1,97},{33,65},{65,33},{97,1},{2,98}... | collective-permute-start | bytes 1179656 | tf_op jit(solution)/shard_map/ppermute | solution.py:363
  18.6 3.0 %shard_map.272 = (bf16[1024,512]{1,0:T(8,128)(2,1)}, f32[256,512]{1,0:T(8,128)S(1)}, s32[32,256]{1,0:T(8,128)S(1)}, bf16[512,512]{1,0:T(8,128)(2,1)S(1)}, bf16[5...) custom-call(bf16[1024,256]{1,0:T(8,128)(2,1)S(1)} %get-tuple-element, ...), custom_call_target="tpu_custom_call" | custom-call | flops 3000000000 | bytes 3000000 | tf_op jit(solution)/shard_map/pallas_call | solution.py:60
  21.7 2.9 %shard_map.273 = (bf16[256,512]{1,0:T(8,128)(2,1)S(1)}, bf16[256,512]{1,0:T(8,128)(2,1)S(1)}, bf16[512,512]{1,0:T(8,128)(2,1)}) custom-call(f32[256,512]{1,0:T(8,128)S(1)} %get-tuple-element.36.agg_ref, bf16[272,256]{1,0:T(8,128)(2,1)S(1)} %collective-permute-done.near_ref, bf16[272,256]{1,0:T(8,128)(2,1)S(1)} %collective-permute-done.1.cross_ref, ...), custom_call_target="tpu_custom_call" | custom-call | flops 1000000000 | bytes 3000000 | tf_op jit(solution)/shard_map/pallas_call | solution.py:60
  24.6 8.4 %all-to-all-start = ((bf16[32,16,512]{2,1,0:T(8,128)(2,1)}), bf16[32,16,512]{2,1,0:T(8,128)(2,1)S(1)}, u32[]{:S(2)}, u32[]{:S(2)}) async-start(bf16[32,16,512]{2,1,0:T(8,128)(2,1)} %bitcast.9), calls=%async_computation | async-start | bytes 1048576 | tf_op jit(solution)/shard_map/all_to_all | solution.py:438
  33.0 0.5 collective-permute-start.8
  33.4 0.1 collective-permute-start.10
  33.6 0.4 collective-permute-start.9
  34.1 0.4 collective-permute-start.13
  34.5 6.4 %shard_map.274 = (bf16[3,1024,256]{2,1,0:T(8,128)(2,1)}, bf16[256,768]{1,0:T(8,128)(2,1)S(1)}) custom-call(s32[1,2560]{1,0:T(1,128)S(1)} %get-tuple-element.46.src_ref, s32[1,2560]{1,0:T(1,128)S(1)} %get-tuple-element.47.dst_ref, s32[32,256]{1,0:T(8,128)S(1)} %get-tuple-element.48.far_dst_ref, s32[32]{0:T(128)S(1)} %bitcast.18, ...), custom_call_target="tpu_custom_call" | custom-call | flops 4000000000 | bytes 8000000 | tf_op jit(solution)/shard_map/pallas_call | solution.py:60
  40.8 2.4 %all-to-all-done = bf16[32,16,512]{2,1,0:T(8,128)(2,1)S(1)} async-done(((bf16[32,16,512]{2,1,0:T(8,128)(2,1)}), bf16[32,16,512]{2,1,0:T(8,128)(2,1)S(1)}, u32[]{:S(2)}, u32[]{:S(2)}) %all-to-all-start) | async-done | bytes 524320 | tf_op jit(solution)/shard_map/all_to_all | solution.py:438
  43.3 0.7 %copy-done.4 = bf16[6,64,512]{2,1,0:T(8,128)(2,1)} copy-done((bf16[6,64,512]{2,1,0:T(8,128)(2,1)}, bf16[6,64,512]{2,1,0:T(8,128)(2,1)S(1)}, u32[]{:S(2)}) %copy-start.4) | copy-done | bytes 393240
  44.0 7.7 %shard_map.275.back_ref = bf16[256,512]{1,0:T(8,128)(2,1)S(1)} custom-call(bf16[256,512]{1,0:T(8,128)(2,1)S(1)} %get-tuple-element.44.normed_ref, bf16[512,512]{1,0:T(8,128)(2,1)S(1)} %bitcast.15, bf16[256,768]{1,0:T(8,128)(2,1)S(1)} %get-tuple-element.50.rep_ref, bf16[256,512]{1,0:T(8,128)(2,1)S(1)} %get-tuple-element.51.state_ref, f32[1,512]{1,0:T(1,128)} %bitcast.29, ...), custom_call_target="tpu_custom_call" | custom-call | flops 5000000000 | bytes 6000000 | tf_op jit(solution)/shard_map/pallas_call | solution.py:60
  51.8 1.7 %collective-permute-start.15 = (bf16[256,512]{1,0:T(8,128)(2,1)S(1)}, bf16[256,512]{1,0:T(8,128)(2,1)S(1)}, u32[]{:S(2)}, u32[]{:S(2)}) collective-permute-start(bf16[256,512]{1,0:T(8,128)(2,1)S(1)} %shard_map.275.back_ref), channel_id=1, source_target_pairs={{0,32},{1,2},{2,1},{3,4},{4,3},{5,6},{6,5},{7,8},{8,7},{9,10},{10,... | collective-permute-start | bytes 786440 | tf_op jit(solution)/shard_map/ppermute | solution.py:367
  53.5 2.5 %shard_map.276 = (f32[1024,512]{1,0:T(8,128)S(1)}, bf16[2,1024,256]{2,1,0:T(8,128)(2,1)S(1)}, bf16[84,512]{1,0:T(8,128)(2,1)S(1)}) custom-call(bf16[256,512]{1,0:T(8,128)(2,1)S(1)} %shard_map.275.back_ref, bf16[3,1024,256]{2,1,0:T(8,128)(2,1)} %get-tuple-element.54.links_hbm, bf16[1024,512]{1,0:T(8,128)(2,1)} %get-tuple-element.55.latent_hbm, ...), custom_call_target="tpu_custom_call" | custom-call | flops 1000000000 | bytes 2000000 | tf_op jit(solution)/shard_map/pallas_call | solution.py:60
  56.0 3.7 %collective-permute-done.15.cross_ref = bf16[256,512]{1,0:T(8,128)(2,1)S(1)} collective-permute-done((bf16[256,512]{1,0:T(8,128)(2,1)S(1)}, bf16[256,512]{1,0:T(8,128)(2,1)S(1)}, u32[]{:S(2)}, u32[]{:S(2)}) %collective-permute-start.15) | collective-permute-done | bytes 262176 | tf_op jit(solution)/shard_map/ppermute | solution.py:367
  59.8 1.9 %shard_map.277 = bf16[84,1024]{1,0:T(8,128)(2,1)} custom-call(f32[1024,512]{1,0:T(8,128)S(1)} %get-tuple-element.56.part_ref, bf16[2,1024,256]{2,1,0:T(8,128)(2,1)S(1)} %get-tuple-element.57.links_ref, bf16[256,512]{1,0:T(8,128)(2,1)S(1)} %collective-permute-done.14.near_ref, bf16[256,512]{1,0:T(8,128)(2,1)S(1)} %collective-permute-done.15.cross_ref, ...), custom_call_target="tpu_custom_call" | custom-call | flops 2000000000 | bytes 8000000 | tf_op jit(solution)/shard_map/pallas_call | solution.py:60
  (27 shorter events, 0.3 us)
Async XLA Ops:
  0.0 18.6 %copy-start = (s32[32,1]{0,1:T(1,128)S(1)}, s32[32,1]{0,1:T(1,128)}, u32[]{:S(2)}) copy-start(s32[32,1]{0,1:T(1,128)} %param.35) | copy-start | bytes 388
  1.8 11.4 %collective-permute-start.5 = (bf16[6,64,512]{2,1,0:T(8,128)(2,1)S(1)}, bf16[6,64,512]{2,1,0:T(8,128)(2,1)S(1)}, u32[]{:S(2)}, u32[]{:S(2)}) collective-permute-start(bf16[6,64,512]{2,1,0:T(8,128)(2,1)S(1)} %get-tuple-element.53), channel_id=1, source_target_pairs={{0,96},{32,64},{64,32},{96,0},{1,97},{33,65},{65,33},{97,1},{2,98}... | collective-permute-start | bytes 1179656 | tf_op jit(solution)/shard_map/ppermute | solution.py:363
  4.6 11.5 %collective-permute-start.2 = (bf16[6,64,512]{2,1,0:T(8,128)(2,1)S(1)}, bf16[6,64,512]{2,1,0:T(8,128)(2,1)}, u32[]{:S(2)}, u32[]{:S(2)}) collective-permute-start(bf16[6,64,512]{2,1,0:T(8,128)(2,1)S(1)} %get-tuple-element.52), channel_id=1, source_target_pairs={{0,32},{32,0},{64,96},{96,64},{1,33},{33,1},{65,97},{97,65},{2,34}... | collective-permute-start | bytes 1179656 | tf_op jit(solution)/shard_map/ppermute | solution.py:363
  4.6 3.3 %collective-permute-start = (bf16[272,256]{1,0:T(8,128)(2,1)S(1)}, bf16[272,256]{1,0:T(8,128)(2,1)S(1)}, u32[]{:S(2)}, u32[]{:S(2)}) collective-permute-start(bf16[272,256]{1,0:T(8,128)(2,1)S(1)} %get-tuple-element.37), channel_id=1, source_target_pairs={{0,1},{1,0},{2,3},{3,2},{4,5},{5,4},{6,7},{7,6},{8,9},{9,8},{10,11... | collective-permute-start | bytes 417800 | tf_op jit(solution)/shard_map/ppermute | solution.py:367
  5.7 7.6 %collective-permute-start.1 = (bf16[272,256]{1,0:T(8,128)(2,1)S(1)}, bf16[272,256]{1,0:T(8,128)(2,1)S(1)}, u32[]{:S(2)}, u32[]{:S(2)}) collective-permute-start(bf16[272,256]{1,0:T(8,128)(2,1)S(1)} %get-tuple-element.38), channel_id=1, source_target_pairs={{0,32},{1,2},{2,1},{3,4},{4,3},{5,6},{6,5},{7,8},{8,7},{9,10},{10,... | collective-permute-start | bytes 417800 | tf_op jit(solution)/shard_map/ppermute | solution.py:367
  7.2 25.8 %collective-permute-start.4 = (bf16[6,64,512]{2,1,0:T(8,128)(2,1)S(1)}, bf16[6,64,512]{2,1,0:T(8,128)(2,1)}, u32[]{:S(2)}, u32[]{:S(2)}) collective-permute-start(bf16[6,64,512]{2,1,0:T(8,128)(2,1)S(1)} %get-tuple-element.52), channel_id=1, source_target_pairs={{0,96},{32,64},{64,32},{96,0},{1,97},{33,65},{65,33},{97,1},{2,98}... | collective-permute-start | bytes 1179656 | tf_op jit(solution)/shard_map/ppermute | solution.py:363
  7.9 25.5 %collective-permute-start.3 = (bf16[6,64,512]{2,1,0:T(8,128)(2,1)S(1)}, bf16[6,64,512]{2,1,0:T(8,128)(2,1)}, u32[]{:S(2)}, u32[]{:S(2)}) collective-permute-start(bf16[6,64,512]{2,1,0:T(8,128)(2,1)S(1)} %get-tuple-element.53), channel_id=1, source_target_pairs={{0,32},{32,0},{64,96},{96,64},{1,33},{33,1},{65,97},{97,65},{2,34}... | collective-permute-start | bytes 1179656 | tf_op jit(solution)/shard_map/ppermute | solution.py:363
  13.2 8.4 %copy-start.3 = (bf16[6,64,512]{2,1,0:T(8,128)(2,1)}, bf16[6,64,512]{2,1,0:T(8,128)(2,1)S(1)}, u32[]{:S(2)}) copy-start(bf16[6,64,512]{2,1,0:T(8,128)(2,1)S(1)} %collective-permute-done.5.refs_3_) | copy-start | bytes 1179652
  13.2 20.7 %collective-permute-start.7 = (bf16[6,64,512]{2,1,0:T(8,128)(2,1)S(1)}, bf16[6,64,512]{2,1,0:T(8,128)(2,1)}, u32[]{:S(2)}, u32[]{:S(2)}) collective-permute-start(bf16[6,64,512]{2,1,0:T(8,128)(2,1)S(1)} %collective-permute-done.5.refs_3_), channel_id=1, source_target_pairs={{0,32},{32,0},{64,96},{96,64},{1,33},{33,1},{65,97},{97,65},{2,34}... | collective-permute-start | bytes 1179656 | tf_op jit(solution)/shard_map/ppermute | solution.py:363
  13.3 20.8 %collective-permute-start.11 = (bf16[6,64,512]{2,1,0:T(8,128)(2,1)S(1)}, bf16[6,64,512]{2,1,0:T(8,128)(2,1)S(1)}, u32[]{:S(2)}, u32[]{:S(2)}) collective-permute-start(bf16[6,64,512]{2,1,0:T(8,128)(2,1)S(1)} %collective-permute-done.5.refs_3_), channel_id=1, source_target_pairs={{0,1},{1,0},{2,3},{3,2},{4,5},{5,4},{6,7},{7,6},{8,9},{9,8},{10,11... | collective-permute-start | bytes 1179656 | tf_op jit(solution)/shard_map/ppermute | solution.py:367
  16.1 17.4 %collective-permute-start.6 = (bf16[6,64,512]{2,1,0:T(8,128)(2,1)}, bf16[6,64,512]{2,1,0:T(8,128)(2,1)}, u32[]{:S(2)}, u32[]{:S(2)}) collective-permute-start(bf16[6,64,512]{2,1,0:T(8,128)(2,1)} %collective-permute-done.2.refs_0_), channel_id=1, source_target_pairs={{0,96},{32,64},{64,32},{96,0},{1,97},{33,65},{65,33},{97,1},{2,98}... | collective-permute-start | bytes 1179656 | tf_op jit(solution)/shard_map/ppermute | solution.py:363
  18.6 3.1 %copy-start.1 = (s32[1,16]{1,0:T(1,128)S(1)}, s32[1,16]{1,0:T(1,128)}, u32[]{:S(2)}) copy-start(s32[1,16]{1,0:T(1,128)} %rows_ref.1) | copy-start | bytes 196
  21.7 12.8 %copy-start.2 = (s32[32,1]{0,1:T(1,128)S(1)}, s32[32,1]{0,1:T(1,128)}, u32[]{:S(2)}) copy-start(s32[32,1]{0,1:T(1,128)} %param.42) | copy-start | bytes 388
  24.6 18.6 %all-to-all-start = ((bf16[32,16,512]{2,1,0:T(8,128)(2,1)}), bf16[32,16,512]{2,1,0:T(8,128)(2,1)S(1)}, u32[]{:S(2)}, u32[]{:S(2)}) async-start(bf16[32,16,512]{2,1,0:T(8,128)(2,1)} %bitcast.9), calls=%async_computation | async-start | bytes 1048576 | tf_op jit(solution)/shard_map/all_to_all | solution.py:438
  33.0 10.2 %collective-permute-start.8 = (bf16[6,64,512]{2,1,0:T(8,128)(2,1)}, bf16[6,64,512]{2,1,0:T(8,128)(2,1)S(1)}, u32[]{:S(2)}, u32[]{:S(2)}) collective-permute-start(bf16[6,64,512]{2,1,0:T(8,128)(2,1)} %collective-permute-done.2.refs_0_), channel_id=1, source_target_pairs={{0,1},{1,0},{2,3},{3,2},{4,5},{5,4},{6,7},{7,6},{8,9},{9,8},{10,11... | collective-permute-start | bytes 1179656 | tf_op jit(solution)/shard_map/ppermute | solution.py:367
  33.4 9.8 %collective-permute-start.10 = (bf16[6,64,512]{2,1,0:T(8,128)(2,1)}, bf16[6,64,512]{2,1,0:T(8,128)(2,1)S(1)}, u32[]{:S(2)}, u32[]{:S(2)}) collective-permute-start(bf16[6,64,512]{2,1,0:T(8,128)(2,1)} %collective-permute-done.4.refs_2_), channel_id=1, source_target_pairs={{0,1},{1,0},{2,3},{3,2},{4,5},{5,4},{6,7},{7,6},{8,9},{9,8},{10,11... | collective-permute-start | bytes 1179656 | tf_op jit(solution)/shard_map/ppermute | solution.py:367
  33.6 9.7 %collective-permute-start.9 = (bf16[6,64,512]{2,1,0:T(8,128)(2,1)}, bf16[6,64,512]{2,1,0:T(8,128)(2,1)}, u32[]{:S(2)}, u32[]{:S(2)}) collective-permute-start(bf16[6,64,512]{2,1,0:T(8,128)(2,1)} %collective-permute-done.3.refs_1_), channel_id=1, source_target_pairs={{0,1},{1,0},{2,3},{3,2},{4,5},{5,4},{6,7},{7,6},{8,9},{9,8},{10,11... | collective-permute-start | bytes 1179656 | tf_op jit(solution)/shard_map/ppermute | solution.py:367
  34.0 9.3 %collective-permute-start.12 = (bf16[6,64,512]{2,1,0:T(8,128)(2,1)}, bf16[6,64,512]{2,1,0:T(8,128)(2,1)}, u32[]{:S(2)}, u32[]{:S(2)}) collective-permute-start(bf16[6,64,512]{2,1,0:T(8,128)(2,1)} %collective-permute-done.6.refs_4_), channel_id=1, source_target_pairs={{0,1},{1,0},{2,3},{3,2},{4,5},{5,4},{6,7},{7,6},{8,9},{9,8},{10,11... | collective-permute-start | bytes 1179656 | tf_op jit(solution)/shard_map/ppermute | solution.py:367
  34.1 9.2 %collective-permute-start.13 = (bf16[6,64,512]{2,1,0:T(8,128)(2,1)}, bf16[6,64,512]{2,1,0:T(8,128)(2,1)S(1)}, u32[]{:S(2)}, u32[]{:S(2)}) collective-permute-start(bf16[6,64,512]{2,1,0:T(8,128)(2,1)} %collective-permute-done.7.refs_5_), channel_id=1, source_target_pairs={{0,1},{1,0},{2,3},{3,2},{4,5},{5,4},{6,7},{7,6},{8,9},{9,8},{10,11... | collective-permute-start | bytes 1179656 | tf_op jit(solution)/shard_map/ppermute | solution.py:367
  43.2 0.8 %copy-start.4 = (bf16[6,64,512]{2,1,0:T(8,128)(2,1)}, bf16[6,64,512]{2,1,0:T(8,128)(2,1)S(1)}, u32[]{:S(2)}) copy-start(bf16[6,64,512]{2,1,0:T(8,128)(2,1)S(1)} %collective-permute-done.13.refs_11_) | copy-start | bytes 1179652
  51.7 4.3 %collective-permute-start.14 = (bf16[256,512]{1,0:T(8,128)(2,1)S(1)}, bf16[256,512]{1,0:T(8,128)(2,1)S(1)}, u32[]{:S(2)}, u32[]{:S(2)}) collective-permute-start(bf16[256,512]{1,0:T(8,128)(2,1)S(1)} %shard_map.275.back_ref), channel_id=1, source_target_pairs={{0,1},{1,0},{2,3},{3,2},{4,5},{5,4},{6,7},{7,6},{8,9},{9,8},{10,11... | collective-permute-start | bytes 786440 | tf_op jit(solution)/shard_map/ppermute | solution.py:367
  51.8 8.0 %collective-permute-start.15 = (bf16[256,512]{1,0:T(8,128)(2,1)S(1)}, bf16[256,512]{1,0:T(8,128)(2,1)S(1)}, u32[]{:S(2)}, u32[]{:S(2)}) collective-permute-start(bf16[256,512]{1,0:T(8,128)(2,1)S(1)} %shard_map.275.back_ref), channel_id=1, source_target_pairs={{0,32},{1,2},{2,1},{3,4},{4,3},{5,6},{6,5},{7,8},{8,7},{9,10},{10,... | collective-permute-start | bytes 786440 | tf_op jit(solution)/shard_map/ppermute | solution.py:367

commit v5 on v4

--- a/solution.py
+++ b/solution.py
@@ -41,6 +41,12 @@
 def live(row, length):
     slot = lax.broadcasted_iota(jnp.int32, row.shape, 1)
     return jnp.where(slot < length, row, -1)
+
+
+def length_at(len_ref, at, some=True):
+    lanes = lax.broadcasted_iota(jnp.int32, len_ref.shape, 1)
+    here = jnp.where((lanes == at) & some, len_ref[...].astype(F32), 0.0)
+    return jnp.sum(here, axis=1, keepdims=True).astype(jnp.int32)
 
 
 def layer_norm(values, gain):
@@ -78,12 +84,13 @@
 
 def pick_body(
     bands, x_hbm, src_hbm, back_hbm, wq, wk, wv, wp, wu, wd, we_hbm, own_hbm, land_hbm,
-    near_ref, cross_ref, a_ref, b_ref, x_ref, we_ref, own_ref, land_ref, src_ref, back_ref, sem,
+    len_hbm, near_ref, cross_ref, a_ref, b_ref, x_ref, we_ref, own_ref, land_ref, len_ref,
+    src_ref, back_ref, sem,
 ):
     band, near, cross, _ = around(bands)
     copies = [(src_hbm, src_ref), (back_hbm, back_ref), (x_hbm, x_ref)]
     copies += half_weights((wq, wk, wv, wp), wu, wd, band % 2, a_ref, b_ref)
-    copies += [(we_hbm, we_ref), (own_hbm, own_ref), (land_hbm, land_ref)]
+    copies += [(we_hbm, we_ref), (own_hbm, own_ref), (land_hbm, land_ref), (len_hbm, len_ref)]
     copies = start_all(copies, sem)
     for copy in copies[:3]:
         copy.wait()
@@ -142,7 +149,7 @@
     copies += start_all([(latent_ref, latent_hbm)], sem, count)
     mesh_rows = agg_ref.shape[0]
     src_hot = hot_rows(src_ref[...], x_ref.shape[0])
-    dst_hot = hot_rows(live(dst_ref[...], len_ref[band]), mesh_rows)
+    dst_hot = hot_rows(live(dst_ref[...], length_at(len_ref, band)), mesh_rows)
     links = dot_nt(dst_hot, src_hot).astype(BF)
     agg_ref[...] = dot(links, latent)
     for copy in copies:
@@ -165,15 +172,13 @@
     state_ref,
     normed_ref,
     halo_ref,
-    wide,
-    own,
 ):
     _, near, cross, there = around(bands)
     total = agg_ref[...]
     mesh_rows = total.shape[0]
     slots = dst_ref.shape[1]
     for ref, at, some in ((near_ref, near, True), (cross_ref, cross, there)):
-        count = jnp.where(some, len_ref[at], 0)
+        count = length_at(len_ref, at, some)
         latent = silu(dot(ref[0:slots, :], we_ref[...])).astype(BF)
         dst_hot = hot_rows(live(dst_ref[pl.ds(at, 1), :], count), mesh_rows)
         total = total + dot(dst_hot, latent)
@@ -182,46 +187,68 @@
     state_ref[...] = state
     normed = layer_norm(state.astype(F32), gain_ref[...]).astype(BF)
     normed_ref[...] = normed
-    wide[...] = normed.astype(F32)
-    published = own.shape[0]
-    for j in range(published):
-        own[j : j + 1, :] = wide[pl.ds(rows_ref[0, j], 1), :]
-    halo = own[...].astype(BF)
+    published = rows_ref.shape[1]
+    eye = lax.broadcasted_iota(jnp.int32, (published, published), 0) == lax.broadcasted_iota(
+        jnp.int32, (published, published), 1
+    )
+    column = jnp.sum(jnp.where(eye, rows_ref[...].astype(F32), 0.0), axis=1, keepdims=True)
+    ids = lax.broadcasted_iota(jnp.int32, (published, mesh_rows), 1)
+    picker = jnp.where(ids == column.astype(jnp.int32), 1.0, 0.0).astype(BF)
+    own = dot(picker, normed).astype(BF)
+    split = own.shape[1] // 2
+    halves = own[:, :split], own[:, split:]
     for b in range(bands):
-        halo_ref[b * published : (b + 1) * published, :] = halo
+        halo_ref[b * published : (b + 1) * published, :] = halves[b % 2]
+
+
+def count_labels(nbr_ref, lab_ref, inc_ref, acc_ref, rep_ref):
+    mesh_rows, table = rep_ref.shape
+    fields = table // mesh_rows
+    labels = nbr_ref[...]
+    local, step = labels, jnp.ones_like(labels)
+    for f in range(1, fields):
+        local = jnp.where(labels >= f * mesh_rows, labels - f * mesh_rows, local)
+        step = jnp.where(labels >= f * mesh_rows, 1 << (10 * f), step)
+    lab_ref[...] = local
+    inc_ref[...] = step
+    chunk = 64
+    for c in range(0, mesh_rows, chunk):
+        ids = lax.broadcasted_iota(jnp.int32, (chunk, mesh_rows), 0) + c
+        total = jnp.where(ids == lax.broadcasted_iota(jnp.int32, ids.shape, 1), 1, 0)
+        for k in range(labels.shape[0]):
+            total = total + jnp.where(ids == lab_ref[k : k + 1, :], inc_ref[k : k + 1, :], 0)
+        acc_ref[c : c + chunk, :] = total
+    counts = jnp.transpose(acc_ref[...], (1, 0))
+    for f in range(fields):
+        part = (counts >> (10 * f)) & 1023
+        rep_ref[:, f * mesh_rows : (f + 1) * mesh_rows] = part.astype(F32).astype(BF)
 
 
 def fill_body(
     bands, src_ref, dst_ref, far_dst_ref, len_ref, near_ref, cross_ref, nbr_ref,
-    links_hbm, rep_ref, links_ref, sem,
+    links_hbm, rep_ref, links_ref, lab_ref, inc_ref, acc_ref, sem,
 ):
     band, near, cross, there = around(bands)
-    mesh_rows, table = rep_ref.shape
+    mesh_rows, _ = rep_ref.shape
     rows = links_ref.shape[1]
     slots = far_dst_ref.shape[1]
     src_hot = hot_rows(src_ref[...], mesh_rows)
-    dst_hot = hot_rows(live(dst_ref[...], len_ref[band]), rows)
+    dst_hot = hot_rows(live(dst_ref[...], length_at(len_ref, band)), rows)
     links_ref[0] = dot_nt(dst_hot, src_hot).astype(BF)
     for i, (ref, at, some) in enumerate(((near_ref, near, True), (cross_ref, cross, there))):
-        count = jnp.where(some, len_ref[at], 0)
+        count = length_at(len_ref, at, some)
         src = ref[slots : slots + 1, :].astype(F32).astype(jnp.int32)
         src_hot = hot_rows(src, mesh_rows)
         dst_hot = hot_rows(live(far_dst_ref[pl.ds(at, 1), :], count), rows)
         links_ref[i + 1] = dot_nt(dst_hot, src_hot).astype(BF)
     copies = start_all([(links_ref, links_hbm)], sem)
-    labels = jnp.transpose(nbr_ref[...], (1, 0))
-    ids = lax.broadcasted_iota(jnp.int32, (mesh_rows, table), 1)
-    own = lax.broadcasted_iota(jnp.int32, (mesh_rows, 1), 0)
-    repeats = jnp.where(ids == own, 1.0, 0.0)
-    for k in range(labels.shape[1]):
-        repeats = repeats + jnp.where(ids == labels[:, k : k + 1], 1.0, 0.0)
-    rep_ref[...] = repeats.astype(BF)
+    count_labels(nbr_ref, lab_ref, inc_ref, acc_ref, rep_ref)
     for copy in copies:
         copy.wait()
 
 
 def layer_body(
-    normed_ref, far_ref, rep_ref, state_ref, gain_hbm, wr_hbm, wg_hbm, wq, wk, wv, wp, wu, wd, *refs
+    normed_ref, far_ref, got_ref, rep_ref, state_ref, gain_hbm, wr_hbm, wg_hbm, wq, wk, wv, wp, wu, wd, *refs
 ):
     pieces, refs = refs[:12], refs[12:]
     out_ref, m_ref, u_ref, d_ref, att_ref, bias_ref, gain_ref, wr_ref, wg_ref, sem = refs
@@ -258,7 +285,9 @@
     for copy in heads + heads_gain:
         copy.wait()
     normed = normed_ref[...]
-    far = far_ref[...]
+    mine, other = far_ref[...], got_ref[...]
+    first = half == 0
+    far = jnp.concatenate([jnp.where(first, mine, other), jnp.where(first, other, mine)], 1)
     queries = dot(normed, m_ref[0]).astype(BF)
     keys = jnp.concatenate([dot(normed, m_ref[1]).astype(BF), dot(far, m_ref[1]).astype(BF)], 0)
     values = jnp.concatenate([dot(normed, m_ref[2]).astype(BF), dot(far, m_ref[2]).astype(BF)], 0)
@@ -283,24 +312,24 @@
 
 
 def part_body(
-    back_ref, links_hbm, latent_hbm, ws_hbm, wo_hbm,
+    back_ref, near_ref, links_hbm, latent_hbm, ws_hbm, wo_hbm,
     out_ref, far_ref, wo_ref, own_ref, latent_ref, ws_ref, sem,
 ):
-    copies = [(latent_hbm, latent_ref), (ws_hbm, ws_ref), (links_hbm.at[0], own_ref)]
-    copies += [(links_hbm.at[1:3], far_ref), (wo_hbm, wo_ref)]
+    copies = [(latent_hbm, latent_ref), (ws_hbm, ws_ref), (links_hbm.at[0:2], own_ref)]
+    copies += [(links_hbm.at[2], far_ref), (wo_hbm, wo_ref)]
     copies = start_all(copies, sem)
     copies[0].wait()
     copies[1].wait()
     total = dot(latent_ref[...], ws_ref[...])
     copies[2].wait()
-    out_ref[...] = total + dot(own_ref[...], back_ref[...])
+    total = total + dot(own_ref[0], back_ref[...])
+    out_ref[...] = total + dot(own_ref[1], near_ref[...])
     copies[3].wait()
     copies[4].wait()
 
 
-def final_body(part_ref, links_ref, near_ref, cross_ref, wo_ref, out_ref):
-    total = part_ref[...] + dot(links_ref[0], near_ref[...])
-    total = total + dot(links_ref[1], cross_ref[...])
+def final_body(part_ref, links_ref, cross_ref, wo_ref, out_ref):
+    total = part_ref[...] + dot(links_ref[...], cross_ref[...])
     out_ref[...] = dot_nt(wo_ref[...], silu(total).astype(BF)).astype(BF)
 
 
@@ -345,8 +374,8 @@
     hidden = w_up.shape[1]
     published = halo_rows.shape[1]
     table = mesh_rows + bands * published
-    g2m_count = g2m_len.reshape(-1)
-    m2g_count = m2g_len.reshape(-1)
+    g2m_count = g2m_len.reshape(1, -1)
+    m2g_count = m2g_len.reshape(1, -1)
     w_deep = w_down.reshape(-1, piece, width)
     deep = w_deep.shape[0] // 4
     blocks = hidden // width
@@ -372,17 +401,17 @@
     def tag(where, *arrays):
         return [(where, a) for a in arrays]
 
-    near, cross, own_a, own_b, x, w_embed, g2m_own_src, g2m_own_dst = call(
+    near, cross, own_a, own_b, x, w_embed, g2m_own_src, g2m_own_dst, g2m_count = call(
         bind(pick_body, bands),
         [
             ("v", (slots + 16, channels), BF),
             ("v", (slots + 16, channels), BF),
             ("v", (4 + deep, piece, width), BF),
             ("v", (deep + blocks, piece, width), BF),
-            *map(like, (x, w_embed, g2m_own_src, g2m_own_dst)),
+            *map(like, (x, w_embed, g2m_own_src, g2m_own_dst, g2m_count)),
         ],
         tag("h", x, g2m_src[0], m2g_src[0], *square, w_up, w_deep, w_embed, g2m_own_src)
-        + tag("h", g2m_own_dst),
+        + tag("h", g2m_own_dst, g2m_count),
         [
             pltpu.VMEM(g2m_src.shape[1:], jnp.int32),
             pltpu.VMEM(m2g_src.shape[1:], jnp.int32),
@@ -409,11 +438,13 @@
         m2g_own_dst,
         m2g_dst[0],
         mesh_nbr.T,
+        halo_rows,
+        m2g_count,
     ]
     latent, agg, *ahead = call(
         bind(embed_body, len(ahead)),
         [("h", (rows, width), BF), ("v", (mesh_rows, width), F32), *map(like, ahead)],
-        tag("v", x, w_embed, g2m_own_src, g2m_own_dst) + tag("s", g2m_count) + tag("h", *ahead),
+        tag("v", x, w_embed, g2m_own_src, g2m_own_dst, g2m_count) + tag("h", *ahead),
         [pltpu.VMEM((rows, width), BF), pltpu.SemaphoreType.DMA((len(ahead) + 1,))],
         flops=int(3e9),
         nbytes=int(3e6),
@@ -423,27 +454,31 @@
         [
             ("v", (mesh_rows, width), BF),
             ("v", (mesh_rows, width), BF),
-            ("v", (bands * published, width), BF),
+            ("v", (bands * published, width // 2), BF),
         ],
         tag("v", agg)
         + tag("d", near, cross)
         + tag("v", ahead[0])
-        + tag("s", g2m_count)
-        + tag("v", w_embed, *ahead[1:5])
-        + tag("s", halo_rows),
-        [pltpu.VMEM((mesh_rows, width), F32), pltpu.VMEM((published, width), F32)],
+        + tag("v", g2m_count, w_embed, *ahead[1:5], ahead[9]),
         flops=int(1e9),
         nbytes=int(3e6),
     )
     far = lax.all_to_all(halo, "space", 0, 0, tiled=True)
+    got = pass_on(far, swap)
     links, repeats = call(
         bind(fill_body, bands),
         [("h", (3, rows, mesh_rows), BF), ("v", (mesh_rows, table), BF)],
         tag("v", *ahead[5:8])
-        + tag("s", m2g_count)
+        + tag("v", ahead[10])
         + tag("d", near, cross)
         + tag("v", ahead[8]),
-        [pltpu.VMEM((3, rows, mesh_rows), BF), pltpu.SemaphoreType.DMA((1,))],
+        [
+            pltpu.VMEM((3, rows, mesh_rows), BF),
+            pltpu.VMEM(ahead[8].shape, jnp.int32),
+            pltpu.VMEM(ahead[8].shape, jnp.int32),
+            pltpu.VMEM((mesh_rows, mesh_rows), jnp.int32),
+            pltpu.SemaphoreType.DMA((1,)),
+        ],
         flops=int(4e9),
         nbytes=int(8e6),
     )
@@ -453,12 +488,12 @@
         layer_body,
         [("v", (mesh_rows, width), BF)],
         tag("v", normed)
-        + tag("d", far)
+        + tag("d", far, got)
         + tag("v", repeats, state)
         + tag("h", mlp_gain.reshape(1, width), w_return, w_grid)
         + tag("h", *square, w_up, w_deep)
         + tag("h", *fetched)
-        + [("v" if i in (0, 2, 3) else "h", w) for i, w in enumerate(shared)],
+        + [("v" if i in (4, 5) else "h", w) for i, w in enumerate(shared)],
         [
             pltpu.VMEM((4, 4 * part, width), BF),
             pltpu.VMEM((blocks, 4 * part, width), BF),
@@ -477,10 +512,10 @@
     back_cross = pass_on(back, chain)
     part, far_links, w_last = call(
         part_body,
-        [("v", (rows, width), F32), ("v", (2, rows, mesh_rows), BF), like(w_out.T)],
-        tag("v", back) + tag("h", links, latent, w_skip, w_out.T),
+        [("v", (rows, width), F32), ("v", (rows, mesh_rows), BF), like(w_out.T)],
+        tag("v", back) + tag("d", back_near) + tag("h", links, latent, w_skip, w_out.T),
         [
-            pltpu.VMEM((rows, mesh_rows), BF),
+            pltpu.VMEM((2, rows, mesh_rows), BF),
             pltpu.VMEM((rows, width), BF),
             pltpu.VMEM((width, width), BF),
             pltpu.SemaphoreType.DMA((5,)),
@@ -491,7 +526,7 @@
     (result,) = call(
         final_body,
         [("d", (w_out.shape[1], rows), BF)],
-        tag("v", part, far_links) + tag("d", back_near, back_cross) + tag("v", w_last),
+        tag("v", part, far_links) + tag("d", back_cross) + tag("v", w_last),
         flops=int(2e9),
         nbytes=int(8e6),
     )

time: 62.3 us -> 72.3 us (1.16)
  waiting for transfers between devices: 10.6 us -> 18.9 us
  starting transfers between devices: 24 us -> 29.3 us
  Pallas kernels: 26.2 us -> 22.7 us
    ppermute x6, waiting for transfers between devices: 4.46 us -> 10.4 us  [turn(): return lax.ppermute(block, 'member', [(i, i ^ d) for i in range(4)])]
    all_to_all x1, starting transfers between devices: 8.38 us -> 12.9 us  [shards(): far = lax.all_to_all(halo, 'space', 0, 0, tiled=True)]
    pallas_call x7, Pallas kernels: 26.2 us -> 22.7 us  [call(): pl.pallas_call(body, out_shape=shapes, in_specs=[specs[w] for w, _ in ope...]
    all_to_all x1, waiting for transfers between devices: 2.37 us -> 3.63 us  [shards(): far = lax.all_to_all(halo, 'space', 0, 0, tiled=True)]
    ppermute x10 -> x11, waiting for transfers between devices: 3.75 us -> 4.8 us  [pass_on(): return lax.ppermute(block, axes, route)]
    ppermute x10 -> x11, starting transfers between devices: 8.66 us -> 9.21 us  [pass_on(): return lax.ppermute(block, axes, route)]
  transfers between devices with their start and end apart: 17 -> 18, of which waited for: 3 -> 5; matrix products, arithmetic and copies ran while one was open for 0% -> 0% of each run, Pallas kernels for 24% -> 16%
where the time goes in v5:
time: 72.3 us; the launch traced here: 72 us
  starting transfers between devices  29.3 us (41%)
  Pallas kernels  22.7 us (31%)
  waiting for transfers between devices  18.9 us (26%)
  local copies, waits for them, and re-layouts  0.98 us (1%)
    pallas_call x7, Pallas kernels, call(): pl.pallas_call(body, out_shape=shapes, in_specs=[specs[w] for w, _ in ope...  22.7 us
    all_to_all x1, starting transfers between devices, shards(): far = lax.all_to_all(halo, 'space', 0, 0, tiled=True)  12.9 us
    ppermute x6, waiting for transfers between devices, turn(): return lax.ppermute(block, 'member', [(i, i ^ d) for i in range(4)])  10.4 us
    ppermute x11, starting transfers between devices, pass_on(): return lax.ppermute(block, axes, route)  9.21 us
    ppermute x6, starting transfers between devices, turn(): return lax.ppermute(block, 'member', [(i, i ^ d) for i in range(4)])  7.18 us
    ppermute x11, waiting for transfers between devices, pass_on(): return lax.ppermute(block, axes, route)  4.8 us
    all_to_all x1, waiting for transfers between devices, shards(): far = lax.all_to_all(halo, 'space', 0, 0, tiled=True)  3.63 us
  transfers between devices with their start and end apart: 18, of which 5 were waited for; matrix products, arithmetic and copies ran while one was open for 0% of the time, Pallas kernels for 16%

profile of v5, /device:TPU:7, one launch (start us, length us, event | category | flops | bytes accessed | tf_op | source)
XLA Modules:
  0.0 72.0 jit_solution(4621547121645803700)
XLA Ops:
  0.0 1.8 %shard_map.271 = (bf16[272,256]{1,0:T(8,128)(2,1)S(1)}, bf16[272,256]{1,0:T(8,128)(2,1)S(1)}, bf16[6,64,512]{2,1,0:T(8,128)(2,1)S(1)}, bf16[6,64,512]{2,1,0:T(8,...) custom-call(bf16[1024,256]{1,0:T(8,128)(2,1)} %bitcast.17, ...), custom_call_target="tpu_custom_call" | custom-call | flops 300000000 | bytes 3000000 | tf_op jit(solution)/shard_map/pallas_call | solution.py:66
  1.8 2.8 %collective-permute-start.6 = (bf16[6,64,512]{2,1,0:T(8,128)(2,1)S(1)}, bf16[6,64,512]{2,1,0:T(8,128)(2,1)S(1)}, u32[]{:S(2)}, u32[]{:S(2)}) collective-permute-start(bf16[6,64,512]{2,1,0:T(8,128)(2,1)S(1)} %get-tuple-element.59), channel_id=1, source_target_pairs={{0,96},{32,64},{64,32},{96,0},{1,97},{33,65},{65,33},{97,1},{2,98}... | collective-permute-start | bytes 1179656 | tf_op jit(solution)/shard_map/ppermute | solution.py:392
  4.6 1.1 %collective-permute-start = (bf16[272,256]{1,0:T(8,128)(2,1)S(1)}, bf16[272,256]{1,0:T(8,128)(2,1)S(1)}, u32[]{:S(2)}, u32[]{:S(2)}) collective-permute-start(bf16[272,256]{1,0:T(8,128)(2,1)S(1)} %get-tuple-element.41), channel_id=1, source_target_pairs={{0,1},{1,0},{2,3},{3,2},{4,5},{5,4},{6,7},{7,6},{8,9},{9,8},{10,11... | collective-permute-start | bytes 417800 | tf_op jit(solution)/shard_map/ppermute | solution.py:396
  5.7 1.4 %collective-permute-start.1 = (bf16[272,256]{1,0:T(8,128)(2,1)S(1)}, bf16[272,256]{1,0:T(8,128)(2,1)S(1)}, u32[]{:S(2)}, u32[]{:S(2)}) collective-permute-start(bf16[272,256]{1,0:T(8,128)(2,1)S(1)} %get-tuple-element.42), channel_id=1, source_target_pairs={{0,32},{1,2},{2,1},{3,4},{4,3},{5,6},{6,5},{7,8},{8,7},{9,10},{10,... | collective-permute-start | bytes 417800 | tf_op jit(solution)/shard_map/ppermute | solution.py:396
  7.1 1.6 %collective-permute-start.3 = (bf16[6,64,512]{2,1,0:T(8,128)(2,1)S(1)}, bf16[6,64,512]{2,1,0:T(8,128)(2,1)S(1)}, u32[]{:S(2)}, u32[]{:S(2)}) collective-permute-start(bf16[6,64,512]{2,1,0:T(8,128)(2,1)S(1)} %get-tuple-element.58), channel_id=1, source_target_pairs={{0,32},{32,0},{64,96},{96,64},{1,33},{33,1},{65,97},{97,65},{2,34}... | collective-permute-start | bytes 1179656 | tf_op jit(solution)/shard_map/ppermute | solution.py:392
  8.8 2.3 %shard_map.272 = (bf16[1024,512]{1,0:T(8,128)(2,1)}, f32[256,512]{1,0:T(8,128)S(1)}, s32[32,256]{1,0:T(8,128)S(1)}, bf16[512,512]{1,0:T(8,128)(2,1)S(1)}, bf16[5...) custom-call(bf16[1024,256]{1,0:T(8,128)(2,1)S(1)} %get-tuple-element, ...), custom_call_target="tpu_custom_call" | custom-call | flops 3000000000 | bytes 3000000 | tf_op jit(solution)/shard_map/pallas_call | solution.py:66
  11.1 1.2 %collective-permute-done.1.cross_ref = bf16[272,256]{1,0:T(8,128)(2,1)S(1)} collective-permute-done((bf16[272,256]{1,0:T(8,128)(2,1)S(1)}, bf16[272,256]{1,0:T(8,128)(2,1)S(1)}, u32[]{:S(2)}, u32[]{:S(2)}) %collective-permute-start.1) | collective-permute-done | bytes 139296 | tf_op jit(solution)/shard_map/ppermute | solution.py:396
  12.3 2.3 %shard_map.273 = (bf16[256,512]{1,0:T(8,128)(2,1)S(1)}, bf16[256,512]{1,0:T(8,128)(2,1)S(1)}, bf16[512,256]{1,0:T(8,128)(2,1)}) custom-call(f32[256,512]{1,0:T(8,128)S(1)} %get-tuple-element.40.agg_ref, bf16[272,256]{1,0:T(8,128)(2,1)S(1)} %collective-permute-done.near_ref, bf16[272,256]{1,0:T(8,128)(2,1)S(1)} %collective-permute-done.1.cross_ref, ...), custom_call_target="tpu_custom_call" | custom-call | flops 1000000000 | bytes 3000000 | tf_op jit(solution)/shard_map/pallas_call | solution.py:66
  14.6 12.9 %all-to-all-start = ((bf16[32,16,256]{2,1,0:T(8,128)(2,1)}), bf16[32,16,256]{2,1,0:T(8,128)(2,1)S(1)}, u32[]{:S(2)}, u32[]{:S(2)}) async-start(bf16[32,16,256]{2,1,0:T(8,128)(2,1)} %bitcast.10), calls=%async_computation | async-start | bytes 524288 | tf_op jit(solution)/shard_map/all_to_all | solution.py:466
  27.8 2.4 %collective-permute-start.7 = (bf16[6,64,512]{2,1,0:T(8,128)(2,1)S(1)}, bf16[6,64,512]{2,1,0:T(8,128)(2,1)}, u32[]{:S(2)}, u32[]{:S(2)}) collective-permute-start(bf16[6,64,512]{2,1,0:T(8,128)(2,1)S(1)} %collective-permute-done.3.refs_0_), channel_id=1, source_target_pairs={{0,96},{32,64},{64,32},{96,0},{1,97},{33,65},{65,33},{97,1},{2,98}... | collective-permute-start | bytes 1179656 | tf_op jit(solution)/shard_map/ppermute | solution.py:392
  30.3 1.0 %collective-permute-start.12 = (bf16[6,64,512]{2,1,0:T(8,128)(2,1)S(1)}, bf16[6,64,512]{2,1,0:T(8,128)(2,1)}, u32[]{:S(2)}, u32[]{:S(2)}) collective-permute-start(bf16[6,64,512]{2,1,0:T(8,128)(2,1)S(1)} %collective-permute-done.6.refs_3_), channel_id=1, source_target_pairs={{0,1},{1,0},{2,3},{3,2},{4,5},{5,4},{6,7},{7,6},{8,9},{9,8},{10,11... | collective-permute-start | bytes 1179656 | tf_op jit(solution)/shard_map/ppermute | solution.py:396
  31.3 3.6 %all-to-all-done = bf16[32,16,256]{2,1,0:T(8,128)(2,1)S(1)} async-done(((bf16[32,16,256]{2,1,0:T(8,128)(2,1)}), bf16[32,16,256]{2,1,0:T(8,128)(2,1)S(1)}, u32[]{:S(2)}, u32[]{:S(2)}) %all-to-all-start) | async-done | bytes 262176 | tf_op jit(solution)/shard_map/all_to_all | solution.py:466
  35.0 4.1 %collective-permute-done.5.refs_2_ = bf16[6,64,512]{2,1,0:T(8,128)(2,1)S(1)} collective-permute-done((bf16[6,64,512]{2,1,0:T(8,128)(2,1)S(1)}, bf16[6,64,512]{2,1,0:T(8,128)(2,1)S(1)}, u32[]{:S(2)}, u32[]{:S(2)}) %collective-permute-start.5) | collective-permute-done | bytes 393248 | tf_op jit(solution)/shard_map/ppermute | solution.py:392
  39.1 2.1 %collective-permute-start.9 = (bf16[6,64,512]{2,1,0:T(8,128)(2,1)S(1)}, bf16[6,64,512]{2,1,0:T(8,128)(2,1)S(1)}, u32[]{:S(2)}, u32[]{:S(2)}) collective-permute-start(bf16[6,64,512]{2,1,0:T(8,128)(2,1)S(1)} %collective-permute-done.3.refs_0_), channel_id=1, source_target_pairs={{0,1},{1,0},{2,3},{3,2},{4,5},{5,4},{6,7},{7,6},{8,9},{9,8},{10,11... | collective-permute-start | bytes 1179656 | tf_op jit(solution)/shard_map/ppermute | solution.py:396
  41.3 6.3 %collective-permute-done.7.refs_4_ = bf16[6,64,512]{2,1,0:T(8,128)(2,1)} collective-permute-done((bf16[6,64,512]{2,1,0:T(8,128)(2,1)S(1)}, bf16[6,64,512]{2,1,0:T(8,128)(2,1)}, u32[]{:S(2)}, u32[]{:S(2)}) %collective-permute-start.7) | collective-permute-done | bytes 393248 | tf_op jit(solution)/shard_map/ppermute | solution.py:392
  47.6 1.3 %collective-permute-start.11 = (bf16[6,64,512]{2,1,0:T(8,128)(2,1)S(1)}, bf16[6,64,512]{2,1,0:T(8,128)(2,1)S(1)}, u32[]{:S(2)}, u32[]{:S(2)}) collective-permute-start(bf16[6,64,512]{2,1,0:T(8,128)(2,1)S(1)} %collective-permute-done.5.refs_2_), channel_id=1, source_target_pairs={{0,1},{1,0},{2,3},{3,2},{4,5},{5,4},{6,7},{7,6},{8,9},{9,8},{10,11... | collective-permute-start | bytes 1179656 | tf_op jit(solution)/shard_map/ppermute | solution.py:396
  48.9 0.5 collective-permute-start.14
  49.4 4.1 %shard_map.274 = (bf16[3,1024,256]{2,1,0:T(8,128)(2,1)}, bf16[256,768]{1,0:T(8,128)(2,1)S(1)}) custom-call(s32[1,2560]{1,0:T(1,128)S(1)} %get-tuple-element.51.src_ref, s32[1,2560]{1,0:T(1,128)S(1)} %get-tuple-element.52.dst_ref, s32[32,256]{1,0:T(8,128)S(1)} %get-tuple-element.53.far_dst_ref, s32[1,32]{1,0:T(1,128)S(1)} %get-tuple-element.54.len_ref, ...), custom_call_target="tpu_custom_call" | custom-call | flops 4000000000 | bytes 8000000 | tf_op jit(solution)/shard_map/pallas_call | solution.py:66
  53.6 0.7 copy-done.4
  54.5 7.7 %shard_map.275.back_ref = bf16[256,512]{1,0:T(8,128)(2,1)S(1)} custom-call(bf16[256,512]{1,0:T(8,128)(2,1)S(1)} %get-tuple-element.49.normed_ref, bf16[512,256]{1,0:T(8,128)(2,1)S(1)} %bitcast.16, bf16[512,256]{1,0:T(8,128)(2,1)S(1)} %collective-permute-done.2.got_ref, bf16[256,768]{1,0:T(8,128)(2,1)S(1)} %get-tuple-element.56.rep_ref, ...), custom_call_target="tpu_custom_call" | custom-call | flops 5000000000 | bytes 6000000 | tf_op jit(solution)/shard_map/pallas_call | solution.py:66
  62.6 1.3 %collective-permute-start.16 = (bf16[256,512]{1,0:T(8,128)(2,1)S(1)}, bf16[256,512]{1,0:T(8,128)(2,1)S(1)}, u32[]{:S(2)}, u32[]{:S(2)}) collective-permute-start(bf16[256,512]{1,0:T(8,128)(2,1)S(1)} %shard_map.275.back_ref), channel_id=1, source_target_pairs={{0,32},{1,2},{2,1},{3,4},{4,3},{5,6},{6,5},{7,8},{8,7},{9,10},{10,... | collective-permute-start | bytes 786440 | tf_op jit(solution)/shard_map/ppermute | solution.py:396
  63.9 3.0 %shard_map.276 = (f32[1024,512]{1,0:T(8,128)S(1)}, bf16[1024,256]{1,0:T(8,128)(2,1)S(1)}, bf16[84,512]{1,0:T(8,128)(2,1)S(1)}) custom-call(bf16[256,512]{1,0:T(8,128)(2,1)S(1)} %shard_map.275.back_ref, bf16[256,512]{1,0:T(8,128)(2,1)S(1)} %collective-permute-done.15.near_ref, bf16[3,1024,256]{2,1,0:T(8,128)(2,1)} %get-tuple-element.60.links_hbm, ...), custom_call_target="tpu_custom_call" | custom-call | flops 1000000000 | bytes 2000000 | tf_op jit(solution)/shard_map/pallas_call | solution.py:66
  66.9 3.6 %collective-permute-done.16.cross_ref = bf16[256,512]{1,0:T(8,128)(2,1)S(1)} collective-permute-done((bf16[256,512]{1,0:T(8,128)(2,1)S(1)}, bf16[256,512]{1,0:T(8,128)(2,1)S(1)}, u32[]{:S(2)}, u32[]{:S(2)}) %collective-permute-start.16) | collective-permute-done | bytes 262176 | tf_op jit(solution)/shard_map/ppermute | solution.py:396
  70.5 1.5 %shard_map.277 = bf16[84,1024]{1,0:T(8,128)(2,1)} custom-call(f32[1024,512]{1,0:T(8,128)S(1)} %get-tuple-element.62.part_ref, bf16[1024,256]{1,0:T(8,128)(2,1)S(1)} %get-tuple-element.63.links_ref, bf16[256,512]{1,0:T(8,128)(2,1)S(1)} %collective-permute-done.16.cross_ref, bf16[84,512]{1,0:T(8,128)(2,1)S(1)} %get-tuple-element.64.wo_ref), custom_call_target="tpu_custom_call" | custom-call | flops 2000000000 | bytes 8000000 | tf_op jit(solution)/shard_map/pallas_call | solution.py:66
  (33 shorter events, 1.1 us)
Async XLA Ops:
  1.8 28.5 %collective-permute-start.6 = (bf16[6,64,512]{2,1,0:T(8,128)(2,1)S(1)}, bf16[6,64,512]{2,1,0:T(8,128)(2,1)S(1)}, u32[]{:S(2)}, u32[]{:S(2)}) collective-permute-start(bf16[6,64,512]{2,1,0:T(8,128)(2,1)S(1)} %get-tuple-element.59), channel_id=1, source_target_pairs={{0,96},{32,64},{64,32},{96,0},{1,97},{33,65},{65,33},{97,1},{2,98}... | collective-permute-start | bytes 1179656 | tf_op jit(solution)/shard_map/ppermute | solution.py:392
  4.6 26.7 %collective-permute-start.4 = (bf16[6,64,512]{2,1,0:T(8,128)(2,1)S(1)}, bf16[6,64,512]{2,1,0:T(8,128)(2,1)S(1)}, u32[]{:S(2)}, u32[]{:S(2)}) collective-permute-start(bf16[6,64,512]{2,1,0:T(8,128)(2,1)S(1)} %get-tuple-element.59), channel_id=1, source_target_pairs={{0,32},{32,0},{64,96},{96,64},{1,33},{33,1},{65,97},{97,65},{2,34}... | collective-permute-start | bytes 1179656 | tf_op jit(solution)/shard_map/ppermute | solution.py:392
  4.6 6.5 %collective-permute-start = (bf16[272,256]{1,0:T(8,128)(2,1)S(1)}, bf16[272,256]{1,0:T(8,128)(2,1)S(1)}, u32[]{:S(2)}, u32[]{:S(2)}) collective-permute-start(bf16[272,256]{1,0:T(8,128)(2,1)S(1)} %get-tuple-element.41), channel_id=1, source_target_pairs={{0,1},{1,0},{2,3},{3,2},{4,5},{5,4},{6,7},{7,6},{8,9},{9,8},{10,11... | collective-permute-start | bytes 417800 | tf_op jit(solution)/shard_map/ppermute | solution.py:396
  5.7 6.6 %collective-permute-start.1 = (bf16[272,256]{1,0:T(8,128)(2,1)S(1)}, bf16[272,256]{1,0:T(8,128)(2,1)S(1)}, u32[]{:S(2)}, u32[]{:S(2)}) collective-permute-start(bf16[272,256]{1,0:T(8,128)(2,1)S(1)} %get-tuple-element.42), channel_id=1, source_target_pairs={{0,32},{1,2},{2,1},{3,4},{4,3},{5,6},{6,5},{7,8},{8,7},{9,10},{10,... | collective-permute-start | bytes 417800 | tf_op jit(solution)/shard_map/ppermute | solution.py:396
  7.1 20.7 %collective-permute-start.3 = (bf16[6,64,512]{2,1,0:T(8,128)(2,1)S(1)}, bf16[6,64,512]{2,1,0:T(8,128)(2,1)S(1)}, u32[]{:S(2)}, u32[]{:S(2)}) collective-permute-start(bf16[6,64,512]{2,1,0:T(8,128)(2,1)S(1)} %get-tuple-element.58), channel_id=1, source_target_pairs={{0,32},{32,0},{64,96},{96,64},{1,33},{33,1},{65,97},{97,65},{2,34}... | collective-permute-start | bytes 1179656 | tf_op jit(solution)/shard_map/ppermute | solution.py:392
  14.6 20.3 %all-to-all-start = ((bf16[32,16,256]{2,1,0:T(8,128)(2,1)}), bf16[32,16,256]{2,1,0:T(8,128)(2,1)S(1)}, u32[]{:S(2)}, u32[]{:S(2)}) async-start(bf16[32,16,256]{2,1,0:T(8,128)(2,1)} %bitcast.10), calls=%async_computation | async-start | bytes 524288 | tf_op jit(solution)/shard_map/all_to_all | solution.py:466
  27.5 11.6 %collective-permute-start.5 = (bf16[6,64,512]{2,1,0:T(8,128)(2,1)S(1)}, bf16[6,64,512]{2,1,0:T(8,128)(2,1)S(1)}, u32[]{:S(2)}, u32[]{:S(2)}) collective-permute-start(bf16[6,64,512]{2,1,0:T(8,128)(2,1)S(1)} %get-tuple-element.58), channel_id=1, source_target_pairs={{0,96},{32,64},{64,32},{96,0},{1,97},{33,65},{65,33},{97,1},{2,98}... | collective-permute-start | bytes 1179656 | tf_op jit(solution)/shard_map/ppermute | solution.py:392
  27.8 25.6 %copy-start.2 = (bf16[6,64,512]{2,1,0:T(8,128)(2,1)}, bf16[6,64,512]{2,1,0:T(8,128)(2,1)S(1)}, u32[]{:S(2)}) copy-start(bf16[6,64,512]{2,1,0:T(8,128)(2,1)S(1)} %collective-permute-done.3.refs_0_) | copy-start | bytes 1179652
  27.8 19.8 %collective-permute-start.7 = (bf16[6,64,512]{2,1,0:T(8,128)(2,1)S(1)}, bf16[6,64,512]{2,1,0:T(8,128)(2,1)}, u32[]{:S(2)}, u32[]{:S(2)}) collective-permute-start(bf16[6,64,512]{2,1,0:T(8,128)(2,1)S(1)} %collective-permute-done.3.refs_0_), channel_id=1, source_target_pairs={{0,96},{32,64},{64,32},{96,0},{1,97},{33,65},{65,33},{97,1},{2,98}... | collective-permute-start | bytes 1179656 | tf_op jit(solution)/shard_map/ppermute | solution.py:392
  30.3 23.2 %copy-start = (bf16[6,64,512]{2,1,0:T(8,128)(2,1)}, bf16[6,64,512]{2,1,0:T(8,128)(2,1)S(1)}, u32[]{:S(2)}) copy-start(bf16[6,64,512]{2,1,0:T(8,128)(2,1)S(1)} %collective-permute-done.6.refs_3_) | copy-start | bytes 1179652
  30.3 18.6 %collective-permute-start.8 = (bf16[6,64,512]{2,1,0:T(8,128)(2,1)S(1)}, bf16[6,64,512]{2,1,0:T(8,128)(2,1)}, u32[]{:S(2)}, u32[]{:S(2)}) collective-permute-start(bf16[6,64,512]{2,1,0:T(8,128)(2,1)S(1)} %collective-permute-done.6.refs_3_), channel_id=1, source_target_pairs={{0,32},{32,0},{64,96},{96,64},{1,33},{33,1},{65,97},{97,65},{2,34}... | collective-permute-start | bytes 1179656 | tf_op jit(solution)/shard_map/ppermute | solution.py:392
  30.3 18.6 %collective-permute-start.12 = (bf16[6,64,512]{2,1,0:T(8,128)(2,1)S(1)}, bf16[6,64,512]{2,1,0:T(8,128)(2,1)}, u32[]{:S(2)}, u32[]{:S(2)}) collective-permute-start(bf16[6,64,512]{2,1,0:T(8,128)(2,1)S(1)} %collective-permute-done.6.refs_3_), channel_id=1, source_target_pairs={{0,1},{1,0},{2,3},{3,2},{4,5},{5,4},{6,7},{7,6},{8,9},{9,8},{10,11... | collective-permute-start | bytes 1179656 | tf_op jit(solution)/shard_map/ppermute | solution.py:396
  31.3 22.2 %copy-start.1 = (bf16[6,64,512]{2,1,0:T(8,128)(2,1)}, bf16[6,64,512]{2,1,0:T(8,128)(2,1)S(1)}, u32[]{:S(2)}) copy-start(bf16[6,64,512]{2,1,0:T(8,128)(2,1)S(1)} %collective-permute-done.4.refs_1_) | copy-start | bytes 1179652
  35.0 6.2 %collective-permute-start.2 = (bf16[512,256]{1,0:T(8,128)(2,1)S(1)}, bf16[512,256]{1,0:T(8,128)(2,1)S(1)}, u32[]{:S(2)}, u32[]{:S(2)}) collective-permute-start(bf16[512,256]{1,0:T(8,128)(2,1)S(1)} %bitcast.15), channel_id=1, source_target_pairs={{0,1},{1,0},{2,3},{3,2},{4,5},{5,4},{6,7},{7,6},{8,9},{9,8},{10,11... | collective-permute-start | bytes 786440 | tf_op jit(solution)/shard_map/ppermute | solution.py:396
  39.1 14.4 %copy-start.3 = (bf16[6,64,512]{2,1,0:T(8,128)(2,1)}, bf16[6,64,512]{2,1,0:T(8,128)(2,1)S(1)}, u32[]{:S(2)}) copy-start(bf16[6,64,512]{2,1,0:T(8,128)(2,1)S(1)} %collective-permute-done.5.refs_2_) | copy-start | bytes 1179652
  39.1 14.4 %collective-permute-start.9 = (bf16[6,64,512]{2,1,0:T(8,128)(2,1)S(1)}, bf16[6,64,512]{2,1,0:T(8,128)(2,1)S(1)}, u32[]{:S(2)}, u32[]{:S(2)}) collective-permute-start(bf16[6,64,512]{2,1,0:T(8,128)(2,1)S(1)} %collective-permute-done.3.refs_0_), channel_id=1, source_target_pairs={{0,1},{1,0},{2,3},{3,2},{4,5},{5,4},{6,7},{7,6},{8,9},{9,8},{10,11... | collective-permute-start | bytes 1179656 | tf_op jit(solution)/shard_map/ppermute | solution.py:396
  41.2 12.3 %collective-permute-start.10 = (bf16[6,64,512]{2,1,0:T(8,128)(2,1)S(1)}, bf16[6,64,512]{2,1,0:T(8,128)(2,1)S(1)}, u32[]{:S(2)}, u32[]{:S(2)}) collective-permute-start(bf16[6,64,512]{2,1,0:T(8,128)(2,1)S(1)} %collective-permute-done.4.refs_1_), channel_id=1, source_target_pairs={{0,1},{1,0},{2,3},{3,2},{4,5},{5,4},{6,7},{7,6},{8,9},{9,8},{10,11... | collective-permute-start | bytes 1179656 | tf_op jit(solution)/shard_map/ppermute | solution.py:396
  47.6 5.9 %collective-permute-start.11 = (bf16[6,64,512]{2,1,0:T(8,128)(2,1)S(1)}, bf16[6,64,512]{2,1,0:T(8,128)(2,1)S(1)}, u32[]{:S(2)}, u32[]{:S(2)}) collective-permute-start(bf16[6,64,512]{2,1,0:T(8,128)(2,1)S(1)} %collective-permute-done.5.refs_2_), channel_id=1, source_target_pairs={{0,1},{1,0},{2,3},{3,2},{4,5},{5,4},{6,7},{7,6},{8,9},{9,8},{10,11... | collective-permute-start | bytes 1179656 | tf_op jit(solution)/shard_map/ppermute | solution.py:396
  48.9 4.7 %collective-permute-start.13 = (bf16[6,64,512]{2,1,0:T(8,128)(2,1)}, bf16[6,64,512]{2,1,0:T(8,128)(2,1)S(1)}, u32[]{:S(2)}, u32[]{:S(2)}) collective-permute-start(bf16[6,64,512]{2,1,0:T(8,128)(2,1)} %collective-permute-done.7.refs_4_), channel_id=1, source_target_pairs={{0,1},{1,0},{2,3},{3,2},{4,5},{5,4},{6,7},{7,6},{8,9},{9,8},{10,11... | collective-permute-start | bytes 1179656 | tf_op jit(solution)/shard_map/ppermute | solution.py:396
  48.9 4.7 %collective-permute-start.14 = (bf16[6,64,512]{2,1,0:T(8,128)(2,1)}, bf16[6,64,512]{2,1,0:T(8,128)(2,1)S(1)}, u32[]{:S(2)}, u32[]{:S(2)}) collective-permute-start(bf16[6,64,512]{2,1,0:T(8,128)(2,1)} %collective-permute-done.8.refs_5_), channel_id=1, source_target_pairs={{0,1},{1,0},{2,3},{3,2},{4,5},{5,4},{6,7},{7,6},{8,9},{9,8},{10,11... | collective-permute-start | bytes 1179656 | tf_op jit(solution)/shard_map/ppermute | solution.py:396
  53.5 0.9 %copy-start.5 = (bf16[6,64,512]{2,1,0:T(8,128)(2,1)}, bf16[6,64,512]{2,1,0:T(8,128)(2,1)S(1)}, u32[]{:S(2)}) copy-start(bf16[6,64,512]{2,1,0:T(8,128)(2,1)S(1)} %collective-permute-done.10.refs_7_) | copy-start | bytes 1179652
  53.6 1.0 %copy-start.6 = (bf16[6,64,512]{2,1,0:T(8,128)(2,1)}, bf16[6,64,512]{2,1,0:T(8,128)(2,1)S(1)}, u32[]{:S(2)}) copy-start(bf16[6,64,512]{2,1,0:T(8,128)(2,1)S(1)} %collective-permute-done.11.refs_8_) | copy-start | bytes 1179652
  62.3 1.7 %collective-permute-start.15 = (bf16[256,512]{1,0:T(8,128)(2,1)S(1)}, bf16[256,512]{1,0:T(8,128)(2,1)S(1)}, u32[]{:S(2)}, u32[]{:S(2)}) collective-permute-start(bf16[256,512]{1,0:T(8,128)(2,1)S(1)} %shard_map.275.back_ref), channel_id=1, source_target_pairs={{0,1},{1,0},{2,3},{3,2},{4,5},{5,4},{6,7},{7,6},{8,9},{9,8},{10,11... | collective-permute-start | bytes 786440 | tf_op jit(solution)/shard_map/ppermute | solution.py:396
  62.6 7.9 %collective-permute-start.16 = (bf16[256,512]{1,0:T(8,128)(2,1)S(1)}, bf16[256,512]{1,0:T(8,128)(2,1)S(1)}, u32[]{:S(2)}, u32[]{:S(2)}) collective-permute-start(bf16[256,512]{1,0:T(8,128)(2,1)S(1)} %shard_map.275.back_ref), channel_id=1, source_target_pairs={{0,32},{1,2},{2,1},{3,4},{4,3},{5,6},{6,5},{7,8},{8,7},{9,10},{10,... | collective-permute-start | bytes 786440 | tf_op jit(solution)/shard_map/ppermute | solution.py:396
  (1 other events, 0.8 us)

commit v6 on v5

--- a/solution.py
+++ b/solution.py
@@ -277,13 +277,12 @@
             downs.append((a.at[count:], d_ref.at[pl.ds(low, deep)]))
             downs.append((b.at[0:deep], d_ref.at[pl.ds(low + deep, deep)]))
     heads = start_all(heads, sem)
+    downs += [(gain_hbm, gain_ref), (wr_hbm, wr_ref), (wg_hbm, wg_ref)]
+    bias_ref[...] = jnp.log(rep_ref[...].astype(F32)) * LOG2E
+    for copy in heads:
+        copy.wait()
     ups = start_all(ups, sem, len(heads))
-    downs += [(wr_hbm, wr_ref), (wg_hbm, wg_ref)]
-    heads_gain = start_all([(gain_hbm, gain_ref)], sem, len(heads) + len(ups) + len(downs))
     downs = start_all(downs, sem, len(heads) + len(ups))
-    bias_ref[...] = jnp.log(rep_ref[...].astype(F32)) * LOG2E
-    for copy in heads + heads_gain:
-        copy.wait()
     normed = normed_ref[...]
     mine, other = far_ref[...], got_ref[...]
     first = half == 0
@@ -291,16 +290,18 @@
     queries = dot(normed, m_ref[0]).astype(BF)
     keys = jnp.concatenate([dot(normed, m_ref[1]).astype(BF), dot(far, m_ref[1]).astype(BF)], 0)
     values = jnp.concatenate([dot(normed, m_ref[2]).astype(BF), dot(far, m_ref[2]).astype(BF)], 0)
+    ones = jnp.ones((values.shape[0], DH), BF)
     for h in range(width // DH):
         at = slice(h * DH, (h + 1) * DH)
         scores = dot_nt(queries[:, at], keys[:, at]) * (LOG2E / math.sqrt(DH)) + bias_ref[...]
         weights = jnp.exp2(scores - jnp.max(scores, axis=-1, keepdims=True))
-        total = jnp.sum(weights, axis=-1, keepdims=True)
-        att_ref[:, at] = (dot(weights.astype(BF), values[:, at]) / total).astype(BF)
+        both = jnp.concatenate([values[:, at], ones], 1)
+        mixed = dot(weights.astype(BF), both)
+        att_ref[:, at] = (mixed[:, :DH] / mixed[:, DH:]).astype(BF)
     after = state_ref[...].astype(F32) + dot(att_ref[...], m_ref[3])
-    normed = layer_norm(after, gain_ref[...]).astype(BF)
     for copy in ups + downs:
         copy.wait()
+    normed = layer_norm(after, gain_ref[...]).astype(BF)
     total = after
     span = width // piece
     for i in range(blocks):

time: 72.3 us -> 72.2 us (level)
  no operation moved by 1% of the time
where the time goes in v6:
time: 72.2 us; the launch traced here: 72 us
  starting transfers between devices  29.3 us (41%)
  Pallas kernels  22.7 us (31%)
  waiting for transfers between devices  18.9 us (26%)
  local copies, waits for them, and re-layouts  0.98 us (1%)
    pallas_call x7, Pallas kernels, call(): pl.pallas_call(body, out_shape=shapes, in_specs=[specs[w] for w, _ in ope...  22.7 us
    all_to_all x1, starting transfers between devices, shards(): far = lax.all_to_all(halo, 'space', 0, 0, tiled=True)  12.9 us
    ppermute x6, waiting for transfers between devices, turn(): return lax.ppermute(block, 'member', [(i, i ^ d) for i in range(4)])  10.4 us
    ppermute x11, starting transfers between devices, pass_on(): return lax.ppermute(block, axes, route)  9.21 us
    ppermute x6, starting transfers between devices, turn(): return lax.ppermute(block, 'member', [(i, i ^ d) for i in range(4)])  7.18 us
    ppermute x11, waiting for transfers between devices, pass_on(): return lax.ppermute(block, axes, route)  4.8 us
    all_to_all x1, waiting for transfers between devices, shards(): far = lax.all_to_all(halo, 'space', 0, 0, tiled=True)  3.63 us
  transfers between devices with their start and end apart: 18, of which 5 were waited for; matrix products, arithmetic and copies ran while one was open for 0% of the time, Pallas kernels for 16%

profile of v6, /device:TPU:7, one launch (start us, length us, event | category | flops | bytes accessed | tf_op | source)
XLA Modules:
  0.0 72.0 jit_solution(15225636332659947290)
XLA Ops:
  0.0 1.8 %shard_map.271 = (bf16[272,256]{1,0:T(8,128)(2,1)S(1)}, bf16[272,256]{1,0:T(8,128)(2,1)S(1)}, bf16[6,64,512]{2,1,0:T(8,128)(2,1)S(1)}, bf16[6,64,512]{2,1,0:T(8,...) custom-call(bf16[1024,256]{1,0:T(8,128)(2,1)} %bitcast.17, ...), custom_call_target="tpu_custom_call" | custom-call | flops 300000000 | bytes 3000000 | tf_op jit(solution)/shard_map/pallas_call | solution.py:66
  1.8 2.8 %collective-permute-start.6 = (bf16[6,64,512]{2,1,0:T(8,128)(2,1)S(1)}, bf16[6,64,512]{2,1,0:T(8,128)(2,1)S(1)}, u32[]{:S(2)}, u32[]{:S(2)}) collective-permute-start(bf16[6,64,512]{2,1,0:T(8,128)(2,1)S(1)} %get-tuple-element.59), channel_id=1, source_target_pairs={{0,96},{32,64},{64,32},{96,0},{1,97},{33,65},{65,33},{97,1},{2,98}... | collective-permute-start | bytes 1179656 | tf_op jit(solution)/shard_map/ppermute | solution.py:393
  4.6 1.1 %collective-permute-start = (bf16[272,256]{1,0:T(8,128)(2,1)S(1)}, bf16[272,256]{1,0:T(8,128)(2,1)S(1)}, u32[]{:S(2)}, u32[]{:S(2)}) collective-permute-start(bf16[272,256]{1,0:T(8,128)(2,1)S(1)} %get-tuple-element.41), channel_id=1, source_target_pairs={{0,1},{1,0},{2,3},{3,2},{4,5},{5,4},{6,7},{7,6},{8,9},{9,8},{10,11... | collective-permute-start | bytes 417800 | tf_op jit(solution)/shard_map/ppermute | solution.py:397
  5.7 1.4 %collective-permute-start.1 = (bf16[272,256]{1,0:T(8,128)(2,1)S(1)}, bf16[272,256]{1,0:T(8,128)(2,1)S(1)}, u32[]{:S(2)}, u32[]{:S(2)}) collective-permute-start(bf16[272,256]{1,0:T(8,128)(2,1)S(1)} %get-tuple-element.42), channel_id=1, source_target_pairs={{0,32},{1,2},{2,1},{3,4},{4,3},{5,6},{6,5},{7,8},{8,7},{9,10},{10,... | collective-permute-start | bytes 417800 | tf_op jit(solution)/shard_map/ppermute | solution.py:397
  7.1 1.6 %collective-permute-start.3 = (bf16[6,64,512]{2,1,0:T(8,128)(2,1)S(1)}, bf16[6,64,512]{2,1,0:T(8,128)(2,1)S(1)}, u32[]{:S(2)}, u32[]{:S(2)}) collective-permute-start(bf16[6,64,512]{2,1,0:T(8,128)(2,1)S(1)} %get-tuple-element.58), channel_id=1, source_target_pairs={{0,32},{32,0},{64,96},{96,64},{1,33},{33,1},{65,97},{97,65},{2,34}... | collective-permute-start | bytes 1179656 | tf_op jit(solution)/shard_map/ppermute | solution.py:393
  8.8 2.3 %shard_map.272 = (bf16[1024,512]{1,0:T(8,128)(2,1)}, f32[256,512]{1,0:T(8,128)S(1)}, s32[32,256]{1,0:T(8,128)S(1)}, bf16[512,512]{1,0:T(8,128)(2,1)S(1)}, bf16[5...) custom-call(bf16[1024,256]{1,0:T(8,128)(2,1)S(1)} %get-tuple-element, ...), custom_call_target="tpu_custom_call" | custom-call | flops 3000000000 | bytes 3000000 | tf_op jit(solution)/shard_map/pallas_call | solution.py:66
  11.1 1.2 %collective-permute-done.1.cross_ref = bf16[272,256]{1,0:T(8,128)(2,1)S(1)} collective-permute-done((bf16[272,256]{1,0:T(8,128)(2,1)S(1)}, bf16[272,256]{1,0:T(8,128)(2,1)S(1)}, u32[]{:S(2)}, u32[]{:S(2)}) %collective-permute-start.1) | collective-permute-done | bytes 139296 | tf_op jit(solution)/shard_map/ppermute | solution.py:397
  12.3 2.3 %shard_map.273 = (bf16[256,512]{1,0:T(8,128)(2,1)S(1)}, bf16[256,512]{1,0:T(8,128)(2,1)S(1)}, bf16[512,256]{1,0:T(8,128)(2,1)}) custom-call(f32[256,512]{1,0:T(8,128)S(1)} %get-tuple-element.40.agg_ref, bf16[272,256]{1,0:T(8,128)(2,1)S(1)} %collective-permute-done.near_ref, bf16[272,256]{1,0:T(8,128)(2,1)S(1)} %collective-permute-done.1.cross_ref, ...), custom_call_target="tpu_custom_call" | custom-call | flops 1000000000 | bytes 3000000 | tf_op jit(solution)/shard_map/pallas_call | solution.py:66
  14.6 12.9 %all-to-all-start = ((bf16[32,16,256]{2,1,0:T(8,128)(2,1)}), bf16[32,16,256]{2,1,0:T(8,128)(2,1)S(1)}, u32[]{:S(2)}, u32[]{:S(2)}) async-start(bf16[32,16,256]{2,1,0:T(8,128)(2,1)} %bitcast.10), calls=%async_computation | async-start | bytes 524288 | tf_op jit(solution)/shard_map/all_to_all | solution.py:467
  27.8 2.4 %collective-permute-start.7 = (bf16[6,64,512]{2,1,0:T(8,128)(2,1)S(1)}, bf16[6,64,512]{2,1,0:T(8,128)(2,1)}, u32[]{:S(2)}, u32[]{:S(2)}) collective-permute-start(bf16[6,64,512]{2,1,0:T(8,128)(2,1)S(1)} %collective-permute-done.3.refs_0_), channel_id=1, source_target_pairs={{0,96},{32,64},{64,32},{96,0},{1,97},{33,65},{65,33},{97,1},{2,98}... | collective-permute-start | bytes 1179656 | tf_op jit(solution)/shard_map/ppermute | solution.py:393
  30.3 1.0 %collective-permute-start.12 = (bf16[6,64,512]{2,1,0:T(8,128)(2,1)S(1)}, bf16[6,64,512]{2,1,0:T(8,128)(2,1)}, u32[]{:S(2)}, u32[]{:S(2)}) collective-permute-start(bf16[6,64,512]{2,1,0:T(8,128)(2,1)S(1)} %collective-permute-done.6.refs_3_), channel_id=1, source_target_pairs={{0,1},{1,0},{2,3},{3,2},{4,5},{5,4},{6,7},{7,6},{8,9},{9,8},{10,11... | collective-permute-start | bytes 1179656 | tf_op jit(solution)/shard_map/ppermute | solution.py:397
  31.3 3.6 %all-to-all-done = bf16[32,16,256]{2,1,0:T(8,128)(2,1)S(1)} async-done(((bf16[32,16,256]{2,1,0:T(8,128)(2,1)}), bf16[32,16,256]{2,1,0:T(8,128)(2,1)S(1)}, u32[]{:S(2)}, u32[]{:S(2)}) %all-to-all-start) | async-done | bytes 262176 | tf_op jit(solution)/shard_map/all_to_all | solution.py:467
  35.0 4.1 %collective-permute-done.5.refs_2_ = bf16[6,64,512]{2,1,0:T(8,128)(2,1)S(1)} collective-permute-done((bf16[6,64,512]{2,1,0:T(8,128)(2,1)S(1)}, bf16[6,64,512]{2,1,0:T(8,128)(2,1)S(1)}, u32[]{:S(2)}, u32[]{:S(2)}) %collective-permute-start.5) | collective-permute-done | bytes 393248 | tf_op jit(solution)/shard_map/ppermute | solution.py:393
  39.1 2.1 %collective-permute-start.9 = (bf16[6,64,512]{2,1,0:T(8,128)(2,1)S(1)}, bf16[6,64,512]{2,1,0:T(8,128)(2,1)S(1)}, u32[]{:S(2)}, u32[]{:S(2)}) collective-permute-start(bf16[6,64,512]{2,1,0:T(8,128)(2,1)S(1)} %collective-permute-done.3.refs_0_), channel_id=1, source_target_pairs={{0,1},{1,0},{2,3},{3,2},{4,5},{5,4},{6,7},{7,6},{8,9},{9,8},{10,11... | collective-permute-start | bytes 1179656 | tf_op jit(solution)/shard_map/ppermute | solution.py:397
  41.3 6.3 %collective-permute-done.7.refs_4_ = bf16[6,64,512]{2,1,0:T(8,128)(2,1)} collective-permute-done((bf16[6,64,512]{2,1,0:T(8,128)(2,1)S(1)}, bf16[6,64,512]{2,1,0:T(8,128)(2,1)}, u32[]{:S(2)}, u32[]{:S(2)}) %collective-permute-start.7) | collective-permute-done | bytes 393248 | tf_op jit(solution)/shard_map/ppermute | solution.py:393
  47.6 1.3 %collective-permute-start.11 = (bf16[6,64,512]{2,1,0:T(8,128)(2,1)S(1)}, bf16[6,64,512]{2,1,0:T(8,128)(2,1)S(1)}, u32[]{:S(2)}, u32[]{:S(2)}) collective-permute-start(bf16[6,64,512]{2,1,0:T(8,128)(2,1)S(1)} %collective-permute-done.5.refs_2_), channel_id=1, source_target_pairs={{0,1},{1,0},{2,3},{3,2},{4,5},{5,4},{6,7},{7,6},{8,9},{9,8},{10,11... | collective-permute-start | bytes 1179656 | tf_op jit(solution)/shard_map/ppermute | solution.py:397
  48.9 0.5 collective-permute-start.14
  49.4 4.1 %shard_map.274 = (bf16[3,1024,256]{2,1,0:T(8,128)(2,1)}, bf16[256,768]{1,0:T(8,128)(2,1)S(1)}) custom-call(s32[1,2560]{1,0:T(1,128)S(1)} %get-tuple-element.51.src_ref, s32[1,2560]{1,0:T(1,128)S(1)} %get-tuple-element.52.dst_ref, s32[32,256]{1,0:T(8,128)S(1)} %get-tuple-element.53.far_dst_ref, s32[1,32]{1,0:T(1,128)S(1)} %get-tuple-element.54.len_ref, ...), custom_call_target="tpu_custom_call" | custom-call | flops 4000000000 | bytes 8000000 | tf_op jit(solution)/shard_map/pallas_call | solution.py:66
  53.6 0.7 copy-done.4
  54.5 7.6 %shard_map.275.back_ref = bf16[256,512]{1,0:T(8,128)(2,1)S(1)} custom-call(bf16[256,512]{1,0:T(8,128)(2,1)S(1)} %get-tuple-element.49.normed_ref, bf16[512,256]{1,0:T(8,128)(2,1)S(1)} %bitcast.16, bf16[512,256]{1,0:T(8,128)(2,1)S(1)} %collective-permute-done.2.got_ref, bf16[256,768]{1,0:T(8,128)(2,1)S(1)} %get-tuple-element.56.rep_ref, ...), custom_call_target="tpu_custom_call" | custom-call | flops 5000000000 | bytes 6000000 | tf_op jit(solution)/shard_map/pallas_call | solution.py:66
  62.5 1.3 %collective-permute-start.16 = (bf16[256,512]{1,0:T(8,128)(2,1)S(1)}, bf16[256,512]{1,0:T(8,128)(2,1)S(1)}, u32[]{:S(2)}, u32[]{:S(2)}) collective-permute-start(bf16[256,512]{1,0:T(8,128)(2,1)S(1)} %shard_map.275.back_ref), channel_id=1, source_target_pairs={{0,32},{1,2},{2,1},{3,4},{4,3},{5,6},{6,5},{7,8},{8,7},{9,10},{10,... | collective-permute-start | bytes 786440 | tf_op jit(solution)/shard_map/ppermute | solution.py:397
  63.8 3.0 %shard_map.276 = (f32[1024,512]{1,0:T(8,128)S(1)}, bf16[1024,256]{1,0:T(8,128)(2,1)S(1)}, bf16[84,512]{1,0:T(8,128)(2,1)S(1)}) custom-call(bf16[256,512]{1,0:T(8,128)(2,1)S(1)} %shard_map.275.back_ref, bf16[256,512]{1,0:T(8,128)(2,1)S(1)} %collective-permute-done.15.near_ref, bf16[3,1024,256]{2,1,0:T(8,128)(2,1)} %get-tuple-element.60.links_hbm, ...), custom_call_target="tpu_custom_call" | custom-call | flops 1000000000 | bytes 2000000 | tf_op jit(solution)/shard_map/pallas_call | solution.py:66
  66.8 3.6 %collective-permute-done.16.cross_ref = bf16[256,512]{1,0:T(8,128)(2,1)S(1)} collective-permute-done((bf16[256,512]{1,0:T(8,128)(2,1)S(1)}, bf16[256,512]{1,0:T(8,128)(2,1)S(1)}, u32[]{:S(2)}, u32[]{:S(2)}) %collective-permute-start.16) | collective-permute-done | bytes 262176 | tf_op jit(solution)/shard_map/ppermute | solution.py:397
  70.4 1.5 %shard_map.277 = bf16[84,1024]{1,0:T(8,128)(2,1)} custom-call(f32[1024,512]{1,0:T(8,128)S(1)} %get-tuple-element.62.part_ref, bf16[1024,256]{1,0:T(8,128)(2,1)S(1)} %get-tuple-element.63.links_ref, bf16[256,512]{1,0:T(8,128)(2,1)S(1)} %collective-permute-done.16.cross_ref, bf16[84,512]{1,0:T(8,128)(2,1)S(1)} %get-tuple-element.64.wo_ref), custom_call_target="tpu_custom_call" | custom-call | flops 2000000000 | bytes 8000000 | tf_op jit(solution)/shard_map/pallas_call | solution.py:66
  (33 shorter events, 1.1 us)
Async XLA Ops:
  1.8 28.5 %collective-permute-start.6 = (bf16[6,64,512]{2,1,0:T(8,128)(2,1)S(1)}, bf16[6,64,512]{2,1,0:T(8,128)(2,1)S(1)}, u32[]{:S(2)}, u32[]{:S(2)}) collective-permute-start(bf16[6,64,512]{2,1,0:T(8,128)(2,1)S(1)} %get-tuple-element.59), channel_id=1, source_target_pairs={{0,96},{32,64},{64,32},{96,0},{1,97},{33,65},{65,33},{97,1},{2,98}... | collective-permute-start | bytes 1179656 | tf_op jit(solution)/shard_map/ppermute | solution.py:393
  4.6 26.7 %collective-permute-start.4 = (bf16[6,64,512]{2,1,0:T(8,128)(2,1)S(1)}, bf16[6,64,512]{2,1,0:T(8,128)(2,1)S(1)}, u32[]{:S(2)}, u32[]{:S(2)}) collective-permute-start(bf16[6,64,512]{2,1,0:T(8,128)(2,1)S(1)} %get-tuple-element.59), channel_id=1, source_target_pairs={{0,32},{32,0},{64,96},{96,64},{1,33},{33,1},{65,97},{97,65},{2,34}... | collective-permute-start | bytes 1179656 | tf_op jit(solution)/shard_map/ppermute | solution.py:393
  4.6 6.5 %collective-permute-start = (bf16[272,256]{1,0:T(8,128)(2,1)S(1)}, bf16[272,256]{1,0:T(8,128)(2,1)S(1)}, u32[]{:S(2)}, u32[]{:S(2)}) collective-permute-start(bf16[272,256]{1,0:T(8,128)(2,1)S(1)} %get-tuple-element.41), channel_id=1, source_target_pairs={{0,1},{1,0},{2,3},{3,2},{4,5},{5,4},{6,7},{7,6},{8,9},{9,8},{10,11... | collective-permute-start | bytes 417800 | tf_op jit(solution)/shard_map/ppermute | solution.py:397
  5.7 6.6 %collective-permute-start.1 = (bf16[272,256]{1,0:T(8,128)(2,1)S(1)}, bf16[272,256]{1,0:T(8,128)(2,1)S(1)}, u32[]{:S(2)}, u32[]{:S(2)}) collective-permute-start(bf16[272,256]{1,0:T(8,128)(2,1)S(1)} %get-tuple-element.42), channel_id=1, source_target_pairs={{0,32},{1,2},{2,1},{3,4},{4,3},{5,6},{6,5},{7,8},{8,7},{9,10},{10,... | collective-permute-start | bytes 417800 | tf_op jit(solution)/shard_map/ppermute | solution.py:397
  7.1 20.7 %collective-permute-start.3 = (bf16[6,64,512]{2,1,0:T(8,128)(2,1)S(1)}, bf16[6,64,512]{2,1,0:T(8,128)(2,1)S(1)}, u32[]{:S(2)}, u32[]{:S(2)}) collective-permute-start(bf16[6,64,512]{2,1,0:T(8,128)(2,1)S(1)} %get-tuple-element.58), channel_id=1, source_target_pairs={{0,32},{32,0},{64,96},{96,64},{1,33},{33,1},{65,97},{97,65},{2,34}... | collective-permute-start | bytes 1179656 | tf_op jit(solution)/shard_map/ppermute | solution.py:393
  14.6 20.3 %all-to-all-start = ((bf16[32,16,256]{2,1,0:T(8,128)(2,1)}), bf16[32,16,256]{2,1,0:T(8,128)(2,1)S(1)}, u32[]{:S(2)}, u32[]{:S(2)}) async-start(bf16[32,16,256]{2,1,0:T(8,128)(2,1)} %bitcast.10), calls=%async_computation | async-start | bytes 524288 | tf_op jit(solution)/shard_map/all_to_all | solution.py:467
  27.5 11.6 %collective-permute-start.5 = (bf16[6,64,512]{2,1,0:T(8,128)(2,1)S(1)}, bf16[6,64,512]{2,1,0:T(8,128)(2,1)S(1)}, u32[]{:S(2)}, u32[]{:S(2)}) collective-permute-start(bf16[6,64,512]{2,1,0:T(8,128)(2,1)S(1)} %get-tuple-element.58), channel_id=1, source_target_pairs={{0,96},{32,64},{64,32},{96,0},{1,97},{33,65},{65,33},{97,1},{2,98}... | collective-permute-start | bytes 1179656 | tf_op jit(solution)/shard_map/ppermute | solution.py:393
  27.8 25.6 %copy-start.2 = (bf16[6,64,512]{2,1,0:T(8,128)(2,1)}, bf16[6,64,512]{2,1,0:T(8,128)(2,1)S(1)}, u32[]{:S(2)}) copy-start(bf16[6,64,512]{2,1,0:T(8,128)(2,1)S(1)} %collective-permute-done.3.refs_0_) | copy-start | bytes 1179652
  27.8 19.8 %collective-permute-start.7 = (bf16[6,64,512]{2,1,0:T(8,128)(2,1)S(1)}, bf16[6,64,512]{2,1,0:T(8,128)(2,1)}, u32[]{:S(2)}, u32[]{:S(2)}) collective-permute-start(bf16[6,64,512]{2,1,0:T(8,128)(2,1)S(1)} %collective-permute-done.3.refs_0_), channel_id=1, source_target_pairs={{0,96},{32,64},{64,32},{96,0},{1,97},{33,65},{65,33},{97,1},{2,98}... | collective-permute-start | bytes 1179656 | tf_op jit(solution)/shard_map/ppermute | solution.py:393
  30.3 23.2 %copy-start = (bf16[6,64,512]{2,1,0:T(8,128)(2,1)}, bf16[6,64,512]{2,1,0:T(8,128)(2,1)S(1)}, u32[]{:S(2)}) copy-start(bf16[6,64,512]{2,1,0:T(8,128)(2,1)S(1)} %collective-permute-done.6.refs_3_) | copy-start | bytes 1179652
  30.3 18.6 %collective-permute-start.8 = (bf16[6,64,512]{2,1,0:T(8,128)(2,1)S(1)}, bf16[6,64,512]{2,1,0:T(8,128)(2,1)}, u32[]{:S(2)}, u32[]{:S(2)}) collective-permute-start(bf16[6,64,512]{2,1,0:T(8,128)(2,1)S(1)} %collective-permute-done.6.refs_3_), channel_id=1, source_target_pairs={{0,32},{32,0},{64,96},{96,64},{1,33},{33,1},{65,97},{97,65},{2,34}... | collective-permute-start | bytes 1179656 | tf_op jit(solution)/shard_map/ppermute | solution.py:393
  30.3 18.6 %collective-permute-start.12 = (bf16[6,64,512]{2,1,0:T(8,128)(2,1)S(1)}, bf16[6,64,512]{2,1,0:T(8,128)(2,1)}, u32[]{:S(2)}, u32[]{:S(2)}) collective-permute-start(bf16[6,64,512]{2,1,0:T(8,128)(2,1)S(1)} %collective-permute-done.6.refs_3_), channel_id=1, source_target_pairs={{0,1},{1,0},{2,3},{3,2},{4,5},{5,4},{6,7},{7,6},{8,9},{9,8},{10,11... | collective-permute-start | bytes 1179656 | tf_op jit(solution)/shard_map/ppermute | solution.py:397
  31.3 22.2 %copy-start.1 = (bf16[6,64,512]{2,1,0:T(8,128)(2,1)}, bf16[6,64,512]{2,1,0:T(8,128)(2,1)S(1)}, u32[]{:S(2)}) copy-start(bf16[6,64,512]{2,1,0:T(8,128)(2,1)S(1)} %collective-permute-done.4.refs_1_) | copy-start | bytes 1179652
  35.0 6.2 %collective-permute-start.2 = (bf16[512,256]{1,0:T(8,128)(2,1)S(1)}, bf16[512,256]{1,0:T(8,128)(2,1)S(1)}, u32[]{:S(2)}, u32[]{:S(2)}) collective-permute-start(bf16[512,256]{1,0:T(8,128)(2,1)S(1)} %bitcast.15), channel_id=1, source_target_pairs={{0,1},{1,0},{2,3},{3,2},{4,5},{5,4},{6,7},{7,6},{8,9},{9,8},{10,11... | collective-permute-start | bytes 786440 | tf_op jit(solution)/shard_map/ppermute | solution.py:397
  39.1 14.4 %copy-start.3 = (bf16[6,64,512]{2,1,0:T(8,128)(2,1)}, bf16[6,64,512]{2,1,0:T(8,128)(2,1)S(1)}, u32[]{:S(2)}) copy-start(bf16[6,64,512]{2,1,0:T(8,128)(2,1)S(1)} %collective-permute-done.5.refs_2_) | copy-start | bytes 1179652
  39.1 14.4 %collective-permute-start.9 = (bf16[6,64,512]{2,1,0:T(8,128)(2,1)S(1)}, bf16[6,64,512]{2,1,0:T(8,128)(2,1)S(1)}, u32[]{:S(2)}, u32[]{:S(2)}) collective-permute-start(bf16[6,64,512]{2,1,0:T(8,128)(2,1)S(1)} %collective-permute-done.3.refs_0_), channel_id=1, source_target_pairs={{0,1},{1,0},{2,3},{3,2},{4,5},{5,4},{6,7},{7,6},{8,9},{9,8},{10,11... | collective-permute-start | bytes 1179656 | tf_op jit(solution)/shard_map/ppermute | solution.py:397
  41.2 12.3 %collective-permute-start.10 = (bf16[6,64,512]{2,1,0:T(8,128)(2,1)S(1)}, bf16[6,64,512]{2,1,0:T(8,128)(2,1)S(1)}, u32[]{:S(2)}, u32[]{:S(2)}) collective-permute-start(bf16[6,64,512]{2,1,0:T(8,128)(2,1)S(1)} %collective-permute-done.4.refs_1_), channel_id=1, source_target_pairs={{0,1},{1,0},{2,3},{3,2},{4,5},{5,4},{6,7},{7,6},{8,9},{9,8},{10,11... | collective-permute-start | bytes 1179656 | tf_op jit(solution)/shard_map/ppermute | solution.py:397
  47.6 5.9 %collective-permute-start.11 = (bf16[6,64,512]{2,1,0:T(8,128)(2,1)S(1)}, bf16[6,64,512]{2,1,0:T(8,128)(2,1)S(1)}, u32[]{:S(2)}, u32[]{:S(2)}) collective-permute-start(bf16[6,64,512]{2,1,0:T(8,128)(2,1)S(1)} %collective-permute-done.5.refs_2_), channel_id=1, source_target_pairs={{0,1},{1,0},{2,3},{3,2},{4,5},{5,4},{6,7},{7,6},{8,9},{9,8},{10,11... | collective-permute-start | bytes 1179656 | tf_op jit(solution)/shard_map/ppermute | solution.py:397
  48.9 4.7 %collective-permute-start.13 = (bf16[6,64,512]{2,1,0:T(8,128)(2,1)}, bf16[6,64,512]{2,1,0:T(8,128)(2,1)S(1)}, u32[]{:S(2)}, u32[]{:S(2)}) collective-permute-start(bf16[6,64,512]{2,1,0:T(8,128)(2,1)} %collective-permute-done.7.refs_4_), channel_id=1, source_target_pairs={{0,1},{1,0},{2,3},{3,2},{4,5},{5,4},{6,7},{7,6},{8,9},{9,8},{10,11... | collective-permute-start | bytes 1179656 | tf_op jit(solution)/shard_map/ppermute | solution.py:397
  48.9 4.7 %collective-permute-start.14 = (bf16[6,64,512]{2,1,0:T(8,128)(2,1)}, bf16[6,64,512]{2,1,0:T(8,128)(2,1)S(1)}, u32[]{:S(2)}, u32[]{:S(2)}) collective-permute-start(bf16[6,64,512]{2,1,0:T(8,128)(2,1)} %collective-permute-done.8.refs_5_), channel_id=1, source_target_pairs={{0,1},{1,0},{2,3},{3,2},{4,5},{5,4},{6,7},{7,6},{8,9},{9,8},{10,11... | collective-permute-start | bytes 1179656 | tf_op jit(solution)/shard_map/ppermute | solution.py:397
  53.5 0.9 %copy-start.5 = (bf16[6,64,512]{2,1,0:T(8,128)(2,1)}, bf16[6,64,512]{2,1,0:T(8,128)(2,1)S(1)}, u32[]{:S(2)}) copy-start(bf16[6,64,512]{2,1,0:T(8,128)(2,1)S(1)} %collective-permute-done.10.refs_7_) | copy-start | bytes 1179652
  53.6 1.0 %copy-start.6 = (bf16[6,64,512]{2,1,0:T(8,128)(2,1)}, bf16[6,64,512]{2,1,0:T(8,128)(2,1)S(1)}, u32[]{:S(2)}) copy-start(bf16[6,64,512]{2,1,0:T(8,128)(2,1)S(1)} %collective-permute-done.11.refs_8_) | copy-start | bytes 1179652
  62.2 1.7 %collective-permute-start.15 = (bf16[256,512]{1,0:T(8,128)(2,1)S(1)}, bf16[256,512]{1,0:T(8,128)(2,1)S(1)}, u32[]{:S(2)}, u32[]{:S(2)}) collective-permute-start(bf16[256,512]{1,0:T(8,128)(2,1)S(1)} %shard_map.275.back_ref), channel_id=1, source_target_pairs={{0,1},{1,0},{2,3},{3,2},{4,5},{5,4},{6,7},{7,6},{8,9},{9,8},{10,11... | collective-permute-start | bytes 786440 | tf_op jit(solution)/shard_map/ppermute | solution.py:397
  62.5 7.9 %collective-permute-start.16 = (bf16[256,512]{1,0:T(8,128)(2,1)S(1)}, bf16[256,512]{1,0:T(8,128)(2,1)S(1)}, u32[]{:S(2)}, u32[]{:S(2)}) collective-permute-start(bf16[256,512]{1,0:T(8,128)(2,1)S(1)} %shard_map.275.back_ref), channel_id=1, source_target_pairs={{0,32},{1,2},{2,1},{3,4},{4,3},{5,6},{6,5},{7,8},{8,7},{9,10},{10,... | collective-permute-start | bytes 786440 | tf_op jit(solution)/shard_map/ppermute | solution.py:397
  (1 other events, 0.8 us)
